TPU v7x, 256 devices: a whole 4x4x8 slice. The times are simulated.
256 devices in a mesh: wide: 8 (over y, core), narrow: 4 (over z_lo), net: 8 (over z_hi, x).
Axes of the slice: x: 4, y: 4, z: 8 (z_hi: 2, z_lo: 4; z = z_hi * 4 + z_lo), core: 2. Of those that a mesh axis runs over, the one named last changes fastest.
Arguments:
- fields: float32 [4, 64, 32, 1024], P(None, 'net', 'wide', 'narrow'), may hold values from -7.5 to 7.5
- conv1_weight: bfloat16 [27, 32, 4], replicated, may hold values from -0.625 to 0.625
- conv1_bias: float32 [32], replicated, may hold values from -6 to 6
- conv2_weight: bfloat16 [27, 6, 32], replicated, may hold values from -0.21875 to 0.21875
Outputs:
- advanced: float32 [4, 64, 32, 1024], P(None, 'net', 'wide', 'narrow')
All inputs are finite; a program needn't handle non-finite values.
Results may differ from a plain program's by a relative error of at most 0.0028.
Values may be sent and summed in bfloat16 or wider, within the bound.
No kernel may reach another device: no remote copies, remote signals or barrier semaphores. Data moves between devices by JAX's collectives and lax.ppermute only.
A program may use at most 64 MiB of HBM per device.

v0:
```python
import functools

import jax
import jax.numpy as jnp
import numpy as np
from jax import lax
from jax.experimental import pallas as pl
from jax.experimental.pallas import tpu as pltpu
from jax.sharding import PartitionSpec as P

time_step = 0.2
viscosity = 0.05
EDGE = 9
HALF = 64
F32 = jnp.float32
BF16 = jnp.bfloat16
HIGH = lax.Precision.HIGHEST
VM = pl.BlockSpec(memory_space=pltpu.VMEM)
SM = pl.BlockSpec(memory_space=pltpu.SMEM)


def split_parity():
    m = np.zeros((256, 256), np.float32)
    for l in range(128):
        m[2 * l, l] = 1.0
        m[2 * l + 1, 128 + l] = 1.0
    return m


def row_order():
    m = np.zeros((256, 256), np.float32)
    for z in range(8):
        for x in range(4):
            for p in range(2):
                for c in range(4):
                    m[((z * 4 + x) * 2 + p) * 4 + c, ((p * 4 + c) * 8 + z) * 4 + x] = 1.0
    return m


def place_conv1():
    m = np.zeros((27, 4, 8, 512), np.float32)
    for dz in range(3):
        for dx in range(3):
            for dy in range(3):
                for c in range(4):
                    for xo in range(8):
                        xi = xo + 1 + dx
                        m[9 * dz + 3 * dx + dy, c, xo, ((dz * 3 + dy) * 12 + xi) * 4 + c] = 1.0
    return m.reshape(108, 4096)


def place_conv2():
    m = np.zeros((3, 32, 6, 8, 32), np.float32)
    for dx in range(3):
        for h in range(32):
            for xo in range(6):
                m[dx, h, xo, xo + dx, h] = 1.0
    return m.reshape(96, 6 * 256)


def divergence_matrix():
    m = np.zeros((4, 2, 4, 5, 6, 8), np.float32)
    sx, sy, sz = (0, 3, 4), (3, 1, 5), (4, 5, 2)
    for x in range(4):
        for comp in range(3):
            m[x, :, comp, 1, x + 2, sx[comp]] += 0.25
            m[x, :, comp, 1, x, sx[comp]] -= 0.25
            m[x, :, comp, 4, x + 1, sy[comp]] += 0.25
            m[x, :, comp, 3, x + 1, sy[comp]] -= 0.25
            m[x, :, comp, 2, x + 1, sz[comp]] += 0.25
            m[x, :, comp, 0, x + 1, sz[comp]] -= 0.25
    return m.reshape(32, 240)


def call(kernel, outs, scratch, *args):
    specs = [SM if a.ndim == 1 else VM for a in args]
    return pl.pallas_call(
        kernel,
        out_shape=[jax.ShapeDtypeStruct(s, d) for s, d in outs],
        in_specs=specs,
        out_specs=[VM] * len(outs),
        scratch_shapes=scratch,
    )(*args)


def exact(a, b, dims=(((1,), (0,)), ((), ()))):
    return lax.dot_general(a, b, dims, precision=HIGH, preferred_element_type=F32)


def lanes_of(shape):
    return lax.broadcasted_iota(jnp.int32, shape, len(shape) - 1)


def pack_kernel(core_ref, fields_ref, parity_ref, order_ref, native_ref, same_ref, cross_ref, flat):
    core = core_ref[0]
    for c in range(4):
        for z in range(8):
            flat[pl.ds((c * 8 + z) * 4, 4), :] = fields_ref[c, z]
    parts = exact(flat[...], parity_ref[...].astype(F32))
    stacked = jnp.concatenate([parts[:, :128], parts[:, 128:]], axis=0)
    native = exact(order_ref[...].astype(F32), stacked)
    native_ref[...] = native
    row = lax.broadcasted_iota(jnp.int32, (16, 128), 0)
    lane = lanes_of((16, 128))
    first = jnp.where((lane == row) & (row < EDGE), 1.0, 0.0).astype(F32)
    last = jnp.where((lane == row + 128 - EDGE) & (row < EDGE), 1.0, 0.0).astype(F32)
    over_lanes = (((1,), (1,)), ((), ()))
    left = exact(first, native, over_lanes)
    right = exact(last, native, over_lanes)
    same_ref[...] = jnp.where(core == 0, right, left)
    cross_ref[...] = jnp.where(core == 0, left, right)


def emit_messages(q_ref, coarse_ref, left_ref, right_ref, down_ref, up_ref):
    low = lax.broadcasted_iota(jnp.int32, (8, 128), 0) < 4
    for zc in range(4):
        means = []
        for xc in range(4):
            t = (q_ref[2 * zc, 2 * xc] + q_ref[2 * zc, 2 * xc + 1]) + (
                q_ref[2 * zc + 1, 2 * xc] + q_ref[2 * zc + 1, 2 * xc + 1]
            )
            means.append((t + pltpu.roll(t, 4, 0)) * 0.125)
        slab = jnp.concatenate(
            [jnp.where(low, means[0], means[1]), jnp.where(low, means[2], means[3])], axis=0
        ).astype(BF16)
        coarse_ref[pl.ds(zc * 16, 16), :] = slab
        left_ref[pl.ds(zc * 16, 16), :] = slab
        right_ref[pl.ds(zc * 16, 16), :] = slab
    for z in range(0, 8, 2):
        at = pl.ds(64 + z * 8, 16)
        left_ref[at, :] = jnp.concatenate([q_ref[z, 0], q_ref[z + 1, 0]], axis=0).astype(BF16)
        right_ref[at, :] = jnp.concatenate([q_ref[z, 7], q_ref[z + 1, 7]], axis=0).astype(BF16)
    for x in range(0, 8, 2):
        at = pl.ds(x * 8, 16)
        down_ref[at, :] = jnp.concatenate([q_ref[0, x], q_ref[0, x + 1]], axis=0).astype(BF16)
        up_ref[at, :] = jnp.concatenate([q_ref[7, x], q_ref[7, x + 1]], axis=0).astype(BF16)


MESSAGES = [((64, 128), BF16), ((128, 128), BF16), ((128, 128), BF16), ((64, 128), BF16), ((64, 128), BF16)]


def assemble_kernel(
    core_ref, own_ref, other_ref, same_ref, cross_ref, q_ref, coarse_ref, left_ref, right_ref, down_ref, up_ref
):
    core = core_ref[0]
    row = lax.broadcasted_iota(jnp.int32, (16, 128), 0)
    lane16 = lanes_of((16, 128))
    start = jnp.where(core == 0, 0, HALF + EDGE)
    place = jnp.where((lane16 == row + start) & (row < EDGE), 1.0, 0.0).astype(F32)
    lane = lanes_of((256, 128))
    begin = jnp.where(core == 0, EDGE, 0)
    inside = (lane >= begin) & (lane < begin + HALF + EDGE)
    shift = jnp.where(core == 0, EDGE, HALF + EDGE)
    over_rows = (((0,), (0,)), ((), ()))
    for block_ref, edge_ref, position in ((own_ref, same_ref, core), (other_ref, cross_ref, 1 - core)):
        edge = exact(edge_ref[...], place, over_rows)
        block = jnp.where(inside, pltpu.roll(block_ref[...], shift, 1), edge)
        q_ref[:, pl.ds(position * 4, 4)] = block.reshape(8, 4, 8, 128)
    emit_messages(q_ref, coarse_ref, left_ref, right_ref, down_ref, up_ref)


def weights_kernel(w1_ref, w2_ref, place1_ref, place2_ref, band1_ref, band2_ref):
    spread1 = jnp.dot(w1_ref[...], place1_ref[...], preferred_element_type=F32).astype(BF16)
    for xo in range(8):
        band1_ref[pl.ds(xo * 32, 32), :] = spread1[:, xo * 512 : (xo + 1) * 512]
    spread2 = jnp.dot(w2_ref[...], place2_ref[...], preferred_element_type=F32).astype(BF16)
    for xo in range(6):
        band2_ref[pl.ds(xo * 80, 80), :] = spread2[:, xo * 256 : (xo + 1) * 256]


def stage_body(
    q_ref, coarse_ref, from_left_ref, from_right_ref, below_ref, above_ref,
    band1_ref, band2_ref, bias_ref, div_ref, columns, parts, stress, update, new_ref,
):
    for j in range(10):
        if j < 3:
            ref, starts = below_ref, (j * 16, 48 + j * 16, 96 + j * 16)
            pieces = [ref[pl.ds(s, 16), :] for s in starts]
        elif j >= 7:
            ref, starts = above_ref, ((j - 7) * 16, 48 + (j - 7) * 16, 96 + (j - 7) * 16)
            pieces = [ref[pl.ds(s, 16), :] for s in starts]
        else:
            at = pl.ds((j - 3) * 16, 16)
            pieces = [from_left_ref[at, :], coarse_ref[at, :], from_right_ref[at, :]]
        for i, piece in enumerate(pieces):
            wide = piece.astype(F32)
            columns[pl.ds(j * 144 + i * 16, 16), :] = pltpu.roll(wide, 1, 1).astype(BF16)
            columns[pl.ds(j * 144 + 48 + i * 16, 16), :] = piece
            columns[pl.ds(j * 144 + 96 + i * 16, 16), :] = pltpu.roll(wide, 127, 1).astype(BF16)

    bias = jnp.concatenate([bias_ref[...]] * 8, axis=0)

    def layer(j, carry):
        rows = columns[pl.ds(pl.multiple_of(j * 144, 16), 432), :]
        pre = jnp.dot(band1_ref[:, :432], rows, preferred_element_type=F32) + bias
        inner = pre * (0.7978845608028654 + 0.7978845608028654 * 0.044715 * (pre * pre))
        half = 0.5 * pre
        hidden = (half + half * jnp.tanh(inner)).astype(BF16)
        parts[j] = jnp.dot(band2_ref[...], hidden, preferred_element_type=F32)
        return carry

    lax.fori_loop(0, 8, layer, 0, unroll=True)

    for k in range(6):
        rows = []
        for xo in range(6):
            sums = []
            for dy in range(3):
                at = [pl.ds(xo * 80 + (dz * 3 + dy) * 8, 8) for dz in range(3)]
                sums.append(parts[k, at[0], :] + parts[k + 1, at[1], :] + parts[k + 2, at[2], :])
            rows.append(sums[1] + pltpu.roll(sums[0], 1, 1) + pltpu.roll(sums[2], 127, 1))
        tile = jnp.concatenate(rows, axis=0).astype(BF16)
        stress[pl.ds(k * 48, 48), :] = tile
    low = lax.broadcasted_iota(jnp.int32, (8, 128), 0) < 4
    forces = []
    for k in range(1, 5):
        here = stress[pl.ds(k * 48, 48), :]
        wide = here.astype(F32)
        operand = jnp.concatenate(
            [
                stress[pl.ds((k - 1) * 48, 144), :],
                pltpu.roll(wide, 1, 1).astype(BF16),
                pltpu.roll(wide, 127, 1).astype(BF16),
            ],
            axis=0,
        )
        forces.append(jnp.dot(div_ref[...], operand, preferred_element_type=F32))

    below = [below_ref[pl.ds(144 + x * 8, 16), :].astype(F32) for x in range(0, 8, 2)]
    above = [above_ref[pl.ds(144 + x * 8, 16), :].astype(F32) for x in range(0, 8, 2)]
    left = [from_left_ref[pl.ds(64 + z * 8, 16), :].astype(F32) for z in range(0, 8, 2)]
    right = [from_right_ref[pl.ds(64 + z * 8, 16), :].astype(F32) for z in range(0, 8, 2)]

    def cell(z, x):
        if z < 0:
            return below[x // 2][(x % 2) * 8 : (x % 2) * 8 + 8]
        if z > 7:
            return above[x // 2][(x % 2) * 8 : (x % 2) * 8 + 8]
        if x < 0:
            return left[z // 2][(z % 2) * 8 : (z % 2) * 8 + 8]
        if x > 7:
            return right[z // 2][(z % 2) * 8 : (z % 2) * 8 + 8]
        return q_ref[z, x]

    for z in range(8):
        for x in range(8):
            here = q_ref[z, x]
            zp, zm, xp, xm = cell(z + 1, x), cell(z - 1, x), cell(z, x + 1), cell(z, x - 1)
            swap = pltpu.roll(here, 4, 0)
            back, ahead = pltpu.roll(swap, 1, 1), pltpu.roll(swap, 127, 1)
            far = jnp.where(low, back, ahead)
            slope_y = jnp.where(low, swap - back, ahead - swap)
            spread = (zp + zm) + (xp + xm) + (swap + far) - 6.0 * here

            def velocity(c):
                first = jnp.broadcast_to(q_ref[z, x, c : c + 1, :], (8, 128))
                second = jnp.broadcast_to(q_ref[z, x, c + 4 : c + 5, :], (8, 128))
                return jnp.where(low, first, second)

            advect = velocity(0) * (xp - xm) + velocity(1) * slope_y + velocity(2) * (zp - zm)
            force = forces[z // 2][(x // 2) * 8 : (x // 2) * 8 + 8]
            rate = viscosity * spread - 0.5 * advect + force
            new_ref[z, x] = update(z, x, here, rate)


def stage1_kernel(*refs):
    ins, outs, (columns, parts, stress) = refs[:10], refs[10:16], refs[16:]
    stage_body(*ins, columns, parts, stress, lambda z, x, q, r: q + time_step * r, outs[0])
    emit_messages(*outs)


def stage2_kernel(base_ref, *refs):
    ins, outs, (columns, parts, stress) = refs[:10], refs[10:16], refs[16:]

    def update(z, x, q, r):
        return 0.75 * base_ref[z, x] + 0.25 * (q + time_step * r)

    stage_body(*ins, columns, parts, stress, update, outs[0])
    emit_messages(*outs)


def stage3_kernel(core_ref, base_ref, *refs):
    ins, outs, (columns, parts, stress, new) = refs[:10], refs[10:12], refs[12:]
    core = core_ref[0]

    def update(z, x, q, r):
        return base_ref[z, x] * (1.0 / 3.0) + (2.0 / 3.0) * (q + time_step * r)

    stage_body(*ins, columns, parts, stress, update, new)
    outs[0][...] = new[:, pl.ds(core * 4, 4)]
    outs[1][...] = new[:, pl.ds((1 - core) * 4, 4)]


def finish_kernel(core_ref, own_ref, other_ref, parity_ref, order_ref, out_ref, flat):
    core = core_ref[0]
    lane = lanes_of((256, 128))
    own = own_ref[...].reshape(256, 128)
    other = other_ref[...].reshape(256, 128)
    low = jnp.where(core == 0, own, other)
    high = jnp.where(core == 0, other, own)
    native = jnp.where(lane < HALF, pltpu.roll(low, 128 - EDGE, 1), pltpu.roll(high, HALF - EDGE, 1))
    stacked = exact(order_ref[...].astype(F32), native, (((0,), (0,)), ((), ())))
    parts = jnp.concatenate([stacked[:128], stacked[128:]], axis=1)
    flat[...] = exact(parts, parity_ref[...].astype(F32), (((1,), (1,)), ((), ())))
    for c in range(4):
        for z in range(8):
            out_ref[c, z] = flat[pl.ds((c * 8 + z) * 4, 4), :]


def chip_shift(value, step):
    size = lax.axis_size("wide")
    return lax.ppermute(value, "wide", [(i, (i + 2 * step) % size) for i in range(size)])


def net_shift(value, step):
    size = lax.axis_size("net")
    return lax.ppermute(value, "net", [(i, (i + step) % size) for i in range(size)])


def partner(value):
    return lax.ppermute(value, "wide", [(i, i ^ 1) for i in range(lax.axis_size("wide"))])


def edge_shift(value, cross):
    wide, narrow = lax.axis_size("wide"), lax.axis_size("narrow")
    pairs = []
    for w in range(wide):
        for r in range(narrow):
            if cross:
                step, to = (-1 if w % 2 == 0 else 1), w ^ 1
            else:
                step, to = (1 if w % 2 == 0 else -1), w
            pairs.append((w * narrow + r, to * narrow + (r + step) % narrow))
    return lax.ppermute(value, ("wide", "narrow"), pairs)


def per_device(fields, conv1_weight, conv1_bias, conv2_weight):
    core = (lax.axis_index("wide") % 2).astype(jnp.int32).reshape(1)
    parity = jnp.asarray(split_parity(), BF16)
    order = jnp.asarray(row_order(), BF16)
    native, same, cross = call(
        pack_kernel,
        [((256, 128), F32), ((16, 256), F32), ((16, 256), F32)],
        [pltpu.VMEM((128, 256), F32)],
        core, fields, parity, order,
    )
    other = partner(native)
    same = edge_shift(same, False)
    cross = edge_shift(cross, True)

    w1 = conv1_weight.transpose(1, 0, 2).reshape(32, 108)
    w2 = conv2_weight.reshape(3, 3, 3, 6, 32).transpose(0, 2, 3, 1, 4)
    w2 = jnp.pad(w2, ((0, 0), (0, 0), (0, 2), (0, 0), (0, 0))).reshape(72, 96)
    w2 = jnp.pad(w2, ((0, 8), (0, 0)))
    bias = jnp.broadcast_to(conv1_bias[:, None], (32, 128))
    band1, band2 = call(
        weights_kernel,
        [((256, 512), BF16), ((480, 256), BF16)],
        [],
        w1, w2, jnp.asarray(place_conv1(), BF16), jnp.asarray(place_conv2(), BF16),
    )
    fixed = (band1, band2, bias, jnp.asarray(divergence_matrix(), BF16))

    base, *messages = call(
        assemble_kernel, [((8, 8, 8, 128), F32)] + MESSAGES, [], core, native, other, same, cross
    )
    scratch = [
        pltpu.VMEM((1440, 128), BF16),
        pltpu.VMEM((8, 480, 128), F32),
        pltpu.VMEM((288, 128), BF16),
    ]

    def exchange(coarse, to_left, to_right, down, up):
        from_left, from_right = chip_shift(to_right, 1), chip_shift(to_left, -1)
        going_up = jnp.concatenate([from_left[16:64], coarse[16:64], from_right[16:64], up], axis=0)
        going_down = jnp.concatenate([from_left[:48], coarse[:48], from_right[:48], down], axis=0)
        below, above = net_shift(going_up, 1), net_shift(going_down, -1)
        return coarse, from_left, from_right, below, above

    state_out = [((8, 8, 8, 128), F32)] + MESSAGES
    one, *messages = call(stage1_kernel, state_out, scratch, base, *exchange(*messages), *fixed)
    two, *messages = call(stage2_kernel, state_out, scratch, base, one, *exchange(*messages), *fixed)
    own, away = call(
        stage3_kernel,
        [((8, 4, 8, 128), F32)] * 2,
        scratch + [pltpu.VMEM((8, 8, 8, 128), F32)],
        core, base, two, *exchange(*messages), *fixed,
    )
    back = partner(away)
    (out,) = call(
        finish_kernel,
        [(fields.shape, F32)],
        [pltpu.VMEM((128, 256), F32)],
        core, own, back, parity, order,
    )
    return out


def solution(mesh):
    in_specs = (P(None, "net", "wide", "narrow"), P(), P(), P())
    out_specs = P(None, "net", "wide", "narrow")
    return jax.shard_map(
        per_device, mesh=mesh, in_specs=in_specs, out_specs=out_specs, check_vma=False
    )
```

profile of v0, /device:TPU:31, one launch (start us, length us, event | category | flops | bytes accessed | tf_op | source)
XLA Modules:
  0.0 92.2 jit_solution(4721047087187498430)
XLA Ops:
  0.0 3.0 %shard_map.91 = (f32[256,128]{1,0:T(8,128)}, f32[16,256]{1,0:T(8,128)}, f32[16,256]{1,0:T(8,128)}) custom-call(s32[1]{0:T(128)} %bitcast.core_ref, f32[4,8,4,256]{3,2,1,0:T(4,128)} %fields_ref.1, bf16[256,256]{1,0:T(8,128)(2,1)} %constant.32.clone.parity_ref, bf16[256,256]{1,0:T(8,128)(2,1)} %constant.33.clone.order_ref), custom_call_target="tpu_custom_call" | custom-call | tf_op jit(solution)/shard_map/pallas_call | solution.py:77
  3.0 0.7 collective-permute-start
  3.6 4.3 %collective-permute-start.1 = (f32[16,256]{1,0:T(8,128)}, f32[16,256]{1,0:T(8,128)S(1)}, u32[]{:S(2)}, u32[]{:S(2)}) collective-permute-start(f32[16,256]{1,0:T(8,128)} %get-tuple-element.31), channel_id=1, source_target_pairs={{0,8},{8,16},{16,24},{24,0},{32,56},{40,32},{48,40},{56,48},{64,72... | collective-permute-start | bytes 49160 | tf_op jit(solution)/shard_map/ppermute | solution.py:334
  8.0 0.0 collective-permute-start.2
  8.0 1.1 %collective-permute-done.1.same_ref = f32[16,256]{1,0:T(8,128)S(1)} collective-permute-done((f32[16,256]{1,0:T(8,128)}, f32[16,256]{1,0:T(8,128)S(1)}, u32[]{:S(2)}, u32[]{:S(2)}) %collective-permute-start.1) | collective-permute-done | bytes 16416 | tf_op jit(solution)/shard_map/ppermute | solution.py:334
  9.1 2.3 %collective-permute-done.2.cross_ref = f32[16,256]{1,0:T(8,128)S(1)} collective-permute-done((f32[16,256]{1,0:T(8,128)}, f32[16,256]{1,0:T(8,128)S(1)}, u32[]{:S(2)}, u32[]{:S(2)}) %collective-permute-start.2) | collective-permute-done | bytes 16416 | tf_op jit(solution)/shard_map/ppermute | solution.py:334
  11.4 0.0 collective-permute-done.other_ref
  11.4 0.0 copy-done.16
  11.4 0.6 copy-done.17
  12.0 0.7 copy-done
  12.6 2.2 %shard_map.92 = (f32[8,8,8,128]{3,2,1,0:T(8,128)}, bf16[64,128]{1,0:T(8,128)(2,1)}, bf16[128,128]{1,0:T(8,128)(2,1)}, bf16[128,128]{1,0:T(8,128)(2,1)}, bf16[64,...) custom-call(s32[1]{0:T(128)} %bitcast.core_ref, f32[256,128]{1,0:T(8,128)} %get-tuple-element.30.own_ref, f32[256,128]{1,0:T(8,128)} %copy-done, ...), custom_call_target="tpu_custom_call" | custom-call | tf_op jit(solution)/shard_map/pallas_call | solution.py:77
  14.8 0.1 collective-permute-start.3
  14.9 0.8 fusion.8
  15.7 0.0 copy-done.27
  15.7 1.5 %collective-permute-start.4 = (bf16[128,128]{1,0:T(8,128)(2,1)S(1)}, bf16[128,128]{1,0:T(8,128)(2,1)S(1)}, u32[]{:S(2)}, u32[]{:S(2)}) collective-permute-start(bf16[128,128]{1,0:T(8,128)(2,1)S(1)} %copy-done.27), channel_id=1, source_target_pairs={{0,192},{32,224},{64,0},{96,32},{128,64},{160,96},{192,128},{224,1... | collective-permute-start | bytes 98312 | tf_op jit(solution)/shard_map/ppermute | solution.py:312
  17.1 1.1 %collective-permute-done.3.refs_2_ = bf16[128,128]{1,0:T(8,128)(2,1)S(1)} collective-permute-done((bf16[128,128]{1,0:T(8,128)(2,1)}, bf16[128,128]{1,0:T(8,128)(2,1)S(1)}, u32[]{:S(2)}, u32[]{:S(2)}) %collective-permute-start.3) | collective-permute-done | bytes 32800 | tf_op jit(solution)/shard_map/ppermute | solution.py:312
  18.2 2.1 %collective-permute-done.4.refs_3_ = bf16[128,128]{1,0:T(8,128)(2,1)S(1)} collective-permute-done((bf16[128,128]{1,0:T(8,128)(2,1)S(1)}, bf16[128,128]{1,0:T(8,128)(2,1)S(1)}, u32[]{:S(2)}, u32[]{:S(2)}) %collective-permute-start.4) | collective-permute-done | bytes 32800 | tf_op jit(solution)/shard_map/ppermute | solution.py:312
  20.2 0.0 copy-done.2
  20.2 0.0 copy-done.23
  20.2 0.0 copy-start.20
  20.3 0.6 copy-done.3
  20.8 4.0 %collective-permute-start.5 = (bf16[208,128]{1,0:T(8,128)(2,1)S(1)}, bf16[208,128]{1,0:T(8,128)(2,1)S(1)}, u32[]{:S(2)}, u32[]{:S(2)}) collective-permute-start(bf16[208,128]{1,0:T(8,128)(2,1)S(1)} %pad_maximum_fusion), channel_id=1, source_target_pairs={{0,1},{1,2},{2,3},{3,4},{4,5},{5,6},{6,7},{7,0},{8,9},{9,10},{10,1... | collective-permute-start | bytes 159752 | tf_op jit(solution)/shard_map/ppermute | solution.py:317
  24.8 0.0 copy-done.20
  24.9 0.0 copy-start.14
  24.9 0.1 collective-permute-start.6
  25.0 0.6 copy-done.15
  25.6 0.7 copy.13.w1_ref
  26.4 0.1 reshape.16
  26.5 0.6 pad.9.w2_ref
  27.1 2.4 %shard_map.93 = (bf16[256,512]{1,0:T(8,128)(2,1)}, bf16[480,256]{1,0:T(8,128)(2,1)}) custom-call(bf16[32,108]{1,0:T(8,128)(2,1)} %copy.13.w1_ref, bf16[80,96]{1,0:T(8,128)(2,1)} %pad.9.w2_ref, bf16[108,4096]{1,0:T(8,128)(2,1)} %constant.34.clone.place1_ref, bf16[96,1536]{1,0:T(8,128)(2,1)} %constant.35.clone.place2_ref), custom_call_target="tpu_custom_call" | custom-call | tf_op jit(solution)/shard_map/pallas_call | solution.py:77
  29.5 0.0 collective-permute-done.5.refs_4_
  29.5 4.5 %collective-permute-done.6.refs_5_ = bf16[208,128]{1,0:T(8,128)(2,1)S(1)} collective-permute-done((bf16[208,128]{1,0:T(8,128)(2,1)S(1)}, bf16[208,128]{1,0:T(8,128)(2,1)S(1)}, u32[]{:S(2)}, u32[]{:S(2)}) %collective-permute-start.6) | collective-permute-done | bytes 53280 | tf_op jit(solution)/shard_map/ppermute | solution.py:317
  34.0 0.7 broadcast_in_dim.2.refs_8_
  34.7 3.8 %shard_map.94 = (f32[8,8,8,128]{3,2,1,0:T(8,128)}, bf16[64,128]{1,0:T(8,128)(2,1)}, bf16[128,128]{1,0:T(8,128)(2,1)}, bf16[128,128]{1,0:T(8,128)(2,1)}, bf16[64,...) custom-call(f32[8,8,8,128]{3,2,1,0:T(8,128)} %get-tuple-element.33.refs_0_.base_ref, bf16[64,128]{1,0:T(8,128)(2,1)} %get-tuple-element.34.refs_1_, ...), custom_call_target="tpu_custom_call" | custom-call | tf_op jit(solution)/shard_map/pallas_call | solution.py:77
  38.5 0.4 collective-permute-start.7
  38.9 0.8 fusion.7
  39.7 1.1 %collective-permute-start.8 = (bf16[128,128]{1,0:T(8,128)(2,1)S(1)}, bf16[128,128]{1,0:T(8,128)(2,1)S(1)}, u32[]{:S(2)}, u32[]{:S(2)}) collective-permute-start(bf16[128,128]{1,0:T(8,128)(2,1)S(1)} %copy-done.26), channel_id=1, source_target_pairs={{0,192},{32,224},{64,0},{96,32},{128,64},{160,96},{192,128},{224,1... | collective-permute-start | bytes 98312 | tf_op jit(solution)/shard_map/ppermute | solution.py:312
  40.8 0.7 collective-permute-done.7.refs_2_
  41.6 2.1 %collective-permute-done.8.refs_3_ = bf16[128,128]{1,0:T(8,128)(2,1)S(1)} collective-permute-done((bf16[128,128]{1,0:T(8,128)(2,1)S(1)}, bf16[128,128]{1,0:T(8,128)(2,1)S(1)}, u32[]{:S(2)}, u32[]{:S(2)}) %collective-permute-start.8) | collective-permute-done | bytes 32800 | tf_op jit(solution)/shard_map/ppermute | solution.py:312
  43.8 0.6 copy-done.7
  44.3 2.3 %collective-permute-start.9 = (bf16[208,128]{1,0:T(8,128)(2,1)S(1)}, bf16[208,128]{1,0:T(8,128)(2,1)S(1)}, u32[]{:S(2)}, u32[]{:S(2)}) collective-permute-start(bf16[208,128]{1,0:T(8,128)(2,1)S(1)} %pad_maximum_fusion.2), channel_id=1, source_target_pairs={{0,1},{1,2},{2,3},{3,4},{4,5},{5,6},{6,7},{7,0},{8,9},{9,10},{10,1... | collective-permute-start | bytes 159752 | tf_op jit(solution)/shard_map/ppermute | solution.py:317
  46.6 0.3 collective-permute-start.10
  46.9 0.9 %collective-permute-done.9.refs_4_ = bf16[208,128]{1,0:T(8,128)(2,1)S(1)} collective-permute-done((bf16[208,128]{1,0:T(8,128)(2,1)S(1)}, bf16[208,128]{1,0:T(8,128)(2,1)S(1)}, u32[]{:S(2)}, u32[]{:S(2)}) %collective-permute-start.9) | collective-permute-done | bytes 53280 | tf_op jit(solution)/shard_map/ppermute | solution.py:317
  47.8 8.0 %collective-permute-done.10.refs_5_ = bf16[208,128]{1,0:T(8,128)(2,1)S(1)} collective-permute-done((bf16[208,128]{1,0:T(8,128)(2,1)S(1)}, bf16[208,128]{1,0:T(8,128)(2,1)S(1)}, u32[]{:S(2)}, u32[]{:S(2)}) %collective-permute-start.10) | collective-permute-done | bytes 53280 | tf_op jit(solution)/shard_map/ppermute | solution.py:317
  55.9 0.6 copy-done.11
  56.5 3.9 %shard_map.95 = (f32[8,8,8,128]{3,2,1,0:T(8,128)}, bf16[64,128]{1,0:T(8,128)(2,1)}, bf16[128,128]{1,0:T(8,128)(2,1)}, bf16[128,128]{1,0:T(8,128)(2,1)}, bf16[64,...) custom-call(f32[8,8,8,128]{3,2,1,0:T(8,128)} %get-tuple-element.33.refs_0_.base_ref, ...), custom_call_target="tpu_custom_call" | custom-call | tf_op jit(solution)/shard_map/pallas_call | solution.py:77
  60.4 0.1 collective-permute-start.11
  60.5 0.8 fusion.6
  61.3 1.5 %collective-permute-start.12 = (bf16[128,128]{1,0:T(8,128)(2,1)S(1)}, bf16[128,128]{1,0:T(8,128)(2,1)S(1)}, u32[]{:S(2)}, u32[]{:S(2)}) collective-permute-start(bf16[128,128]{1,0:T(8,128)(2,1)S(1)} %copy-done.25), channel_id=1, source_target_pairs={{0,192},{32,224},{64,0},{96,32},{128,64},{160,96},{192,128},{224,1... | collective-permute-start | bytes 98312 | tf_op jit(solution)/shard_map/ppermute | solution.py:312
  62.7 0.7 collective-permute-done.11.refs_2_
  63.5 1.8 %collective-permute-done.12.refs_3_ = bf16[128,128]{1,0:T(8,128)(2,1)S(1)} collective-permute-done((bf16[128,128]{1,0:T(8,128)(2,1)S(1)}, bf16[128,128]{1,0:T(8,128)(2,1)S(1)}, u32[]{:S(2)}, u32[]{:S(2)}) %collective-permute-start.12) | collective-permute-done | bytes 32800 | tf_op jit(solution)/shard_map/ppermute | solution.py:312
  65.3 0.0 copy-done.4
  65.3 0.6 copy-done.6
  65.9 0.0 collective-permute-start.13
  65.9 0.1 copy-done.18
  66.0 1.4 %collective-permute-start.14 = (bf16[208,128]{1,0:T(8,128)(2,1)S(1)}, bf16[208,128]{1,0:T(8,128)(2,1)S(1)}, u32[]{:S(2)}, u32[]{:S(2)}) collective-permute-start(bf16[208,128]{1,0:T(8,128)(2,1)S(1)} %pad_maximum_fusion.5), channel_id=1, source_target_pairs={{0,7},{1,0},{2,1},{3,2},{4,3},{5,4},{6,5},{7,6},{8,15},{9,8},{10,9... | collective-permute-start | bytes 159752 | tf_op jit(solution)/shard_map/ppermute | solution.py:317
  67.4 1.7 %collective-permute-done.13.refs_4_ = bf16[208,128]{1,0:T(8,128)(2,1)S(1)} collective-permute-done((bf16[208,128]{1,0:T(8,128)(2,1)S(1)}, bf16[208,128]{1,0:T(8,128)(2,1)S(1)}, u32[]{:S(2)}, u32[]{:S(2)}) %collective-permute-start.13) | collective-permute-done | bytes 53280 | tf_op jit(solution)/shard_map/ppermute | solution.py:317
  69.1 5.9 %collective-permute-done.14.refs_5_ = bf16[208,128]{1,0:T(8,128)(2,1)S(1)} collective-permute-done((bf16[208,128]{1,0:T(8,128)(2,1)S(1)}, bf16[208,128]{1,0:T(8,128)(2,1)S(1)}, u32[]{:S(2)}, u32[]{:S(2)}) %collective-permute-start.14) | collective-permute-done | bytes 53280 | tf_op jit(solution)/shard_map/ppermute | solution.py:317
  75.0 0.6 copy-done.10
  75.6 3.9 %shard_map.96 = (f32[8,4,8,128]{3,2,1,0:T(8,128)}, f32[8,4,8,128]{3,2,1,0:T(8,128)}) custom-call(s32[1]{0:T(128)} %bitcast.core_ref, f32[8,8,8,128]{3,2,1,0:T(8,128)} %get-tuple-element.33.refs_0_.base_ref, f32[8,8,8,128]{3,2,1,0:T(8,128)} %get-tuple-element.47.refs_0_, bf16[64,128]{1,0:T(8,128)(2,1)} %get-tuple-element.48.refs_1_, ...), custom_call_target="tpu_custom_call" | custom-call | tf_op jit(solution)/shard_map/pallas_call | solution.py:77
  79.5 7.9 %collective-permute-start.15 = (f32[8,4,8,128]{3,2,1,0:T(8,128)}, f32[8,4,8,128]{3,2,1,0:T(8,128)S(1)}, u32[]{:S(2)}, u32[]{:S(2)}) collective-permute-start(f32[8,4,8,128]{3,2,1,0:T(8,128)} %get-tuple-element.54), channel_id=1, source_target_pairs={{0,32},{32,0},{64,96},{96,64},{128,160},{160,128},{192,224},{224,1... | collective-permute-start | bytes 393224 | tf_op jit(solution)/shard_map/ppermute | solution.py:321
  87.4 1.2 %collective-permute-done.15.other_ref = f32[8,4,8,128]{3,2,1,0:T(8,128)S(1)} collective-permute-done((f32[8,4,8,128]{3,2,1,0:T(8,128)}, f32[8,4,8,128]{3,2,1,0:T(8,128)S(1)}, u32[]{:S(2)}, u32[]{:S(2)}) %collective-permute-start.15) | collective-permute-done | bytes 131104 | tf_op jit(solution)/shard_map/ppermute | solution.py:321
  88.6 0.7 copy-done.1
  89.2 2.9 %shard_map.97 = f32[4,8,4,256]{3,2,1,0:T(4,128)} custom-call(s32[1]{0:T(128)} %bitcast.core_ref, f32[8,4,8,128]{3,2,1,0:T(8,128)} %get-tuple-element.53.own_ref, f32[8,4,8,128]{3,2,1,0:T(8,128)} %copy-done.1, bf16[256,256]{1,0:T(8,128)(2,1)} %constant.32.clone.parity_ref, bf16[256,256]{1,0:T(8,128)(2,1)} %constant.33.clone.order_ref), custom_call_target="tpu_custom_call" | custom-call | tf_op jit(solution)/shard_map/pallas_call | solution.py:77
  (54 shorter events, 0.2 us)
Async XLA Ops:
  3.0 8.4 %collective-permute-start = (f32[256,128]{1,0:T(8,128)}, f32[256,128]{1,0:T(8,128)S(1)}, u32[]{:S(2)}, u32[]{:S(2)}) collective-permute-start(f32[256,128]{1,0:T(8,128)} %get-tuple-element.30.own_ref), channel_id=1, source_target_pairs={{0,32},{32,0},{64,96},{96,64},{128,160},{160,128},{192,224},{224,1... | collective-permute-start | bytes 393224 | tf_op jit(solution)/shard_map/ppermute | solution.py:321
  3.6 5.4 %collective-permute-start.1 = (f32[16,256]{1,0:T(8,128)}, f32[16,256]{1,0:T(8,128)S(1)}, u32[]{:S(2)}, u32[]{:S(2)}) collective-permute-start(f32[16,256]{1,0:T(8,128)} %get-tuple-element.31), channel_id=1, source_target_pairs={{0,8},{8,16},{16,24},{24,0},{32,56},{40,32},{48,40},{56,48},{64,72... | collective-permute-start | bytes 49160 | tf_op jit(solution)/shard_map/ppermute | solution.py:334
  8.0 3.4 %collective-permute-start.2 = (f32[16,256]{1,0:T(8,128)}, f32[16,256]{1,0:T(8,128)S(1)}, u32[]{:S(2)}, u32[]{:S(2)}) collective-permute-start(f32[16,256]{1,0:T(8,128)} %get-tuple-element.32), channel_id=1, source_target_pairs={{0,56},{8,32},{16,40},{24,48},{32,8},{40,16},{48,24},{56,0},{64,12... | collective-permute-start | bytes 49160 | tf_op jit(solution)/shard_map/ppermute | solution.py:334
  9.1 2.3 %copy-start.16 = (f32[16,256]{1,0:T(8,128)}, f32[16,256]{1,0:T(8,128)S(1)}, u32[]{:S(2)}) copy-start(f32[16,256]{1,0:T(8,128)S(1)} %collective-permute-done.1.same_ref) | copy-start | bytes 49156
  11.4 0.6 copy-start.17
  12.0 0.7 copy-start
  14.8 0.9 copy-start.27
  14.8 3.4 %collective-permute-start.3 = (bf16[128,128]{1,0:T(8,128)(2,1)}, bf16[128,128]{1,0:T(8,128)(2,1)S(1)}, u32[]{:S(2)}, u32[]{:S(2)}) collective-permute-start(bf16[128,128]{1,0:T(8,128)(2,1)} %get-tuple-element.35), channel_id=1, source_target_pairs={{0,64},{32,96},{64,128},{96,160},{128,192},{160,224},{192,0},{224,... | collective-permute-start | bytes 98312 | tf_op jit(solution)/shard_map/ppermute | solution.py:312
  15.7 4.6 %collective-permute-start.4 = (bf16[128,128]{1,0:T(8,128)(2,1)S(1)}, bf16[128,128]{1,0:T(8,128)(2,1)S(1)}, u32[]{:S(2)}, u32[]{:S(2)}) collective-permute-start(bf16[128,128]{1,0:T(8,128)(2,1)S(1)} %copy-done.27), channel_id=1, source_target_pairs={{0,192},{32,224},{64,0},{96,32},{128,64},{160,96},{192,128},{224,1... | collective-permute-start | bytes 98312 | tf_op jit(solution)/shard_map/ppermute | solution.py:312
  18.2 2.1 %copy-start.2 = (bf16[128,128]{1,0:T(8,128)(2,1)}, bf16[128,128]{1,0:T(8,128)(2,1)S(1)}, u32[]{:S(2)}) copy-start(bf16[128,128]{1,0:T(8,128)(2,1)S(1)} %collective-permute-done.3.refs_2_) | copy-start | bytes 98308
  18.2 2.1 %copy-start.23 = (bf16[64,128]{1,0:T(8,128)(2,1)S(1)}, bf16[64,128]{1,0:T(8,128)(2,1)}, u32[]{:S(2)}) copy-start(bf16[64,128]{1,0:T(8,128)(2,1)} %get-tuple-element.37) | copy-start | bytes 49156
  20.2 0.6 copy-start.3
  20.2 4.6 %copy-start.20 = (bf16[64,128]{1,0:T(8,128)(2,1)S(1)}, bf16[64,128]{1,0:T(8,128)(2,1)}, u32[]{:S(2)}) copy-start(bf16[64,128]{1,0:T(8,128)(2,1)} %get-tuple-element.38) | copy-start | bytes 49156
  20.8 8.7 %collective-permute-start.5 = (bf16[208,128]{1,0:T(8,128)(2,1)S(1)}, bf16[208,128]{1,0:T(8,128)(2,1)S(1)}, u32[]{:S(2)}, u32[]{:S(2)}) collective-permute-start(bf16[208,128]{1,0:T(8,128)(2,1)S(1)} %pad_maximum_fusion), channel_id=1, source_target_pairs={{0,1},{1,2},{2,3},{3,4},{4,5},{5,6},{6,7},{7,0},{8,9},{9,10},{10,1... | collective-permute-start | bytes 159752 | tf_op jit(solution)/shard_map/ppermute | solution.py:317
  24.8 0.7 copy-start.15
  24.9 1.4 %copy-start.14 = (bf16[27,6,32]{2,0,1:T(8,128)(2,1)S(1)}, bf16[27,6,32]{2,0,1:T(8,128)(2,1)}, u32[]{:S(2)}) copy-start(bf16[27,6,32]{2,0,1:T(8,128)(2,1)} %param.12) | copy-start | bytes 31108
  24.9 9.1 %collective-permute-start.6 = (bf16[208,128]{1,0:T(8,128)(2,1)S(1)}, bf16[208,128]{1,0:T(8,128)(2,1)S(1)}, u32[]{:S(2)}, u32[]{:S(2)}) collective-permute-start(bf16[208,128]{1,0:T(8,128)(2,1)S(1)} %pad_maximum_fusion.1), channel_id=1, source_target_pairs={{0,7},{1,0},{2,1},{3,2},{4,3},{5,4},{6,5},{7,6},{8,15},{9,8},{10,9... | collective-permute-start | bytes 159752 | tf_op jit(solution)/shard_map/ppermute | solution.py:317
  27.1 6.9 %copy-start.24 = (f32[32]{0:T(128)S(1)}, f32[32]{0:T(128)}, u32[]{:S(2)}) copy-start(f32[32]{0:T(128)} %param.11) | copy-start | bytes 388
  29.5 5.2 %copy-start.12 = (bf16[208,128]{1,0:T(8,128)(2,1)}, bf16[208,128]{1,0:T(8,128)(2,1)S(1)}, u32[]{:S(2)}) copy-start(bf16[208,128]{1,0:T(8,128)(2,1)S(1)} %collective-permute-done.5.refs_4_) | copy-start | bytes 159748
  34.0 0.7 copy-start.13
  38.5 1.2 %copy-start.26 = (bf16[128,128]{1,0:T(8,128)(2,1)S(1)}, bf16[128,128]{1,0:T(8,128)(2,1)}, u32[]{:S(2)}) copy-start(bf16[128,128]{1,0:T(8,128)(2,1)} %get-tuple-element.44) | copy-start | bytes 98308
  38.5 3.0 %collective-permute-start.7 = (bf16[128,128]{1,0:T(8,128)(2,1)}, bf16[128,128]{1,0:T(8,128)(2,1)S(1)}, u32[]{:S(2)}, u32[]{:S(2)}) collective-permute-start(bf16[128,128]{1,0:T(8,128)(2,1)} %get-tuple-element.43), channel_id=1, source_target_pairs={{0,64},{32,96},{64,128},{96,160},{128,192},{160,224},{192,0},{224,... | collective-permute-start | bytes 98312 | tf_op jit(solution)/shard_map/ppermute | solution.py:312
  39.7 4.0 %collective-permute-start.8 = (bf16[128,128]{1,0:T(8,128)(2,1)S(1)}, bf16[128,128]{1,0:T(8,128)(2,1)S(1)}, u32[]{:S(2)}, u32[]{:S(2)}) collective-permute-start(bf16[128,128]{1,0:T(8,128)(2,1)S(1)} %copy-done.26), channel_id=1, source_target_pairs={{0,192},{32,224},{64,0},{96,32},{128,64},{160,96},{192,128},{224,1... | collective-permute-start | bytes 98312 | tf_op jit(solution)/shard_map/ppermute | solution.py:312
  41.6 2.2 %copy-start.5 = (bf16[128,128]{1,0:T(8,128)(2,1)}, bf16[128,128]{1,0:T(8,128)(2,1)S(1)}, u32[]{:S(2)}) copy-start(bf16[128,128]{1,0:T(8,128)(2,1)S(1)} %collective-permute-done.7.refs_2_) | copy-start | bytes 98308
  41.6 2.2 %copy-start.22 = (bf16[64,128]{1,0:T(8,128)(2,1)S(1)}, bf16[64,128]{1,0:T(8,128)(2,1)}, u32[]{:S(2)}) copy-start(bf16[64,128]{1,0:T(8,128)(2,1)} %get-tuple-element.45) | copy-start | bytes 49156
  43.7 0.6 copy-start.7
  43.7 2.9 %copy-start.19 = (bf16[64,128]{1,0:T(8,128)(2,1)S(1)}, bf16[64,128]{1,0:T(8,128)(2,1)}, u32[]{:S(2)}) copy-start(bf16[64,128]{1,0:T(8,128)(2,1)} %get-tuple-element.46) | copy-start | bytes 49156
  44.3 3.5 %collective-permute-start.9 = (bf16[208,128]{1,0:T(8,128)(2,1)S(1)}, bf16[208,128]{1,0:T(8,128)(2,1)S(1)}, u32[]{:S(2)}, u32[]{:S(2)}) collective-permute-start(bf16[208,128]{1,0:T(8,128)(2,1)S(1)} %pad_maximum_fusion.2), channel_id=1, source_target_pairs={{0,1},{1,2},{2,3},{3,4},{4,5},{5,6},{6,7},{7,0},{8,9},{9,10},{10,1... | collective-permute-start | bytes 159752 | tf_op jit(solution)/shard_map/ppermute | solution.py:317
  46.6 9.3 %collective-permute-start.10 = (bf16[208,128]{1,0:T(8,128)(2,1)S(1)}, bf16[208,128]{1,0:T(8,128)(2,1)S(1)}, u32[]{:S(2)}, u32[]{:S(2)}) collective-permute-start(bf16[208,128]{1,0:T(8,128)(2,1)S(1)} %pad_maximum_fusion.3), channel_id=1, source_target_pairs={{0,7},{1,0},{2,1},{3,2},{4,3},{5,4},{6,5},{7,6},{8,15},{9,8},{10,9... | collective-permute-start | bytes 159752 | tf_op jit(solution)/shard_map/ppermute | solution.py:317
  47.8 8.1 %copy-start.9 = (bf16[208,128]{1,0:T(8,128)(2,1)}, bf16[208,128]{1,0:T(8,128)(2,1)S(1)}, u32[]{:S(2)}) copy-start(bf16[208,128]{1,0:T(8,128)(2,1)S(1)} %collective-permute-done.9.refs_4_) | copy-start | bytes 159748
  55.9 0.6 copy-start.11
  60.4 0.9 copy-start.25
  60.4 3.0 %collective-permute-start.11 = (bf16[128,128]{1,0:T(8,128)(2,1)}, bf16[128,128]{1,0:T(8,128)(2,1)S(1)}, u32[]{:S(2)}, u32[]{:S(2)}) collective-permute-start(bf16[128,128]{1,0:T(8,128)(2,1)} %get-tuple-element.49), channel_id=1, source_target_pairs={{0,64},{32,96},{64,128},{96,160},{128,192},{160,224},{192,0},{224,... | collective-permute-start | bytes 98312 | tf_op jit(solution)/shard_map/ppermute | solution.py:312
  61.3 4.0 %collective-permute-start.12 = (bf16[128,128]{1,0:T(8,128)(2,1)S(1)}, bf16[128,128]{1,0:T(8,128)(2,1)S(1)}, u32[]{:S(2)}, u32[]{:S(2)}) collective-permute-start(bf16[128,128]{1,0:T(8,128)(2,1)S(1)} %copy-done.25), channel_id=1, source_target_pairs={{0,192},{32,224},{64,0},{96,32},{128,64},{160,96},{192,128},{224,1... | collective-permute-start | bytes 98312 | tf_op jit(solution)/shard_map/ppermute | solution.py:312
  63.5 1.8 %copy-start.4 = (bf16[128,128]{1,0:T(8,128)(2,1)}, bf16[128,128]{1,0:T(8,128)(2,1)S(1)}, u32[]{:S(2)}) copy-start(bf16[128,128]{1,0:T(8,128)(2,1)S(1)} %collective-permute-done.11.refs_2_) | copy-start | bytes 98308
  63.5 1.8 %copy-start.21 = (bf16[64,128]{1,0:T(8,128)(2,1)S(1)}, bf16[64,128]{1,0:T(8,128)(2,1)}, u32[]{:S(2)}) copy-start(bf16[64,128]{1,0:T(8,128)(2,1)} %get-tuple-element.51) | copy-start | bytes 49156
  65.3 0.6 copy-start.6
  65.3 0.7 copy-start.18
  65.9 3.3 %collective-permute-start.13 = (bf16[208,128]{1,0:T(8,128)(2,1)S(1)}, bf16[208,128]{1,0:T(8,128)(2,1)S(1)}, u32[]{:S(2)}, u32[]{:S(2)}) collective-permute-start(bf16[208,128]{1,0:T(8,128)(2,1)S(1)} %pad_maximum_fusion.4), channel_id=1, source_target_pairs={{0,1},{1,2},{2,3},{3,4},{4,5},{5,6},{6,7},{7,0},{8,9},{9,10},{10,1... | collective-permute-start | bytes 159752 | tf_op jit(solution)/shard_map/ppermute | solution.py:317
  66.0 9.0 %collective-permute-start.14 = (bf16[208,128]{1,0:T(8,128)(2,1)S(1)}, bf16[208,128]{1,0:T(8,128)(2,1)S(1)}, u32[]{:S(2)}, u32[]{:S(2)}) collective-permute-start(bf16[208,128]{1,0:T(8,128)(2,1)S(1)} %pad_maximum_fusion.5), channel_id=1, source_target_pairs={{0,7},{1,0},{2,1},{3,2},{4,3},{5,4},{6,5},{7,6},{8,15},{9,8},{10,9... | collective-permute-start | bytes 159752 | tf_op jit(solution)/shard_map/ppermute | solution.py:317
  69.1 5.9 %copy-start.8 = (bf16[208,128]{1,0:T(8,128)(2,1)}, bf16[208,128]{1,0:T(8,128)(2,1)S(1)}, u32[]{:S(2)}) copy-start(bf16[208,128]{1,0:T(8,128)(2,1)S(1)} %collective-permute-done.13.refs_4_) | copy-start | bytes 159748
  75.0 0.6 copy-start.10
  79.5 9.1 %collective-permute-start.15 = (f32[8,4,8,128]{3,2,1,0:T(8,128)}, f32[8,4,8,128]{3,2,1,0:T(8,128)S(1)}, u32[]{:S(2)}, u32[]{:S(2)}) collective-permute-start(f32[8,4,8,128]{3,2,1,0:T(8,128)} %get-tuple-element.54), channel_id=1, source_target_pairs={{0,32},{32,0},{64,96},{96,64},{128,160},{160,128},{192,224},{224,1... | collective-permute-start | bytes 393224 | tf_op jit(solution)/shard_map/ppermute | solution.py:321
  88.6 0.7 copy-start.1
where the time goes:
time: 93 us; the launch traced here: 92.2 us
  waiting for transfers between devices  34.1 us (37%)
  starting transfers between devices  25.6 us (28%)
  Pallas kernels  22 us (24%)
  local copies, waits for them, and re-layouts  10.2 us (11%)
    pallas_call x7, Pallas kernels, call(): pl.pallas_call(kernel, out_shape=[jax.ShapeDtypeStruct(s, d) for s, d in...  22 us
    ppermute x6, waiting for transfers between devices, net_shift(): lax.ppermute(value, 'net', [(i, (i + step) % size) for i in range(size)])  21.1 us
    ppermute x2, starting transfers between devices, partner(): lax.ppermute(value, 'wide', [(i, i ^ 1) for i in range(lax.axis_size('wid...  8.58 us
    ppermute x6, waiting for transfers between devices, chip_shift(): lax.ppermute(value, 'wide', [(i, (i + 2 * step) % size) for i in range(si...  8.49 us
    ppermute x6, starting transfers between devices, net_shift(): lax.ppermute(value, 'net', [(i, (i + step) % size) for i in range(size)])  8.07 us
    unnamed x56, local copies, waits for them, and re-layouts  5.66 us
    ppermute x6, starting transfers between devices, chip_shift(): lax.ppermute(value, 'wide', [(i, (i + 2 * step) % size) for i in range(si...  4.57 us
    ppermute x2, starting transfers between devices, edge_shift(): return lax.ppermute(value, ('wide', 'narrow'), pairs)  4.35 us
  transfers between devices with their start and end apart: 16, of which 14 were waited for; matrix products, arithmetic and copies ran while one was open for 4% of the time, Pallas kernels for 3%

commit v1 on v0

v1 whole, which is shorter than its diff:
```python
import jax
import jax.numpy as jnp
import numpy as np
from jax import lax
from jax.experimental import pallas as pl
from jax.experimental.pallas import tpu as pltpu
from jax.sharding import PartitionSpec as P

time_step = 0.2
viscosity = 0.05
EDGE = 9
HALF = 64
F32 = jnp.float32
BF16 = jnp.bfloat16
VM = pl.BlockSpec(memory_space=pltpu.VMEM)
SM = pl.BlockSpec(memory_space=pltpu.SMEM)


def split_parity():
    m = np.zeros((256, 256), np.float32)
    for l in range(128):
        m[2 * l, l] = 1.0
        m[2 * l + 1, 128 + l] = 1.0
    return m


def divergence_matrix():
    m = np.zeros((4, 2, 4, 5, 6, 8), np.float32)
    sx, sy, sz = (0, 3, 4), (3, 1, 5), (4, 5, 2)
    for x in range(4):
        for comp in range(3):
            m[x, :, comp, 1, x + 2, sx[comp]] += 0.25
            m[x, :, comp, 1, x, sx[comp]] -= 0.25
            m[x, :, comp, 4, x + 1, sy[comp]] += 0.25
            m[x, :, comp, 3, x + 1, sy[comp]] -= 0.25
            m[x, :, comp, 2, x + 1, sz[comp]] += 0.25
            m[x, :, comp, 0, x + 1, sz[comp]] -= 0.25
    return m.reshape(32, 240)


def near(value):
    return pltpu.with_memory_space_constraint(value, pltpu.VMEM)


def call(kernel, outs, scratch, info, *args, result=None):
    return pl.pallas_call(
        kernel,
        out_shape=result or [pltpu.VMEM(s, d) for s, d in outs],
        in_specs=[SM] + [VM] * len(args),
        out_specs=VM if result else [VM] * len(outs),
        scratch_shapes=scratch,
    )(info, *args)


def lanes_of(shape):
    return lax.broadcasted_iota(jnp.int32, shape, len(shape) - 1)


def thirds(value):
    first = value.astype(BF16)
    rest = value - first.astype(F32)
    second = rest.astype(BF16)
    third = (rest - second.astype(F32)).astype(BF16)
    return jnp.concatenate([first, second, third], axis=0)


def pack_kernel(info_ref, fields_ref, parity_ref, native_ref, same_ref, cross_ref, flat):
    core = info_ref[0]
    for c in range(4):
        for z in range(8):
            flat[pl.ds((c * 8 + z) * 4, 4), :] = fields_ref[c, z]
    split = jnp.dot(thirds(flat[...]), parity_ref[...], preferred_element_type=F32)
    parts = split[:128] + split[128:256] + split[256:]
    for p in range(2):
        for c in range(4):
            native_ref[pl.ds(p * 4 + c, 32, stride=8), :] = parts[
                c * 32 : (c + 1) * 32, p * 128 : (p + 1) * 128
            ]
    lane = lanes_of((32, 128))
    for out_ref, take_last in ((same_ref, core == 0), (cross_ref, core == 1)):
        offset = jnp.where(take_last, EDGE, 0)
        total = jnp.zeros((32, 128), F32)
        for g in range(8):
            moved = pltpu.roll(native_ref[pl.ds(g * 32, 32), :], g * 16 + offset, 1)
            total = jnp.where((lane >= g * 16) & (lane < g * 16 + EDGE), moved, total)
        out_ref[...] = total


def emit_messages(info_ref, q_ref, wide_a_ref, wide_b_ref, net_a_ref, net_b_ref):
    chip_even, net_even = info_ref[1] == 0, info_ref[2] == 0
    low = lax.broadcasted_iota(jnp.int32, (8, 128), 0) < 4
    slabs = []
    for zc in range(4):
        means = []
        for xc in range(4):
            t = (q_ref[2 * zc, 2 * xc] + q_ref[2 * zc, 2 * xc + 1]) + (
                q_ref[2 * zc + 1, 2 * xc] + q_ref[2 * zc + 1, 2 * xc + 1]
            )
            means.append((t + pltpu.roll(t, 4, 0)) * 0.125)
        slab = jnp.concatenate(
            [jnp.where(low, means[0], means[1]), jnp.where(low, means[2], means[3])], axis=0
        )
        slabs.append(slab)
        wide_a_ref[pl.ds(zc * 16, 16), :] = slab.astype(BF16)
        wide_b_ref[pl.ds(zc * 16, 16), :] = slab.astype(BF16)
    for zc in range(3):
        at = pl.ds(zc * 16, 16)
        net_a_ref[at, :] = jnp.where(net_even, slabs[zc + 1], slabs[zc]).astype(BF16)
        net_b_ref[at, :] = jnp.where(net_even, slabs[zc], slabs[zc + 1]).astype(BF16)
    xa, xb = jnp.where(chip_even, 7, 0), jnp.where(chip_even, 0, 7)
    za, zb = jnp.where(net_even, 7, 0), jnp.where(net_even, 0, 7)
    for z in range(0, 8, 2):
        at = pl.ds(64 + z * 8, 16)
        wide_a_ref[at, :] = jnp.concatenate([q_ref[z, xa], q_ref[z + 1, xa]], axis=0).astype(BF16)
        wide_b_ref[at, :] = jnp.concatenate([q_ref[z, xb], q_ref[z + 1, xb]], axis=0).astype(BF16)
    for x in range(0, 8, 2):
        at = pl.ds(48 + x * 8, 16)
        net_a_ref[at, :] = jnp.concatenate([q_ref[za, x], q_ref[za, x + 1]], axis=0).astype(BF16)
        net_b_ref[at, :] = jnp.concatenate([q_ref[zb, x], q_ref[zb, x + 1]], axis=0).astype(BF16)


MESSAGES = [((128, 128), BF16), ((128, 128), BF16), ((112, 128), BF16), ((112, 128), BF16)]


def assemble_kernel(
    info_ref, own_ref, other_ref, same_ref, cross_ref, q_ref, wide_a_ref, wide_b_ref, net_a_ref, net_b_ref
):
    core = info_ref[0]
    lane = lanes_of((32, 128))
    begin = jnp.where(core == 0, EDGE, 0)
    inside = (lane >= begin) & (lane < begin + HALF + EDGE)
    shift = jnp.where(core == 0, EDGE, HALF + EDGE)
    start = jnp.where(core == 0, 128, HALF + EDGE + 128)
    for block_ref, edge_ref, position in ((own_ref, same_ref, core), (other_ref, cross_ref, 1 - core)):
        edge = edge_ref[...]
        for g in range(8):
            block = pltpu.roll(block_ref[pl.ds(g * 32, 32), :], shift, 1)
            block = jnp.where(inside, block, pltpu.roll(edge, lax.rem(start - g * 16, 128), 1))
            q_ref[g, pl.ds(position * 4, 4)] = block.reshape(4, 8, 128)
    emit_messages(info_ref, q_ref, wide_a_ref, wide_b_ref, net_a_ref, net_b_ref)


def weights_kernel(info_ref, w1_ref, w2_ref, b_ref, band1_ref, band2_ref, bias_ref, flat1, flat2):
    flat1[...] = jnp.zeros_like(flat1)
    flat2[...] = jnp.zeros_like(flat2)
    for dz in range(3):
        for dx in range(3):
            for dy in range(3):
                tap = 9 * dz + 3 * dx + dy
                flat1[:, pl.ds((dz * 3 + dy) * 48 + (1 + dx) * 4, 4)] = w1_ref[tap].astype(F32)
                flat2[pl.ds((dz * 3 + dy) * 8, 6), pl.ds(dx * 32, 32)] = w2_ref[tap].astype(F32)
    for xo in range(8):
        band1_ref[pl.ds(xo * 32, 32), :] = pltpu.roll(flat1[...], 4 * xo, 1).astype(BF16)
    for xo in range(6):
        band2_ref[pl.ds(xo * 80, 80), :] = pltpu.roll(flat2[...], 32 * xo, 1).astype(BF16)
    square = jnp.broadcast_to(b_ref[...], (32, 32))
    diagonal = lanes_of((32, 32)) == lax.broadcasted_iota(jnp.int32, (32, 32), 0)
    column = jnp.sum(jnp.where(diagonal, square, 0.0), axis=1, keepdims=True)
    bias_ref[...] = jnp.broadcast_to(column, (32, 128))


def stage_body(
    info_ref, q_ref, coarse_ref, wide_a_ref, wide_b_ref, net_a_ref, net_b_ref,
    band1_ref, band2_ref, bias_ref, div_ref, columns, parts, stress, update, new_ref,
):
    chip_even = info_ref[1] == 0
    net_even = info_ref[2] == 0
    left_at, right_at = jnp.where(chip_even, 160, 112), jnp.where(chip_even, 112, 160)

    def slab(j, pieces):
        for i, piece in enumerate(pieces):
            wide = piece.astype(F32)
            columns[pl.ds(j * 144 + i * 16, 16), :] = pltpu.roll(wide, 1, 1).astype(BF16)
            columns[pl.ds(j * 144 + 48 + i * 16, 16), :] = wide.astype(BF16)
            columns[pl.ds(j * 144 + 96 + i * 16, 16), :] = pltpu.roll(wide, 127, 1).astype(BF16)

    def wide_rows(start):
        a = wide_a_ref[pl.ds(start, 16), :].astype(F32)
        b = wide_b_ref[pl.ds(start, 16), :].astype(F32)
        return jnp.where(chip_even, b, a), jnp.where(chip_even, a, b)

    def net_rows(start):
        a = net_a_ref[pl.ds(start, 16), :].astype(F32)
        b = net_b_ref[pl.ds(start, 16), :].astype(F32)
        return jnp.where(net_even, b, a), jnp.where(net_even, a, b)

    bias = jnp.concatenate([bias_ref[...]] * 8, axis=0)
    bias = jnp.concatenate([bias, bias], axis=1)

    def layers(j, k):
        rows = jnp.concatenate(
            [columns[pl.ds(j * 144, 432), :], columns[pl.ds(k * 144, 432), :]], axis=1
        )
        pre = jnp.dot(band1_ref[:, :432], rows, preferred_element_type=F32) + bias
        inner = pre * (0.7978845608028654 + 0.7978845608028654 * 0.044715 * (pre * pre))
        half = 0.5 * pre
        hidden = (half + half * jnp.tanh(inner)).astype(BF16)
        both = jnp.dot(band2_ref[...], hidden, preferred_element_type=F32)
        parts[j] = both[:, :128]
        parts[k] = both[:, 128:]

    for j in range(3, 7):
        at = (j - 3) * 16
        left, right = wide_rows(at)
        slab(j, [left, coarse_ref[pl.ds(at, 16), :], right])
    layers(3, 4)
    for i in range(3):
        starts = [pl.multiple_of(at + i * 16, 16) for at in (left_at, 0, right_at)]
        below, above = zip(*[net_rows(start) for start in starts])
        slab(i, below)
        slab(7 + i, above)
    layers(1, 2)
    layers(5, 6)
    layers(0, 7)

    for k in range(6):
        rows = []
        for xo in range(6):
            sums = []
            for dy in range(3):
                at = [pl.ds(xo * 80 + (dz * 3 + dy) * 8, 8) for dz in range(3)]
                sums.append(parts[k, at[0], :] + parts[k + 1, at[1], :] + parts[k + 2, at[2], :])
            rows.append(sums[1] + pltpu.roll(sums[0], 1, 1) + pltpu.roll(sums[2], 127, 1))
        stress[pl.ds(k * 48, 48), :] = jnp.concatenate(rows, axis=0).astype(BF16)
    low = lax.broadcasted_iota(jnp.int32, (8, 128), 0) < 4
    forces = []
    for k in range(1, 5, 2):
        operands = []
        for m in (k, k + 1):
            wide = stress[pl.ds(m * 48, 48), :].astype(F32)
            operands.append(
                jnp.concatenate(
                    [
                        stress[pl.ds((m - 1) * 48, 144), :],
                        pltpu.roll(wide, 1, 1).astype(BF16),
                        pltpu.roll(wide, 127, 1).astype(BF16),
                    ],
                    axis=0,
                )
            )
        both = jnp.dot(
            div_ref[...], jnp.concatenate(operands, axis=1), preferred_element_type=F32
        )
        forces += [both[:, :128], both[:, 128:]]

    below, above = zip(*[net_rows(48 + x * 8) for x in range(0, 8, 2)])
    left, right = zip(*[wide_rows(64 + z * 8) for z in range(0, 8, 2)])

    def half_of(pair, i):
        return pair[i // 2][(i % 2) * 8 : (i % 2) * 8 + 8]

    def cell(z, x):
        if z < 0:
            return half_of(below, x)
        if z > 7:
            return half_of(above, x)
        if x < 0:
            return half_of(left, z)
        if x > 7:
            return half_of(right, z)
        return q_ref[z, x]

    for z in range(8):
        for x in range(8):
            here = q_ref[z, x]
            zp, zm, xp, xm = cell(z + 1, x), cell(z - 1, x), cell(z, x + 1), cell(z, x - 1)
            swap = pltpu.roll(here, 4, 0)
            back, ahead = pltpu.roll(swap, 1, 1), pltpu.roll(swap, 127, 1)
            far = jnp.where(low, back, ahead)
            slope_y = jnp.where(low, swap - back, ahead - swap)
            spread = (zp + zm) + (xp + xm) + (swap + far) - 6.0 * here

            def velocity(c):
                first = jnp.broadcast_to(q_ref[z, x, c : c + 1, :], (8, 128))
                second = jnp.broadcast_to(q_ref[z, x, c + 4 : c + 5, :], (8, 128))
                return jnp.where(low, first, second)

            advect = velocity(0) * (xp - xm) + velocity(1) * slope_y + velocity(2) * (zp - zm)
            force = forces[z // 2][(x // 2) * 8 : (x // 2) * 8 + 8]
            rate = viscosity * spread - 0.5 * advect + force
            new_ref[z, x] = update(z, x, here, rate)


def stage1_kernel(*refs):
    ins, outs, scratch = refs[:11], refs[11:16], refs[16:]
    stage_body(*ins, *scratch, lambda z, x, q, r: q + time_step * r, outs[0])
    emit_messages(ins[0], *outs)


def stage2_kernel(*refs):
    ins, base_ref, outs, scratch = refs[:11], refs[11], refs[12:17], refs[17:]

    def update(z, x, q, r):
        return 0.75 * base_ref[z, x] + 0.25 * (q + time_step * r)

    stage_body(*ins, *scratch, update, outs[0])
    emit_messages(ins[0], *outs)


def stage3_kernel(*refs):
    ins, base_ref, outs, scratch, new = refs[:11], refs[11], refs[12:14], refs[14:-1], refs[-1]
    core = ins[0][0]

    def update(z, x, q, r):
        return base_ref[z, x] * (1.0 / 3.0) + (2.0 / 3.0) * (q + time_step * r)

    stage_body(*ins, *scratch, update, new)
    outs[0][...] = new[:, pl.ds(core * 4, 4)].reshape(256, 128)
    outs[1][...] = new[:, pl.ds((1 - core) * 4, 4)].reshape(256, 128)


def finish_kernel(info_ref, own_ref, other_ref, parity_ref, out_ref, native, flat):
    core = info_ref[0]
    lane = lanes_of((256, 128))
    low = jnp.where(core == 0, own_ref[...], other_ref[...])
    high = jnp.where(core == 0, other_ref[...], own_ref[...])
    native[...] = jnp.where(
        lane < HALF, pltpu.roll(low, 128 - EDGE, 1), pltpu.roll(high, HALF - EDGE, 1)
    )
    halves = [
        jnp.concatenate([native[pl.ds(p * 4 + c, 32, stride=8), :] for c in range(4)], axis=0)
        for p in range(2)
    ]
    split = lax.dot_general(
        thirds(jnp.concatenate(halves, axis=1)),
        parity_ref[...],
        (((1,), (1,)), ((), ())),
        preferred_element_type=F32,
    )
    flat[...] = split[:128] + split[128:256] + split[256:]
    for c in range(4):
        for z in range(8):
            out_ref[c, z] = flat[pl.ds((c * 8 + z) * 4, 4), :]


def chip_swap(value, odd):
    size = lax.axis_size("wide")
    pairs = []
    for i in range(size):
        chip, core = divmod(i, 2)
        to = chip + 1 if (chip + odd) % 2 == 0 else chip - 1
        pairs.append((i, (2 * to + core) % size))
    return lax.ppermute(value, "wide", pairs)


def net_swap(value, odd):
    size = lax.axis_size("net")
    pairs = [(i, (i + 1 if (i + odd) % 2 == 0 else i - 1) % size) for i in range(size)]
    return lax.ppermute(value, "net", pairs)


def partner(value):
    return lax.ppermute(value, "wide", [(i, i ^ 1) for i in range(lax.axis_size("wide"))])


def edge_shift(value, cross):
    wide, narrow = lax.axis_size("wide"), lax.axis_size("narrow")
    pairs = []
    for w in range(wide):
        for r in range(narrow):
            if cross:
                step, to = (-1 if w % 2 == 0 else 1), w ^ 1
            else:
                step, to = (1 if w % 2 == 0 else -1), w
            pairs.append((w * narrow + r, to * narrow + (r + step) % narrow))
    return lax.ppermute(value, ("wide", "narrow"), pairs)


def per_device(fields, conv1_weight, conv1_bias, conv2_weight):
    wide, net = lax.axis_index("wide"), lax.axis_index("net")
    info = jnp.stack([wide % 2, (wide // 2) % 2, net % 2]).astype(jnp.int32)
    parity = near(jnp.asarray(split_parity(), BF16))
    native, same, cross = call(
        pack_kernel,
        [((256, 128), F32), ((32, 128), F32), ((32, 128), F32)],
        [pltpu.VMEM((128, 256), F32)],
        info, fields, parity,
    )
    other = near(partner(native))
    same = near(edge_shift(same, False))
    cross = near(edge_shift(cross, True))
    fixed = call(
        weights_kernel,
        [((256, 512), BF16), ((480, 256), BF16), ((32, 128), F32)],
        [pltpu.VMEM((32, 512), F32), pltpu.VMEM((80, 256), F32)],
        info, conv1_weight, conv2_weight, conv1_bias.reshape(1, 32),
    )
    fixed = (*map(near, fixed), near(jnp.asarray(divergence_matrix(), BF16)))
    base, *messages = call(
        assemble_kernel,
        [((8, 8, 8, 128), F32)] + MESSAGES,
        [],
        info, near(native), other, same, cross,
    )
    base = near(base)
    scratch = [
        pltpu.VMEM((1440, 128), BF16),
        pltpu.VMEM((8, 480, 128), F32),
        pltpu.VMEM((288, 128), BF16),
    ]
    even = net % 2 == 0

    def exchange(wide_a, wide_b, net_a, net_b):
        got_a, got_b = chip_swap(wide_a, 0), chip_swap(wide_b, 1)
        rows_a = [jnp.where(even, got[16:64], got[:48]) for got in (got_a, got_b)]
        rows_b = [jnp.where(even, got[:48], got[16:64]) for got in (got_a, got_b)]
        far_a = net_swap(jnp.concatenate([net_a, *rows_a], axis=0), 0)
        far_b = net_swap(jnp.concatenate([net_b, *rows_b], axis=0), 1)
        return map(near, (wide_a, got_a, got_b, far_a, far_b))

    state_out = [((8, 8, 8, 128), F32)] + MESSAGES
    one, *messages = call(
        stage1_kernel, state_out, scratch, info, base, *exchange(*messages), *fixed
    )
    two, *messages = call(
        stage2_kernel, state_out, scratch, info, near(one), *exchange(*messages), *fixed, base
    )
    own, away = call(
        stage3_kernel,
        [((256, 128), F32)] * 2,
        scratch + [pltpu.VMEM((8, 8, 8, 128), F32)],
        info, near(two), *exchange(*messages), *fixed, base,
    )
    return call(
        finish_kernel,
        None,
        [pltpu.VMEM((256, 128), F32), pltpu.VMEM((128, 256), F32)],
        info, near(own), near(partner(away)), parity,
        result=jax.ShapeDtypeStruct(fields.shape, F32),
    )


def solution(mesh):
    in_specs = (P(None, "net", "wide", "narrow"), P(), P(), P())
    out_specs = P(None, "net", "wide", "narrow")
    return jax.shard_map(
        per_device, mesh=mesh, in_specs=in_specs, out_specs=out_specs, check_vma=False
    )
```

time: 93 us -> 75.7 us (0.81)
  the two profiles are of different devices: /device:TPU:31 before, /device:TPU:1 now
where the time goes in v1:
time: 75.7 us; the launch traced here: 75.5 us
  starting transfers between devices  38.5 us (51%)
  waiting for transfers between devices  19.7 us (26%)
  Pallas kernels  14 us (18%)
  local copies, waits for them, and re-layouts  2.48 us (3%)
    ppermute x6, starting transfers between devices, net_swap(): return lax.ppermute(value, 'net', pairs)  19.2 us
    pallas_call x7, Pallas kernels, call(): pl.pallas_call(kernel, out_shape=result or [pltpu.VMEM(s, d) for s, d in...  14 us
    ppermute x2, starting transfers between devices, partner(): lax.ppermute(value, 'wide', [(i, i ^ 1) for i in range(lax.axis_size('wid...  11 us
    ppermute x6, waiting for transfers between devices, chip_swap(): return lax.ppermute(value, 'wide', pairs)  8.69 us
    ppermute x6, waiting for transfers between devices, net_swap(): return lax.ppermute(value, 'net', pairs)  6.84 us
    ppermute x6, starting transfers between devices, chip_swap(): return lax.ppermute(value, 'wide', pairs)  5.68 us
    ppermute x2, waiting for transfers between devices, edge_shift(): return lax.ppermute(value, ('wide', 'narrow'), pairs)  3.16 us
    ppermute x2, starting transfers between devices, edge_shift(): return lax.ppermute(value, ('wide', 'narrow'), pairs)  2.64 us
  transfers between devices with their start and end apart: 16, of which 12 were waited for; matrix products, arithmetic and copies ran while one was open for 2% of the time, Pallas kernels for 2%

profile of v1, /device:TPU:1, one launch (start us, length us, event | category | flops | bytes accessed | tf_op | source)
XLA Modules:
  0.0 75.5 jit_solution(6745762847178720165)
XLA Ops:
  0.0 0.6 pad_add_fusion.info_ref.refs_0_
  0.6 0.0 copy-start
  0.6 0.9 %copy-done = bf16[256,256]{1,0:T(8,128)(2,1)S(1)} copy-done((bf16[256,256]{1,0:T(8,128)(2,1)S(1)}, bf16[256,256]{1,0:T(8,128)(2,1)}, u32[]{:S(2)}) %copy-start) | copy-done | bytes 131096
  1.5 1.3 %shard_map.64 = (f32[256,128]{1,0:T(8,128)S(1)}, f32[32,128]{1,0:T(8,128)S(1)}, f32[32,128]{1,0:T(8,128)S(1)}) custom-call(s32[3]{0:T(128)} %pad_add_fusion.info_ref.refs_0_, f32[4,8,4,256]{3,2,1,0:T(4,128)} %fields_ref.1, bf16[256,256]{1,0:T(8,128)(2,1)S(1)} %copy-done), custom_call_target="tpu_custom_call" | custom-call | tf_op jit(solution)/shard_map/pallas_call | solution.py:46
  2.7 3.3 %collective-permute-start = (f32[256,128]{1,0:T(8,128)S(1)}, f32[256,128]{1,0:T(8,128)S(1)}, u32[]{:S(2)}, u32[]{:S(2)}) collective-permute-start(f32[256,128]{1,0:T(8,128)S(1)} %get-tuple-element.28.own_ref), channel_id=1, source_target_pairs={{0,32},{32,0},{64,96},{96,64},{128,160},{160,128},{192,224},{224,1... | collective-permute-start | bytes 393224 | tf_op jit(solution)/shard_map/ppermute | solution.py:353
  6.0 2.6 %collective-permute-start.1 = (f32[32,128]{1,0:T(8,128)S(1)}, f32[32,128]{1,0:T(8,128)S(1)}, u32[]{:S(2)}, u32[]{:S(2)}) collective-permute-start(f32[32,128]{1,0:T(8,128)S(1)} %get-tuple-element.29), channel_id=1, source_target_pairs={{0,8},{8,16},{16,24},{24,0},{32,56},{40,32},{48,40},{56,48},{64,72... | collective-permute-start | bytes 49160 | tf_op jit(solution)/shard_map/ppermute | solution.py:366
  8.7 0.0 collective-permute-start.2
  8.7 0.9 %collective-permute-done.1.same_ref = f32[32,128]{1,0:T(8,128)S(1)} collective-permute-done((f32[32,128]{1,0:T(8,128)S(1)}, f32[32,128]{1,0:T(8,128)S(1)}, u32[]{:S(2)}, u32[]{:S(2)}) %collective-permute-start.1) | collective-permute-done | bytes 16416 | tf_op jit(solution)/shard_map/ppermute | solution.py:366
  9.5 2.3 %collective-permute-done.2.cross_ref = f32[32,128]{1,0:T(8,128)S(1)} collective-permute-done((f32[32,128]{1,0:T(8,128)S(1)}, f32[32,128]{1,0:T(8,128)S(1)}, u32[]{:S(2)}, u32[]{:S(2)}) %collective-permute-start.2) | collective-permute-done | bytes 16416 | tf_op jit(solution)/shard_map/ppermute | solution.py:366
  11.8 0.0 collective-permute-done.other_ref
  11.8 0.9 %shard_map.65 = (f32[8,8,8,128]{3,2,1,0:T(8,128)S(1)}, bf16[128,128]{1,0:T(8,128)(2,1)S(1)}, bf16[128,128]{1,0:T(8,128)(2,1)S(1)}, bf16[112,128]{1,0:T(8,128)(2,1)S(1)}, bf16[112,128]{1,0:T(8,128)(2,1)S(1)}) custom-call(s32[3]{0:T(128)} %pad_add_fusion.info_ref.refs_0_, f32[256,128]{1,0:T(8,128)S(1)} %get-tuple-element.28.own_ref, ...), custom_call_target="tpu_custom_call" | custom-call | tf_op jit(solution)/shard_map/pallas_call | solution.py:46
  12.7 2.8 %collective-permute-start.4 = (bf16[128,128]{1,0:T(8,128)(2,1)S(1)}, bf16[128,128]{1,0:T(8,128)(2,1)S(1)}, u32[]{:S(2)}, u32[]{:S(2)}) collective-permute-start(bf16[128,128]{1,0:T(8,128)(2,1)S(1)} %get-tuple-element.33), channel_id=1, source_target_pairs={{0,192},{32,224},{64,128},{96,160},{128,64},{160,96},{192,0},{224,... | collective-permute-start | bytes 98312 | tf_op jit(solution)/shard_map/ppermute | solution.py:343
  15.5 0.0 collective-permute-start.3
  15.6 1.7 %collective-permute-done.4.refs_4_ = bf16[128,128]{1,0:T(8,128)(2,1)S(1)} collective-permute-done((bf16[128,128]{1,0:T(8,128)(2,1)S(1)}, bf16[128,128]{1,0:T(8,128)(2,1)S(1)}, u32[]{:S(2)}, u32[]{:S(2)}) %collective-permute-start.4) | collective-permute-done | bytes 32800 | tf_op jit(solution)/shard_map/ppermute | solution.py:343
  17.3 1.5 %collective-permute-done.3.refs_3_ = bf16[128,128]{1,0:T(8,128)(2,1)S(1)} collective-permute-done((bf16[128,128]{1,0:T(8,128)(2,1)S(1)}, bf16[128,128]{1,0:T(8,128)(2,1)S(1)}, u32[]{:S(2)}, u32[]{:S(2)}) %collective-permute-start.3) | collective-permute-done | bytes 32800 | tf_op jit(solution)/shard_map/ppermute | solution.py:343
  18.8 1.3 %collective-permute-start.5 = (bf16[208,128]{1,0:T(8,128)(2,1)S(1)}, bf16[208,128]{1,0:T(8,128)(2,1)S(1)}, u32[]{:S(2)}, u32[]{:S(2)}) collective-permute-start(bf16[208,128]{1,0:T(8,128)(2,1)S(1)} %pad_maximum_fusion), channel_id=1, source_target_pairs={{0,1},{1,0},{2,3},{3,2},{4,5},{5,4},{6,7},{7,6},{8,9},{9,8},{10,11... | collective-permute-start | bytes 159752 | tf_op jit(solution)/shard_map/ppermute | solution.py:349
  20.1 0.0 copy-start.3
  20.1 0.0 copy-start.4
  20.1 5.9 %collective-permute-start.6 = (bf16[208,128]{1,0:T(8,128)(2,1)S(1)}, bf16[208,128]{1,0:T(8,128)(2,1)S(1)}, u32[]{:S(2)}, u32[]{:S(2)}) collective-permute-start(bf16[208,128]{1,0:T(8,128)(2,1)S(1)} %pad_maximum_fusion.1), channel_id=1, source_target_pairs={{0,7},{1,2},{2,1},{3,4},{4,3},{5,6},{6,5},{7,0},{8,15},{9,10},{10,... | collective-permute-start | bytes 159752 | tf_op jit(solution)/shard_map/ppermute | solution.py:349
  26.0 0.0 copy-done.3
  26.0 0.6 copy.8.w2_ref
  26.6 0.0 copy-done.4
  26.6 0.9 %copy.7.w1_ref = bf16[27,32,4]{2,1,0:T(8,128)(2,1)} copy(bf16[27,32,4]{1,2,0:T(4,128)(2,1)S(1)} %copy-done.4) | data formatting | bytes 13824 | tf_op args[1]
  27.5 0.0 copy-start.2
  27.5 1.3 %shard_map.66 = (bf16[256,512]{1,0:T(8,128)(2,1)S(1)}, bf16[480,256]{1,0:T(8,128)(2,1)S(1)}, f32[32,128]{1,0:T(8,128)S(1)}) custom-call(s32[3]{0:T(128)} %pad_add_fusion.info_ref.refs_0_, bf16[27,32,4]{2,1,0:T(8,128)(2,1)} %copy.7.w1_ref, bf16[27,6,32]{2,1,0:T(8,128)(2,1)} %copy.8.w2_ref, f32[1,32]{1,0:T(1,128)} %bitcast.4), custom_call_target="tpu_custom_call" | custom-call | tf_op jit(solution)/shard_map/pallas_call | solution.py:46
  28.9 0.0 collective-permute-done.5.refs_5_
  28.9 0.3 collective-permute-done.6.refs_6_
  29.2 0.0 copy-done.2
  29.2 2.9 %shard_map.67 = (f32[8,8,8,128]{3,2,1,0:T(8,128)S(1)}, bf16[128,128]{1,0:T(8,128)(2,1)S(1)}, bf16[128,128]{1,0:T(8,128)(2,1)S(1)}, bf16[112,128]{1,0:T(8,128)(2,1)S(1)}, bf16[112,128]{1,0:T(8,128)(2,1)S(1)}) custom-call(s32[3]{0:T(128)} %pad_add_fusion.info_ref.refs_0_, f32[8,8,8,128]{3,2,1,0:T(8,128)S(1)} %get-tuple-element.31.refs_1_.refs_11_, ...), custom_call_target="tpu_custom_call" | custom-call | tf_op jit(solution)/shard_map/pallas_call | solution.py:46
  32.1 1.5 %collective-permute-start.8 = (bf16[128,128]{1,0:T(8,128)(2,1)S(1)}, bf16[128,128]{1,0:T(8,128)(2,1)S(1)}, u32[]{:S(2)}, u32[]{:S(2)}) collective-permute-start(bf16[128,128]{1,0:T(8,128)(2,1)S(1)} %get-tuple-element.41), channel_id=1, source_target_pairs={{0,192},{32,224},{64,128},{96,160},{128,64},{160,96},{192,0},{224,... | collective-permute-start | bytes 98312 | tf_op jit(solution)/shard_map/ppermute | solution.py:343
  33.6 0.0 collective-permute-start.7
  33.6 2.6 %collective-permute-done.8.refs_4_ = bf16[128,128]{1,0:T(8,128)(2,1)S(1)} collective-permute-done((bf16[128,128]{1,0:T(8,128)(2,1)S(1)}, bf16[128,128]{1,0:T(8,128)(2,1)S(1)}, u32[]{:S(2)}, u32[]{:S(2)}) %collective-permute-start.8) | collective-permute-done | bytes 32800 | tf_op jit(solution)/shard_map/ppermute | solution.py:343
  36.2 0.2 collective-permute-done.7.refs_3_
  36.4 0.1 collective-permute-start.9
  36.5 5.7 %collective-permute-start.10 = (bf16[208,128]{1,0:T(8,128)(2,1)S(1)}, bf16[208,128]{1,0:T(8,128)(2,1)S(1)}, u32[]{:S(2)}, u32[]{:S(2)}) collective-permute-start(bf16[208,128]{1,0:T(8,128)(2,1)S(1)} %pad_maximum_fusion.3), channel_id=1, source_target_pairs={{0,7},{1,2},{2,1},{3,4},{4,3},{5,6},{6,5},{7,0},{8,15},{9,10},{10,... | collective-permute-start | bytes 159752 | tf_op jit(solution)/shard_map/ppermute | solution.py:349
  42.2 0.0 collective-permute-done.9.refs_5_
  42.2 3.3 %collective-permute-done.10.refs_6_ = bf16[208,128]{1,0:T(8,128)(2,1)S(1)} collective-permute-done((bf16[208,128]{1,0:T(8,128)(2,1)S(1)}, bf16[208,128]{1,0:T(8,128)(2,1)S(1)}, u32[]{:S(2)}, u32[]{:S(2)}) %collective-permute-start.10) | collective-permute-done | bytes 53280 | tf_op jit(solution)/shard_map/ppermute | solution.py:349
  45.6 2.9 %shard_map.68 = (f32[8,8,8,128]{3,2,1,0:T(8,128)S(1)}, bf16[128,128]{1,0:T(8,128)(2,1)S(1)}, bf16[128,128]{1,0:T(8,128)(2,1)S(1)}, bf16[112,128]{1,0:T(8,128)(2,1)S(1)}, bf16[112,128]{1,0:T(8,128)(2,1)S(1)}) custom-call(s32[3]{0:T(128)} %pad_add_fusion.info_ref.refs_0_, f32[8,8,8,128]{3,2,1,0:T(8,128)S(1)} %get-tuple-element.39.refs_1_, ...), custom_call_target="tpu_custom_call" | custom-call | tf_op jit(solution)/shard_map/pallas_call | solution.py:46
  48.5 1.4 %collective-permute-start.12 = (bf16[128,128]{1,0:T(8,128)(2,1)S(1)}, bf16[128,128]{1,0:T(8,128)(2,1)S(1)}, u32[]{:S(2)}, u32[]{:S(2)}) collective-permute-start(bf16[128,128]{1,0:T(8,128)(2,1)S(1)} %get-tuple-element.46), channel_id=1, source_target_pairs={{0,192},{32,224},{64,128},{96,160},{128,64},{160,96},{192,0},{224,... | collective-permute-start | bytes 98312 | tf_op jit(solution)/shard_map/ppermute | solution.py:343
  49.9 0.0 collective-permute-start.11
  49.9 2.7 %collective-permute-done.12.refs_4_ = bf16[128,128]{1,0:T(8,128)(2,1)S(1)} collective-permute-done((bf16[128,128]{1,0:T(8,128)(2,1)S(1)}, bf16[128,128]{1,0:T(8,128)(2,1)S(1)}, u32[]{:S(2)}, u32[]{:S(2)}) %collective-permute-start.12) | collective-permute-done | bytes 32800 | tf_op jit(solution)/shard_map/ppermute | solution.py:343
  52.6 0.1 collective-permute-done.11.refs_3_
  52.7 0.3 collective-permute-start.13
  52.9 5.9 %collective-permute-start.14 = (bf16[208,128]{1,0:T(8,128)(2,1)S(1)}, bf16[208,128]{1,0:T(8,128)(2,1)S(1)}, u32[]{:S(2)}, u32[]{:S(2)}) collective-permute-start(bf16[208,128]{1,0:T(8,128)(2,1)S(1)} %pad_maximum_fusion.5), channel_id=1, source_target_pairs={{0,7},{1,2},{2,1},{3,4},{4,3},{5,6},{6,5},{7,0},{8,15},{9,10},{10,... | collective-permute-start | bytes 159752 | tf_op jit(solution)/shard_map/ppermute | solution.py:349
  58.8 0.0 collective-permute-done.13.refs_5_
  58.8 3.2 %collective-permute-done.14.refs_6_ = bf16[208,128]{1,0:T(8,128)(2,1)S(1)} collective-permute-done((bf16[208,128]{1,0:T(8,128)(2,1)S(1)}, bf16[208,128]{1,0:T(8,128)(2,1)S(1)}, u32[]{:S(2)}, u32[]{:S(2)}) %collective-permute-start.14) | collective-permute-done | bytes 53280 | tf_op jit(solution)/shard_map/ppermute | solution.py:349
  62.0 0.0 copy-start.1
  62.0 3.0 %shard_map.69 = (f32[256,128]{1,0:T(8,128)S(1)}, f32[256,128]{1,0:T(8,128)S(1)}) custom-call(s32[3]{0:T(128)} %pad_add_fusion.info_ref.refs_0_, f32[8,8,8,128]{3,2,1,0:T(8,128)S(1)} %get-tuple-element.44.refs_1_, bf16[128,128]{1,0:T(8,128)(2,1)S(1)} %get-tuple-element.45.refs_2_, bf16[128,128]{1,0:T(8,128)(2,1)S(1)} %collective-permute-done.11.refs_3_, ...), custom_call_target="tpu_custom_call" | custom-call | tf_op jit(solution)/shard_map/pallas_call | solution.py:46
  65.1 7.7 %collective-permute-start.15 = (f32[256,128]{1,0:T(8,128)S(1)}, f32[256,128]{1,0:T(8,128)S(1)}, u32[]{:S(2)}, u32[]{:S(2)}) collective-permute-start(f32[256,128]{1,0:T(8,128)S(1)} %get-tuple-element.50), channel_id=1, source_target_pairs={{0,32},{32,0},{64,96},{96,64},{128,160},{160,128},{192,224},{224,1... | collective-permute-start | bytes 393224 | tf_op jit(solution)/shard_map/ppermute | solution.py:353
  72.8 1.0 %collective-permute-done.15.other_ref = f32[256,128]{1,0:T(8,128)S(1)} collective-permute-done((f32[256,128]{1,0:T(8,128)S(1)}, f32[256,128]{1,0:T(8,128)S(1)}, u32[]{:S(2)}, u32[]{:S(2)}) %collective-permute-start.15) | collective-permute-done | bytes 131104 | tf_op jit(solution)/shard_map/ppermute | solution.py:353
  73.8 0.0 copy-done.1
  73.8 1.7 %shard_map.70 = f32[4,8,4,256]{3,2,1,0:T(4,128)} custom-call(s32[3]{0:T(128)} %pad_add_fusion.info_ref.refs_0_, f32[256,128]{1,0:T(8,128)S(1)} %get-tuple-element.49.own_ref, f32[256,128]{1,0:T(8,128)S(1)} %collective-permute-done.15.other_ref, bf16[256,256]{1,0:T(8,128)(2,1)S(1)} %copy-done.1), custom_call_target="tpu_custom_call" | custom-call | tf_op jit(solution)/shard_map/pallas_call | solution.py:46
  (12 shorter events, 0.1 us)
Async XLA Ops:
  0.6 0.9 %copy-start = (bf16[256,256]{1,0:T(8,128)(2,1)S(1)}, bf16[256,256]{1,0:T(8,128)(2,1)}, u32[]{:S(2)}) copy-start(bf16[256,256]{1,0:T(8,128)(2,1)} %constant.47.clone.parity_ref) | copy-start | bytes 393220
  2.7 9.1 %collective-permute-start = (f32[256,128]{1,0:T(8,128)S(1)}, f32[256,128]{1,0:T(8,128)S(1)}, u32[]{:S(2)}, u32[]{:S(2)}) collective-permute-start(f32[256,128]{1,0:T(8,128)S(1)} %get-tuple-element.28.own_ref), channel_id=1, source_target_pairs={{0,32},{32,0},{64,96},{96,64},{128,160},{160,128},{192,224},{224,1... | collective-permute-start | bytes 393224 | tf_op jit(solution)/shard_map/ppermute | solution.py:353
  6.0 3.5 %collective-permute-start.1 = (f32[32,128]{1,0:T(8,128)S(1)}, f32[32,128]{1,0:T(8,128)S(1)}, u32[]{:S(2)}, u32[]{:S(2)}) collective-permute-start(f32[32,128]{1,0:T(8,128)S(1)} %get-tuple-element.29), channel_id=1, source_target_pairs={{0,8},{8,16},{16,24},{24,0},{32,56},{40,32},{48,40},{56,48},{64,72... | collective-permute-start | bytes 49160 | tf_op jit(solution)/shard_map/ppermute | solution.py:366
  8.7 3.2 %collective-permute-start.2 = (f32[32,128]{1,0:T(8,128)S(1)}, f32[32,128]{1,0:T(8,128)S(1)}, u32[]{:S(2)}, u32[]{:S(2)}) collective-permute-start(f32[32,128]{1,0:T(8,128)S(1)} %get-tuple-element.30), channel_id=1, source_target_pairs={{0,56},{8,32},{16,40},{24,48},{32,8},{40,16},{48,24},{56,0},{64,12... | collective-permute-start | bytes 49160 | tf_op jit(solution)/shard_map/ppermute | solution.py:366
  12.7 4.5 %collective-permute-start.4 = (bf16[128,128]{1,0:T(8,128)(2,1)S(1)}, bf16[128,128]{1,0:T(8,128)(2,1)S(1)}, u32[]{:S(2)}, u32[]{:S(2)}) collective-permute-start(bf16[128,128]{1,0:T(8,128)(2,1)S(1)} %get-tuple-element.33), channel_id=1, source_target_pairs={{0,192},{32,224},{64,128},{96,160},{128,64},{160,96},{192,0},{224,... | collective-permute-start | bytes 98312 | tf_op jit(solution)/shard_map/ppermute | solution.py:343
  15.5 3.2 %collective-permute-start.3 = (bf16[128,128]{1,0:T(8,128)(2,1)S(1)}, bf16[128,128]{1,0:T(8,128)(2,1)S(1)}, u32[]{:S(2)}, u32[]{:S(2)}) collective-permute-start(bf16[128,128]{1,0:T(8,128)(2,1)S(1)} %get-tuple-element.32.refs_2_), channel_id=1, source_target_pairs={{0,64},{32,96},{64,0},{96,32},{128,192},{160,224},{192,128},{224,1... | collective-permute-start | bytes 98312 | tf_op jit(solution)/shard_map/ppermute | solution.py:343
  18.8 10.1 %collective-permute-start.5 = (bf16[208,128]{1,0:T(8,128)(2,1)S(1)}, bf16[208,128]{1,0:T(8,128)(2,1)S(1)}, u32[]{:S(2)}, u32[]{:S(2)}) collective-permute-start(bf16[208,128]{1,0:T(8,128)(2,1)S(1)} %pad_maximum_fusion), channel_id=1, source_target_pairs={{0,1},{1,0},{2,3},{3,2},{4,5},{5,4},{6,7},{7,6},{8,9},{9,8},{10,11... | collective-permute-start | bytes 159752 | tf_op jit(solution)/shard_map/ppermute | solution.py:349
  20.1 5.9 %copy-start.3 = (bf16[27,6,32]{2,0,1:T(8,128)(2,1)S(1)}, bf16[27,6,32]{2,0,1:T(8,128)(2,1)}, u32[]{:S(2)}) copy-start(bf16[27,6,32]{2,0,1:T(8,128)(2,1)} %param.9) | copy-start | bytes 31108
  20.1 6.5 %copy-start.4 = (bf16[27,32,4]{1,2,0:T(4,128)(2,1)S(1)}, bf16[27,32,4]{1,2,0:T(4,128)(2,1)}, u32[]{:S(2)}) copy-start(bf16[27,32,4]{1,2,0:T(4,128)(2,1)} %param.7) | copy-start | bytes 20740
  20.1 9.1 %collective-permute-start.6 = (bf16[208,128]{1,0:T(8,128)(2,1)S(1)}, bf16[208,128]{1,0:T(8,128)(2,1)S(1)}, u32[]{:S(2)}, u32[]{:S(2)}) collective-permute-start(bf16[208,128]{1,0:T(8,128)(2,1)S(1)} %pad_maximum_fusion.1), channel_id=1, source_target_pairs={{0,7},{1,2},{2,1},{3,4},{4,3},{5,6},{6,5},{7,0},{8,15},{9,10},{10,... | collective-permute-start | bytes 159752 | tf_op jit(solution)/shard_map/ppermute | solution.py:349
  27.5 1.7 %copy-start.2 = (bf16[32,240]{1,0:T(8,128)(2,1)S(1)}, bf16[32,240]{1,0:T(8,128)(2,1)}, u32[]{:S(2)}) copy-start(bf16[32,240]{1,0:T(8,128)(2,1)} %constant.48.clone.refs_10_) | copy-start | bytes 46084
  32.1 4.1 %collective-permute-start.8 = (bf16[128,128]{1,0:T(8,128)(2,1)S(1)}, bf16[128,128]{1,0:T(8,128)(2,1)S(1)}, u32[]{:S(2)}, u32[]{:S(2)}) collective-permute-start(bf16[128,128]{1,0:T(8,128)(2,1)S(1)} %get-tuple-element.41), channel_id=1, source_target_pairs={{0,192},{32,224},{64,128},{96,160},{128,64},{160,96},{192,0},{224,... | collective-permute-start | bytes 98312 | tf_op jit(solution)/shard_map/ppermute | solution.py:343
  33.6 2.8 %collective-permute-start.7 = (bf16[128,128]{1,0:T(8,128)(2,1)S(1)}, bf16[128,128]{1,0:T(8,128)(2,1)S(1)}, u32[]{:S(2)}, u32[]{:S(2)}) collective-permute-start(bf16[128,128]{1,0:T(8,128)(2,1)S(1)} %get-tuple-element.40.refs_2_), channel_id=1, source_target_pairs={{0,64},{32,96},{64,0},{96,32},{128,192},{160,224},{192,128},{224,1... | collective-permute-start | bytes 98312 | tf_op jit(solution)/shard_map/ppermute | solution.py:343
  36.4 5.9 %collective-permute-start.9 = (bf16[208,128]{1,0:T(8,128)(2,1)S(1)}, bf16[208,128]{1,0:T(8,128)(2,1)S(1)}, u32[]{:S(2)}, u32[]{:S(2)}) collective-permute-start(bf16[208,128]{1,0:T(8,128)(2,1)S(1)} %pad_maximum_fusion.2), channel_id=1, source_target_pairs={{0,1},{1,0},{2,3},{3,2},{4,5},{5,4},{6,7},{7,6},{8,9},{9,8},{10,11... | collective-permute-start | bytes 159752 | tf_op jit(solution)/shard_map/ppermute | solution.py:349
  36.5 9.1 %collective-permute-start.10 = (bf16[208,128]{1,0:T(8,128)(2,1)S(1)}, bf16[208,128]{1,0:T(8,128)(2,1)S(1)}, u32[]{:S(2)}, u32[]{:S(2)}) collective-permute-start(bf16[208,128]{1,0:T(8,128)(2,1)S(1)} %pad_maximum_fusion.3), channel_id=1, source_target_pairs={{0,7},{1,2},{2,1},{3,4},{4,3},{5,6},{6,5},{7,0},{8,15},{9,10},{10,... | collective-permute-start | bytes 159752 | tf_op jit(solution)/shard_map/ppermute | solution.py:349
  48.5 4.1 %collective-permute-start.12 = (bf16[128,128]{1,0:T(8,128)(2,1)S(1)}, bf16[128,128]{1,0:T(8,128)(2,1)S(1)}, u32[]{:S(2)}, u32[]{:S(2)}) collective-permute-start(bf16[128,128]{1,0:T(8,128)(2,1)S(1)} %get-tuple-element.46), channel_id=1, source_target_pairs={{0,192},{32,224},{64,128},{96,160},{128,64},{160,96},{192,0},{224,... | collective-permute-start | bytes 98312 | tf_op jit(solution)/shard_map/ppermute | solution.py:343
  49.9 2.8 %collective-permute-start.11 = (bf16[128,128]{1,0:T(8,128)(2,1)S(1)}, bf16[128,128]{1,0:T(8,128)(2,1)S(1)}, u32[]{:S(2)}, u32[]{:S(2)}) collective-permute-start(bf16[128,128]{1,0:T(8,128)(2,1)S(1)} %get-tuple-element.45.refs_2_), channel_id=1, source_target_pairs={{0,64},{32,96},{64,0},{96,32},{128,192},{160,224},{192,128},{224,1... | collective-permute-start | bytes 98312 | tf_op jit(solution)/shard_map/ppermute | solution.py:343
  52.7 6.2 %collective-permute-start.13 = (bf16[208,128]{1,0:T(8,128)(2,1)S(1)}, bf16[208,128]{1,0:T(8,128)(2,1)S(1)}, u32[]{:S(2)}, u32[]{:S(2)}) collective-permute-start(bf16[208,128]{1,0:T(8,128)(2,1)S(1)} %pad_maximum_fusion.4), channel_id=1, source_target_pairs={{0,1},{1,0},{2,3},{3,2},{4,5},{5,4},{6,7},{7,6},{8,9},{9,8},{10,11... | collective-permute-start | bytes 159752 | tf_op jit(solution)/shard_map/ppermute | solution.py:349
  52.9 9.1 %collective-permute-start.14 = (bf16[208,128]{1,0:T(8,128)(2,1)S(1)}, bf16[208,128]{1,0:T(8,128)(2,1)S(1)}, u32[]{:S(2)}, u32[]{:S(2)}) collective-permute-start(bf16[208,128]{1,0:T(8,128)(2,1)S(1)} %pad_maximum_fusion.5), channel_id=1, source_target_pairs={{0,7},{1,2},{2,1},{3,4},{4,3},{5,6},{6,5},{7,0},{8,15},{9,10},{10,... | collective-permute-start | bytes 159752 | tf_op jit(solution)/shard_map/ppermute | solution.py:349
  62.0 11.8 %copy-start.1 = (bf16[256,256]{1,0:T(8,128)(2,1)S(1)}, bf16[256,256]{1,0:T(8,128)(2,1)}, u32[]{:S(2)}) copy-start(bf16[256,256]{1,0:T(8,128)(2,1)} %constant.47.clone.parity_ref) | copy-start | bytes 393220
  65.1 8.7 %collective-permute-start.15 = (f32[256,128]{1,0:T(8,128)S(1)}, f32[256,128]{1,0:T(8,128)S(1)}, u32[]{:S(2)}, u32[]{:S(2)}) collective-permute-start(f32[256,128]{1,0:T(8,128)S(1)} %get-tuple-element.50), channel_id=1, source_target_pairs={{0,32},{32,0},{64,96},{96,64},{128,160},{160,128},{192,224},{224,1... | collective-permute-start | bytes 393224 | tf_op jit(solution)/shard_map/ppermute | solution.py:353

commit v2 on v1

--- a/solution.py
+++ b/solution.py
@@ -1,3 +1,5 @@
+import functools
+
 import jax
 import jax.numpy as jnp
 import numpy as np
@@ -10,18 +12,11 @@
 viscosity = 0.05
 EDGE = 9
 HALF = 64
+VMEM_LIMIT = 16 << 20
 F32 = jnp.float32
 BF16 = jnp.bfloat16
 VM = pl.BlockSpec(memory_space=pltpu.VMEM)
 SM = pl.BlockSpec(memory_space=pltpu.SMEM)
-
-
-def split_parity():
-    m = np.zeros((256, 256), np.float32)
-    for l in range(128):
-        m[2 * l, l] = 1.0
-        m[2 * l + 1, 128 + l] = 1.0
-    return m
 
 
 def divergence_matrix():
@@ -49,6 +44,7 @@
         in_specs=[SM] + [VM] * len(args),
         out_specs=VM if result else [VM] * len(outs),
         scratch_shapes=scratch,
+        compiler_params=pltpu.CompilerParams(vmem_limit_bytes=VMEM_LIMIT),
     )(info, *args)
 
 
@@ -64,8 +60,11 @@
     return jnp.concatenate([first, second, third], axis=0)
 
 
-def pack_kernel(info_ref, fields_ref, parity_ref, native_ref, same_ref, cross_ref, flat):
+def pack_kernel(info_ref, fields_ref, native_ref, same_ref, cross_ref, parity_ref, flat):
     core = info_ref[0]
+    row, col = lax.broadcasted_iota(jnp.int32, (256, 256), 0), lanes_of((256, 256))
+    source = jnp.where(col < 128, 2 * col, 2 * col - 255)
+    parity_ref[...] = jnp.where(row == source, 1.0, 0.0).astype(F32).astype(BF16)
     for c in range(4):
         for z in range(8):
             flat[pl.ds((c * 8 + z) * 4, 4), :] = fields_ref[c, z]
@@ -123,7 +122,8 @@
 
 
 def assemble_kernel(
-    info_ref, own_ref, other_ref, same_ref, cross_ref, q_ref, wide_a_ref, wide_b_ref, net_a_ref, net_b_ref
+    info_ref, own_ref, other_ref, same_ref, cross_ref, ready_ref,
+    q_ref, wide_a_ref, wide_b_ref, net_a_ref, net_b_ref,
 ):
     core = info_ref[0]
     lane = lanes_of((32, 128))
@@ -140,7 +140,7 @@
     emit_messages(info_ref, q_ref, wide_a_ref, wide_b_ref, net_a_ref, net_b_ref)
 
 
-def weights_kernel(info_ref, w1_ref, w2_ref, b_ref, band1_ref, band2_ref, bias_ref, flat1, flat2):
+def weights_kernel(info_ref, w1_ref, w2_ref, b_ref, band1_ref, band2_ref, bias_ref, flat1, flat2, tall):
     flat1[...] = jnp.zeros_like(flat1)
     flat2[...] = jnp.zeros_like(flat2)
     for dz in range(3):
@@ -152,77 +152,128 @@
     for xo in range(8):
         band1_ref[pl.ds(xo * 32, 32), :] = pltpu.roll(flat1[...], 4 * xo, 1).astype(BF16)
     for xo in range(6):
-        band2_ref[pl.ds(xo * 80, 80), :] = pltpu.roll(flat2[...], 32 * xo, 1).astype(BF16)
+        tall[pl.ds(xo * 72, 72), :] = pltpu.roll(flat2[...], 32 * xo, 1)
+    band2_ref[...] = tall[...].astype(BF16)
     square = jnp.broadcast_to(b_ref[...], (32, 32))
     diagonal = lanes_of((32, 32)) == lax.broadcasted_iota(jnp.int32, (32, 32), 0)
     column = jnp.sum(jnp.where(diagonal, square, 0.0), axis=1, keepdims=True)
     bias_ref[...] = jnp.broadcast_to(column, (32, 128))
 
 
-def stage_body(
-    info_ref, q_ref, coarse_ref, wide_a_ref, wide_b_ref, net_a_ref, net_b_ref,
-    band1_ref, band2_ref, bias_ref, div_ref, columns, parts, stress, update, new_ref,
-):
-    chip_even = info_ref[1] == 0
-    net_even = info_ref[2] == 0
-    left_at, right_at = jnp.where(chip_even, 160, 112), jnp.where(chip_even, 112, 160)
-
-    def slab(j, pieces):
-        for i, piece in enumerate(pieces):
-            wide = piece.astype(F32)
-            columns[pl.ds(j * 144 + i * 16, 16), :] = pltpu.roll(wide, 1, 1).astype(BF16)
-            columns[pl.ds(j * 144 + 48 + i * 16, 16), :] = wide.astype(BF16)
-            columns[pl.ds(j * 144 + 96 + i * 16, 16), :] = pltpu.roll(wide, 127, 1).astype(BF16)
-
-    def wide_rows(start):
-        a = wide_a_ref[pl.ds(start, 16), :].astype(F32)
-        b = wide_b_ref[pl.ds(start, 16), :].astype(F32)
-        return jnp.where(chip_even, b, a), jnp.where(chip_even, a, b)
-
-    def net_rows(start):
-        a = net_a_ref[pl.ds(start, 16), :].astype(F32)
-        b = net_b_ref[pl.ds(start, 16), :].astype(F32)
-        return jnp.where(net_even, b, a), jnp.where(net_even, a, b)
-
+def slab(ref, start, pieces):
+    for i, piece in enumerate(pieces):
+        wide = piece.astype(F32)
+        ref[pl.ds(start + i * 16, 16), :] = pltpu.roll(wide, 1, 1).astype(BF16)
+        ref[pl.ds(start + 48 + i * 16, 16), :] = wide.astype(BF16)
+        ref[pl.ds(start + 96 + i * 16, 16), :] = pltpu.roll(wide, 127, 1).astype(BF16)
+
+
+def rows_of(even, a_ref, b_ref, start):
+    a = a_ref[pl.ds(start, 16), :].astype(F32)
+    b = b_ref[pl.ds(start, 16), :].astype(F32)
+    return jnp.where(even, b, a), jnp.where(even, a, b)
+
+
+def layers(first, second, band1_ref, band2_ref, bias_ref):
+    rows = jnp.concatenate(
+        [jnp.concatenate(first, axis=0), jnp.concatenate(second, axis=0)], axis=1
+    )
     bias = jnp.concatenate([bias_ref[...]] * 8, axis=0)
     bias = jnp.concatenate([bias, bias], axis=1)
-
-    def layers(j, k):
-        rows = jnp.concatenate(
-            [columns[pl.ds(j * 144, 432), :], columns[pl.ds(k * 144, 432), :]], axis=1
-        )
-        pre = jnp.dot(band1_ref[:, :432], rows, preferred_element_type=F32) + bias
-        inner = pre * (0.7978845608028654 + 0.7978845608028654 * 0.044715 * (pre * pre))
-        half = 0.5 * pre
-        hidden = (half + half * jnp.tanh(inner)).astype(BF16)
-        both = jnp.dot(band2_ref[...], hidden, preferred_element_type=F32)
-        parts[j] = both[:, :128]
-        parts[k] = both[:, 128:]
-
-    for j in range(3, 7):
-        at = (j - 3) * 16
-        left, right = wide_rows(at)
-        slab(j, [left, coarse_ref[pl.ds(at, 16), :], right])
-    layers(3, 4)
+    pre = jnp.dot(band1_ref[:, :432], rows, preferred_element_type=F32) + bias
+    inner = pre * (0.7978845608028654 + 0.7978845608028654 * 0.044715 * (pre * pre))
+    half = 0.5 * pre
+    hidden = (half + half * jnp.tanh(inner)).astype(BF16)
+    both = jnp.dot(band2_ref[...], hidden, preferred_element_type=F32)
+    return both[:, :128], both[:, 128:]
+
+
+def half_of(pair, i):
+    return pair[i // 2][(i % 2) * 8 : (i % 2) * 8 + 8]
+
+
+def velocity(q_ref, z, x, c, low):
+    first = jnp.broadcast_to(q_ref[z, x, c : c + 1, :], (8, 128))
+    second = jnp.broadcast_to(q_ref[z, x, c + 4 : c + 5, :], (8, 128))
+    return jnp.where(low, first, second)
+
+
+def before_kernel(weights, *refs):
+    keep_base, keep_state, step = weights
+    info_ref, q_ref, coarse_ref, wide_a_ref, wide_b_ref, band1_ref, band2_ref, bias_ref = refs[:8]
+    base_ref = refs[8] if keep_base else None
+    columns, parts, partial = refs[-3:]
+    chip_even = info_ref[1] == 0
+    for j in range(4):
+        left, right = rows_of(chip_even, wide_a_ref, wide_b_ref, j * 16)
+        slab(columns, j * 144, [left, coarse_ref[pl.ds(j * 16, 16), :], right])
+    pieces = [columns[pl.ds(j * 144, 144), :] for j in range(4)]
+    parts[0], parts[1] = layers(pieces[:3], pieces[1:], band1_ref, band2_ref, bias_ref)
+
+    low = lax.broadcasted_iota(jnp.int32, (8, 128), 0) < 4
+    sides = [rows_of(chip_even, wide_a_ref, wide_b_ref, 64 + z * 8) for z in range(0, 8, 2)]
+    left, right = zip(*sides)
+    for z in range(8):
+        for x in range(8):
+            here = q_ref[z, x]
+            xp = q_ref[z, x + 1] if x < 7 else half_of(right, z)
+            xm = q_ref[z, x - 1] if x > 0 else half_of(left, z)
+            if z == 0:
+                along_z, slope_z = q_ref[1, x], q_ref[1, x]
+            elif z == 7:
+                along_z, slope_z = q_ref[6, x], -q_ref[6, x]
+            else:
+                along_z = q_ref[z + 1, x] + q_ref[z - 1, x]
+                slope_z = q_ref[z + 1, x] - q_ref[z - 1, x]
+            swap = pltpu.roll(here, 4, 0)
+            back, ahead = pltpu.roll(swap, 1, 1), pltpu.roll(swap, 127, 1)
+            far = jnp.where(low, back, ahead)
+            slope_y = jnp.where(low, swap - back, ahead - swap)
+            spread = along_z + (xp + xm) + (swap + far)
+            u, v, w = (velocity(q_ref, z, x, c, low) for c in range(3))
+            advect = u * (xp - xm) + v * slope_y + w * slope_z
+            value = (keep_state - 6.0 * step * viscosity) * here
+            value = value + (step * viscosity) * spread - (0.5 * step) * advect
+            if keep_base:
+                value = value + keep_base * base_ref[z, x]
+            partial[z, x] = value
+
+
+def after_body(
+    step, info_ref, q_ref, own_columns, own_parts, partial_ref, net_a_ref, net_b_ref,
+    band1_ref, band2_ref, bias_ref, div_ref, columns, parts, stress, new_ref,
+):
+    chip_even, net_even = info_ref[1] == 0, info_ref[2] == 0
+    left_at, right_at = jnp.where(chip_even, 160, 112), jnp.where(chip_even, 112, 160)
     for i in range(3):
         starts = [pl.multiple_of(at + i * 16, 16) for at in (left_at, 0, right_at)]
-        below, above = zip(*[net_rows(start) for start in starts])
-        slab(i, below)
-        slab(7 + i, above)
-    layers(1, 2)
-    layers(5, 6)
-    layers(0, 7)
+        below, above = zip(*[rows_of(net_even, net_a_ref, net_b_ref, start) for start in starts])
+        slab(columns, i * 144, below)
+        slab(columns, (3 + i) * 144, above)
+
+    def piece(j):
+        if 3 <= j < 7:
+            return own_columns[pl.ds((j - 3) * 144, 144), :]
+        return columns[pl.ds((j if j < 3 else j - 4) * 144, 144), :]
+
+    for j, k in ((1, 2), (5, 6), (0, 7)):
+        parts[j], parts[k] = layers(
+            [piece(j + i) for i in range(3)], [piece(k + i) for i in range(3)],
+            band1_ref, band2_ref, bias_ref,
+        )
+
+    def part(j, at):
+        return own_parts[j - 3, at, :] if 3 <= j < 5 else parts[j, at, :]
 
     for k in range(6):
         rows = []
         for xo in range(6):
             sums = []
             for dy in range(3):
-                at = [pl.ds(xo * 80 + (dz * 3 + dy) * 8, 8) for dz in range(3)]
-                sums.append(parts[k, at[0], :] + parts[k + 1, at[1], :] + parts[k + 2, at[2], :])
+                at = [pl.ds(xo * 72 + (dz * 3 + dy) * 8, 8) for dz in range(3)]
+                sums.append(part(k, at[0]) + part(k + 1, at[1]) + part(k + 2, at[2]))
             rows.append(sums[1] + pltpu.roll(sums[0], 1, 1) + pltpu.roll(sums[2], 127, 1))
         stress[pl.ds(k * 48, 48), :] = jnp.concatenate(rows, axis=0).astype(BF16)
-    low = lax.broadcasted_iota(jnp.int32, (8, 128), 0) < 4
     forces = []
     for k in range(1, 5, 2):
         operands = []
@@ -238,73 +289,36 @@
                     axis=0,
                 )
             )
-        both = jnp.dot(
+        both = step * jnp.dot(
             div_ref[...], jnp.concatenate(operands, axis=1), preferred_element_type=F32
         )
         forces += [both[:, :128], both[:, 128:]]
 
-    below, above = zip(*[net_rows(48 + x * 8) for x in range(0, 8, 2)])
-    left, right = zip(*[wide_rows(64 + z * 8) for z in range(0, 8, 2)])
-
-    def half_of(pair, i):
-        return pair[i // 2][(i % 2) * 8 : (i % 2) * 8 + 8]
-
-    def cell(z, x):
-        if z < 0:
-            return half_of(below, x)
-        if z > 7:
-            return half_of(above, x)
-        if x < 0:
-            return half_of(left, z)
-        if x > 7:
-            return half_of(right, z)
-        return q_ref[z, x]
-
+    low = lax.broadcasted_iota(jnp.int32, (8, 128), 0) < 4
+    ends = [rows_of(net_even, net_a_ref, net_b_ref, 48 + x * 8) for x in range(0, 8, 2)]
+    below, above = zip(*ends)
     for z in range(8):
         for x in range(8):
-            here = q_ref[z, x]
-            zp, zm, xp, xm = cell(z + 1, x), cell(z - 1, x), cell(z, x + 1), cell(z, x - 1)
-            swap = pltpu.roll(here, 4, 0)
-            back, ahead = pltpu.roll(swap, 1, 1), pltpu.roll(swap, 127, 1)
-            far = jnp.where(low, back, ahead)
-            slope_y = jnp.where(low, swap - back, ahead - swap)
-            spread = (zp + zm) + (xp + xm) + (swap + far) - 6.0 * here
-
-            def velocity(c):
-                first = jnp.broadcast_to(q_ref[z, x, c : c + 1, :], (8, 128))
-                second = jnp.broadcast_to(q_ref[z, x, c + 4 : c + 5, :], (8, 128))
-                return jnp.where(low, first, second)
-
-            advect = velocity(0) * (xp - xm) + velocity(1) * slope_y + velocity(2) * (zp - zm)
-            force = forces[z // 2][(x // 2) * 8 : (x // 2) * 8 + 8]
-            rate = viscosity * spread - 0.5 * advect + force
-            new_ref[z, x] = update(z, x, here, rate)
-
-
-def stage1_kernel(*refs):
+            value = partial_ref[z, x] + forces[z // 2][(x // 2) * 8 : (x // 2) * 8 + 8]
+            if z == 0:
+                w = velocity(q_ref, z, x, 2, low)
+                value = value + (step * viscosity + (0.5 * step) * w) * half_of(below, x)
+            if z == 7:
+                w = velocity(q_ref, z, x, 2, low)
+                value = value + (step * viscosity - (0.5 * step) * w) * half_of(above, x)
+            new_ref[z, x] = value
+
+
+def after_kernel(step, *refs):
     ins, outs, scratch = refs[:11], refs[11:16], refs[16:]
-    stage_body(*ins, *scratch, lambda z, x, q, r: q + time_step * r, outs[0])
+    after_body(step, *ins, *scratch, outs[0])
     emit_messages(ins[0], *outs)
 
 
-def stage2_kernel(*refs):
-    ins, base_ref, outs, scratch = refs[:11], refs[11], refs[12:17], refs[17:]
-
-    def update(z, x, q, r):
-        return 0.75 * base_ref[z, x] + 0.25 * (q + time_step * r)
-
-    stage_body(*ins, *scratch, update, outs[0])
-    emit_messages(ins[0], *outs)
-
-
-def stage3_kernel(*refs):
-    ins, base_ref, outs, scratch, new = refs[:11], refs[11], refs[12:14], refs[14:-1], refs[-1]
+def last_kernel(step, *refs):
+    ins, outs, scratch, new = refs[:11], refs[11:13], refs[13:-1], refs[-1]
     core = ins[0][0]
-
-    def update(z, x, q, r):
-        return base_ref[z, x] * (1.0 / 3.0) + (2.0 / 3.0) * (q + time_step * r)
-
-    stage_body(*ins, *scratch, update, new)
+    after_body(step, *ins, *scratch, new)
     outs[0][...] = new[:, pl.ds(core * 4, 4)].reshape(256, 128)
     outs[1][...] = new[:, pl.ds((1 - core) * 4, 4)].reshape(256, 128)
 
@@ -369,20 +383,19 @@
 def per_device(fields, conv1_weight, conv1_bias, conv2_weight):
     wide, net = lax.axis_index("wide"), lax.axis_index("net")
     info = jnp.stack([wide % 2, (wide // 2) % 2, net % 2]).astype(jnp.int32)
-    parity = near(jnp.asarray(split_parity(), BF16))
-    native, same, cross = call(
+    native, same, cross, parity = call(
         pack_kernel,
-        [((256, 128), F32), ((32, 128), F32), ((32, 128), F32)],
+        [((256, 128), F32), ((32, 128), F32), ((32, 128), F32), ((256, 256), BF16)],
         [pltpu.VMEM((128, 256), F32)],
-        info, fields, parity,
+        info, fields,
     )
     other = near(partner(native))
     same = near(edge_shift(same, False))
     cross = near(edge_shift(cross, True))
     fixed = call(
         weights_kernel,
-        [((256, 512), BF16), ((480, 256), BF16), ((32, 128), F32)],
-        [pltpu.VMEM((32, 512), F32), pltpu.VMEM((80, 256), F32)],
+        [((256, 512), BF16), ((432, 256), BF16), ((32, 128), F32)],
+        [pltpu.VMEM((32, 512), F32), pltpu.VMEM((72, 256), F32), pltpu.VMEM((432, 256), F32)],
         info, conv1_weight, conv2_weight, conv1_bias.reshape(1, 32),
     )
     fixed = (*map(near, fixed), near(jnp.asarray(divergence_matrix(), BF16)))
@@ -390,42 +403,49 @@
         assemble_kernel,
         [((8, 8, 8, 128), F32)] + MESSAGES,
         [],
-        info, near(native), other, same, cross,
-    )
-    base = near(base)
+        info, near(native), other, same, cross, fixed[2],
+    )
+    state = base = near(base)
+    even = net % 2 == 0
+    stages = ((0.0, 1.0, time_step), (0.75, 0.25, 0.25 * time_step), (1.0 / 3.0, 2.0 / 3.0, 2.0 / 3.0 * time_step))
     scratch = [
-        pltpu.VMEM((1440, 128), BF16),
-        pltpu.VMEM((8, 480, 128), F32),
+        pltpu.VMEM((864, 128), BF16),
+        pltpu.VMEM((8, 432, 128), F32),
         pltpu.VMEM((288, 128), BF16),
     ]
-    even = net % 2 == 0
-
-    def exchange(wide_a, wide_b, net_a, net_b):
+    for stage, weights in enumerate(stages):
+        wide_a, wide_b, net_a, net_b = messages
         got_a, got_b = chip_swap(wide_a, 0), chip_swap(wide_b, 1)
         rows_a = [jnp.where(even, got[16:64], got[:48]) for got in (got_a, got_b)]
         rows_b = [jnp.where(even, got[:48], got[16:64]) for got in (got_a, got_b)]
         far_a = net_swap(jnp.concatenate([net_a, *rows_a], axis=0), 0)
         far_b = net_swap(jnp.concatenate([net_b, *rows_b], axis=0), 1)
-        return map(near, (wide_a, got_a, got_b, far_a, far_b))
-
-    state_out = [((8, 8, 8, 128), F32)] + MESSAGES
-    one, *messages = call(
-        stage1_kernel, state_out, scratch, info, base, *exchange(*messages), *fixed
-    )
-    two, *messages = call(
-        stage2_kernel, state_out, scratch, info, near(one), *exchange(*messages), *fixed, base
-    )
+        before = call(
+            functools.partial(before_kernel, weights),
+            [((576, 128), BF16), ((2, 432, 128), F32), ((8, 8, 8, 128), F32)],
+            [],
+            info, state, *map(near, (wide_a, got_a, got_b)), *fixed[:3], *([base] if stage else []),
+        )
+        ins = (info, state, *map(near, before), near(far_a), near(far_b), *fixed)
+        if stage < 2:
+            state, *messages = call(
+                functools.partial(after_kernel, weights[2]),
+                [((8, 8, 8, 128), F32)] + MESSAGES,
+                scratch,
+                *ins,
+            )
+            state = near(state)
     own, away = call(
-        stage3_kernel,
+        functools.partial(last_kernel, stages[2][2]),
         [((256, 128), F32)] * 2,
         scratch + [pltpu.VMEM((8, 8, 8, 128), F32)],
-        info, near(two), *exchange(*messages), *fixed, base,
+        *ins,
     )
     return call(
         finish_kernel,
         None,
         [pltpu.VMEM((256, 128), F32), pltpu.VMEM((128, 256), F32)],
-        info, near(own), near(partner(away)), parity,
+        info, near(own), near(partner(away)), near(parity),
         result=jax.ShapeDtypeStruct(fields.shape, F32),
     )
 

time: 75.7 us -> 71.8 us (0.948)
  waiting for transfers between devices: 19.7 us -> 16.3 us
    ppermute x2, waiting for transfers between devices: 3.16 us -> 0.59 us  [edge_shift(): return lax.ppermute(value, ('wide', 'narrow'), pairs)]
    ppermute x6, waiting for transfers between devices: 6.84 us -> 6.02 us  [net_swap(): return lax.ppermute(value, 'net', pairs)]
    pallas_call x7 -> x10, Pallas kernels: 14 us -> 14.5 us  [call(): pl.pallas_call(kernel, out_shape=result or [pltpu.VMEM(s, d) for s, d in...]
  transfers between devices with their start and end apart: 16 -> 16, of which waited for: 12 -> 11; matrix products, arithmetic and copies ran while one was open for 2% -> 0% of each run, Pallas kernels for 2% -> 6%
where the time goes in v2:
time: 71.8 us; the launch traced here: 71.7 us
  starting transfers between devices  38 us (53%)
  waiting for transfers between devices  16.3 us (23%)
  Pallas kernels  14.5 us (20%)
  local copies, waits for them, and re-layouts  2.58 us (4%)
    ppermute x6, starting transfers between devices, net_swap(): return lax.ppermute(value, 'net', pairs)  19.1 us
    pallas_call x10, Pallas kernels, call(): pl.pallas_call(kernel, out_shape=result or [pltpu.VMEM(s, d) for s, d in...  14.5 us
    ppermute x2, starting transfers between devices, partner(): lax.ppermute(value, 'wide', [(i, i ^ 1) for i in range(lax.axis_size('wid...  10.5 us
    ppermute x6, waiting for transfers between devices, chip_swap(): return lax.ppermute(value, 'wide', pairs)  8.69 us
    ppermute x6, waiting for transfers between devices, net_swap(): return lax.ppermute(value, 'net', pairs)  6.02 us
    ppermute x6, starting transfers between devices, chip_swap(): return lax.ppermute(value, 'wide', pairs)  5.67 us
    ppermute x2, starting transfers between devices, edge_shift(): return lax.ppermute(value, ('wide', 'narrow'), pairs)  2.64 us
    unnamed x12, local copies, waits for them, and re-layouts  2.58 us
  transfers between devices with their start and end apart: 16, of which 11 were waited for; matrix products, arithmetic and copies ran while one was open for 0% of the time, Pallas kernels for 6%

profile of v2, /device:TPU:1, one launch (start us, length us, event | category | flops | bytes accessed | tf_op | source)
XLA Modules:
  0.0 71.7 jit_solution(9034730091592616705)
XLA Ops:
  0.0 0.1 pad_add_fusion.info_ref.refs_0_
  0.1 0.0 copy-start.1
  0.1 0.9 %copy-done.1 = f32[4,8,4,256]{3,2,1,0:T(4,128)S(1)} copy-done((f32[4,8,4,256]{3,2,1,0:T(4,128)S(1)}, f32[4,8,4,256]{3,2,1,0:T(4,128)}, u32[]{:S(2)}) %copy-start.1) | copy-done | bytes 131096
  1.0 0.0 copy-start.3
  1.0 0.9 %shard_map.55 = (f32[256,128]{1,0:T(8,128)S(1)}, f32[32,128]{1,0:T(8,128)S(1)}, f32[32,128]{1,0:T(8,128)S(1)}, bf16[256,256]{1,0:T(8,128)(2,1)S(1)}) custom-call(s32[3]{0:T(128)S(1)} %pad_add_fusion.info_ref.refs_0_, f32[4,8,4,256]{3,2,1,0:T(4,128)S(1)} %copy-done.1), custom_call_target="tpu_custom_call" | custom-call | tf_op jit(solution)/shard_map/pallas_call | solution.py:41
  1.9 3.3 %collective-permute-start = (f32[256,128]{1,0:T(8,128)S(1)}, f32[256,128]{1,0:T(8,128)S(1)}, u32[]{:S(2)}, u32[]{:S(2)}) collective-permute-start(f32[256,128]{1,0:T(8,128)S(1)} %get-tuple-element.38.own_ref), channel_id=1, source_target_pairs={{0,32},{32,0},{64,96},{96,64},{128,160},{160,128},{192,224},{224,1... | collective-permute-start | bytes 393224 | tf_op jit(solution)/shard_map/ppermute | solution.py:367
  5.2 2.6 %collective-permute-start.1 = (f32[32,128]{1,0:T(8,128)S(1)}, f32[32,128]{1,0:T(8,128)S(1)}, u32[]{:S(2)}, u32[]{:S(2)}) collective-permute-start(f32[32,128]{1,0:T(8,128)S(1)} %get-tuple-element.39), channel_id=1, source_target_pairs={{0,8},{8,16},{16,24},{24,0},{32,56},{40,32},{48,40},{56,48},{64,72... | collective-permute-start | bytes 49160 | tf_op jit(solution)/shard_map/ppermute | solution.py:380
  7.8 0.0 copy-start.4
  7.8 0.0 collective-permute-start.2
  7.8 0.0 copy-done.3
  7.9 0.7 copy-done.4
  8.6 0.3 copy.6.w1_ref
  8.8 0.0 copy-start.2
  8.9 0.6 copy-done.2
  9.5 0.9 %shard_map.56 = (bf16[256,512]{1,0:T(8,128)(2,1)S(1)}, bf16[432,256]{1,0:T(8,128)(2,1)S(1)}, f32[32,128]{1,0:T(8,128)S(1)}) custom-call(s32[3]{0:T(128)S(1)} %pad_add_fusion.info_ref.refs_0_, bf16[27,32,4]{2,1,0:T(8,128)(2,1)S(1)} %copy.6.w1_ref, bf16[27,6,32]{2,1,0:T(8,128)(2,1)S(1)} %copy.7.w2_ref, f32[1,32]{1,0:T(1,128)S(1)} %bitcast.4), custom_call_target="tpu_custom_call" | custom-call | tf_op jit(solution)/shard_map/pallas_call | solution.py:41
  10.4 0.0 collective-permute-done.1.same_ref
  10.4 0.6 collective-permute-done.2.cross_ref
  11.0 0.0 collective-permute-done.other_ref
  11.0 0.8 %shard_map.57 = (f32[8,8,8,128]{3,2,1,0:T(8,128)S(1)}, bf16[128,128]{1,0:T(8,128)(2,1)S(1)}, bf16[128,128]{1,0:T(8,128)(2,1)S(1)}, bf16[112,128]{1,0:T(8,128)(2,1)S(1)}, bf16[112,128]{1,0:T(8,128)(2,1)S(1)}) custom-call(s32[3]{0:T(128)S(1)} %pad_add_fusion.info_ref.refs_0_, f32[256,128]{1,0:T(8,128)S(1)} %get-tuple-element.38.own_ref, ...), custom_call_target="tpu_custom_call" | custom-call | tf_op jit(solution)/shard_map/pallas_call | solution.py:41
  11.8 2.8 %collective-permute-start.4 = (bf16[128,128]{1,0:T(8,128)(2,1)S(1)}, bf16[128,128]{1,0:T(8,128)(2,1)S(1)}, u32[]{:S(2)}, u32[]{:S(2)}) collective-permute-start(bf16[128,128]{1,0:T(8,128)(2,1)S(1)} %get-tuple-element.44), channel_id=1, source_target_pairs={{0,192},{32,224},{64,128},{96,160},{128,64},{160,96},{192,0},{224,... | collective-permute-start | bytes 98312 | tf_op jit(solution)/shard_map/ppermute | solution.py:357
  14.6 0.0 collective-permute-start.3
  14.6 1.7 %collective-permute-done.4.refs_4_ = bf16[128,128]{1,0:T(8,128)(2,1)S(1)} collective-permute-done((bf16[128,128]{1,0:T(8,128)(2,1)S(1)}, bf16[128,128]{1,0:T(8,128)(2,1)S(1)}, u32[]{:S(2)}, u32[]{:S(2)}) %collective-permute-start.4) | collective-permute-done | bytes 32800 | tf_op jit(solution)/shard_map/ppermute | solution.py:357
  16.3 1.5 %collective-permute-done.3.refs_3_ = bf16[128,128]{1,0:T(8,128)(2,1)S(1)} collective-permute-done((bf16[128,128]{1,0:T(8,128)(2,1)S(1)}, bf16[128,128]{1,0:T(8,128)(2,1)S(1)}, u32[]{:S(2)}, u32[]{:S(2)}) %collective-permute-start.3) | collective-permute-done | bytes 32800 | tf_op jit(solution)/shard_map/ppermute | solution.py:357
  17.8 1.3 %collective-permute-start.5 = (bf16[208,128]{1,0:T(8,128)(2,1)S(1)}, bf16[208,128]{1,0:T(8,128)(2,1)S(1)}, u32[]{:S(2)}, u32[]{:S(2)}) collective-permute-start(bf16[208,128]{1,0:T(8,128)(2,1)S(1)} %pad_maximum_fusion), channel_id=1, source_target_pairs={{0,1},{1,0},{2,3},{3,2},{4,5},{5,4},{6,7},{7,6},{8,9},{9,8},{10,11... | collective-permute-start | bytes 159752 | tf_op jit(solution)/shard_map/ppermute | solution.py:363
  19.1 5.8 %collective-permute-start.6 = (bf16[208,128]{1,0:T(8,128)(2,1)S(1)}, bf16[208,128]{1,0:T(8,128)(2,1)S(1)}, u32[]{:S(2)}, u32[]{:S(2)}) collective-permute-start(bf16[208,128]{1,0:T(8,128)(2,1)S(1)} %pad_maximum_fusion.1), channel_id=1, source_target_pairs={{0,7},{1,2},{2,1},{3,4},{4,3},{5,6},{6,5},{7,0},{8,15},{9,10},{10,... | collective-permute-start | bytes 159752 | tf_op jit(solution)/shard_map/ppermute | solution.py:363
  24.9 0.0 copy-start
  24.9 1.2 %shard_map.58 = (bf16[576,128]{1,0:T(8,128)(2,1)S(1)}, f32[2,432,128]{2,1,0:T(8,128)S(1)}, f32[8,8,8,128]{3,2,1,0:T(8,128)S(1)}) custom-call(s32[3]{0:T(128)S(1)} %pad_add_fusion.info_ref.refs_0_, f32[8,8,8,128]{3,2,1,0:T(8,128)S(1)} %get-tuple-element.42.refs_1_.refs_8_, bf16[128,128]{1,0:T(8,128)(2,1)S(1)} %get-tuple-element.43.refs_2_, ...), custom_call_target="tpu_custom_call" | custom-call | tf_op jit(solution)/shard_map/pallas_call | solution.py:41
  26.1 0.0 collective-permute-done.5.refs_5_
  26.1 2.0 %collective-permute-done.6.refs_6_ = bf16[208,128]{1,0:T(8,128)(2,1)S(1)} collective-permute-done((bf16[208,128]{1,0:T(8,128)(2,1)S(1)}, bf16[208,128]{1,0:T(8,128)(2,1)S(1)}, u32[]{:S(2)}, u32[]{:S(2)}) %collective-permute-start.6) | collective-permute-done | bytes 53280 | tf_op jit(solution)/shard_map/ppermute | solution.py:363
  28.1 0.0 copy-done
  28.1 2.2 %shard_map.59 = (f32[8,8,8,128]{3,2,1,0:T(8,128)S(1)}, bf16[128,128]{1,0:T(8,128)(2,1)S(1)}, bf16[128,128]{1,0:T(8,128)(2,1)S(1)}, bf16[112,128]{1,0:T(8,128)(2,1)S(1)}, bf16[112,128]{1,0:T(8,128)(2,1)S(1)}) custom-call(s32[3]{0:T(128)S(1)} %pad_add_fusion.info_ref.refs_0_, f32[8,8,8,128]{3,2,1,0:T(8,128)S(1)} %get-tuple-element.42.refs_1_.refs_8_, ...), custom_call_target="tpu_custom_call" | custom-call | tf_op jit(solution)/shard_map/pallas_call | solution.py:41
  30.4 1.5 %collective-permute-start.8 = (bf16[128,128]{1,0:T(8,128)(2,1)S(1)}, bf16[128,128]{1,0:T(8,128)(2,1)S(1)}, u32[]{:S(2)}, u32[]{:S(2)}) collective-permute-start(bf16[128,128]{1,0:T(8,128)(2,1)S(1)} %get-tuple-element.54), channel_id=1, source_target_pairs={{0,192},{32,224},{64,128},{96,160},{128,64},{160,96},{192,0},{224,... | collective-permute-start | bytes 98312 | tf_op jit(solution)/shard_map/ppermute | solution.py:357
  31.9 0.0 collective-permute-start.7
  31.9 2.6 %collective-permute-done.8.refs_4_ = bf16[128,128]{1,0:T(8,128)(2,1)S(1)} collective-permute-done((bf16[128,128]{1,0:T(8,128)(2,1)S(1)}, bf16[128,128]{1,0:T(8,128)(2,1)S(1)}, u32[]{:S(2)}, u32[]{:S(2)}) %collective-permute-start.8) | collective-permute-done | bytes 32800 | tf_op jit(solution)/shard_map/ppermute | solution.py:357
  34.5 0.2 collective-permute-done.7.refs_3_
  34.6 0.1 collective-permute-start.9
  34.8 5.7 %collective-permute-start.10 = (bf16[208,128]{1,0:T(8,128)(2,1)S(1)}, bf16[208,128]{1,0:T(8,128)(2,1)S(1)}, u32[]{:S(2)}, u32[]{:S(2)}) collective-permute-start(bf16[208,128]{1,0:T(8,128)(2,1)S(1)} %pad_maximum_fusion.3), channel_id=1, source_target_pairs={{0,7},{1,2},{2,1},{3,4},{4,3},{5,6},{6,5},{7,0},{8,15},{9,10},{10,... | collective-permute-start | bytes 159752 | tf_op jit(solution)/shard_map/ppermute | solution.py:363
  40.5 1.2 %shard_map.60 = (bf16[576,128]{1,0:T(8,128)(2,1)S(1)}, f32[2,432,128]{2,1,0:T(8,128)S(1)}, f32[8,8,8,128]{3,2,1,0:T(8,128)S(1)}) custom-call(s32[3]{0:T(128)S(1)} %pad_add_fusion.info_ref.refs_0_, f32[8,8,8,128]{3,2,1,0:T(8,128)S(1)} %get-tuple-element.52.refs_1_, bf16[128,128]{1,0:T(8,128)(2,1)S(1)} %get-tuple-element.53.refs_2_, ...), custom_call_target="tpu_custom_call" | custom-call | tf_op jit(solution)/shard_map/pallas_call | solution.py:41
  41.7 0.0 collective-permute-done.9.refs_5_
  41.8 2.1 %collective-permute-done.10.refs_6_ = bf16[208,128]{1,0:T(8,128)(2,1)S(1)} collective-permute-done((bf16[208,128]{1,0:T(8,128)(2,1)S(1)}, bf16[208,128]{1,0:T(8,128)(2,1)S(1)}, u32[]{:S(2)}, u32[]{:S(2)}) %collective-permute-start.10) | collective-permute-done | bytes 53280 | tf_op jit(solution)/shard_map/ppermute | solution.py:363
  43.8 2.2 %shard_map.61 = (f32[8,8,8,128]{3,2,1,0:T(8,128)S(1)}, bf16[128,128]{1,0:T(8,128)(2,1)S(1)}, bf16[128,128]{1,0:T(8,128)(2,1)S(1)}, bf16[112,128]{1,0:T(8,128)(2,1)S(1)}, bf16[112,128]{1,0:T(8,128)(2,1)S(1)}) custom-call(s32[3]{0:T(128)S(1)} %pad_add_fusion.info_ref.refs_0_, f32[8,8,8,128]{3,2,1,0:T(8,128)S(1)} %get-tuple-element.52.refs_1_, ...), custom_call_target="tpu_custom_call" | custom-call | tf_op jit(solution)/shard_map/pallas_call | solution.py:41
  46.1 1.4 %collective-permute-start.12 = (bf16[128,128]{1,0:T(8,128)(2,1)S(1)}, bf16[128,128]{1,0:T(8,128)(2,1)S(1)}, u32[]{:S(2)}, u32[]{:S(2)}) collective-permute-start(bf16[128,128]{1,0:T(8,128)(2,1)S(1)} %get-tuple-element.62), channel_id=1, source_target_pairs={{0,192},{32,224},{64,128},{96,160},{128,64},{160,96},{192,0},{224,... | collective-permute-start | bytes 98312 | tf_op jit(solution)/shard_map/ppermute | solution.py:357
  47.5 0.0 collective-permute-start.11
  47.5 2.7 %collective-permute-done.12.refs_4_ = bf16[128,128]{1,0:T(8,128)(2,1)S(1)} collective-permute-done((bf16[128,128]{1,0:T(8,128)(2,1)S(1)}, bf16[128,128]{1,0:T(8,128)(2,1)S(1)}, u32[]{:S(2)}, u32[]{:S(2)}) %collective-permute-start.12) | collective-permute-done | bytes 32800 | tf_op jit(solution)/shard_map/ppermute | solution.py:357
  50.2 0.1 collective-permute-done.11.refs_3_
  50.2 0.1 collective-permute-start.13
  50.4 6.1 %collective-permute-start.14 = (bf16[208,128]{1,0:T(8,128)(2,1)S(1)}, bf16[208,128]{1,0:T(8,128)(2,1)S(1)}, u32[]{:S(2)}, u32[]{:S(2)}) collective-permute-start(bf16[208,128]{1,0:T(8,128)(2,1)S(1)} %pad_maximum_fusion.5), channel_id=1, source_target_pairs={{0,7},{1,2},{2,1},{3,4},{4,3},{5,6},{6,5},{7,0},{8,15},{9,10},{10,... | collective-permute-start | bytes 159752 | tf_op jit(solution)/shard_map/ppermute | solution.py:363
  56.4 1.2 %shard_map.62 = (bf16[576,128]{1,0:T(8,128)(2,1)S(1)}, f32[2,432,128]{2,1,0:T(8,128)S(1)}, f32[8,8,8,128]{3,2,1,0:T(8,128)S(1)}) custom-call(s32[3]{0:T(128)S(1)} %pad_add_fusion.info_ref.refs_0_, f32[8,8,8,128]{3,2,1,0:T(8,128)S(1)} %get-tuple-element.60.refs_1_, bf16[128,128]{1,0:T(8,128)(2,1)S(1)} %get-tuple-element.61.refs_2_, ...), custom_call_target="tpu_custom_call" | custom-call | tf_op jit(solution)/shard_map/pallas_call | solution.py:41
  57.7 0.0 collective-permute-done.13.refs_5_
  57.7 1.9 %collective-permute-done.14.refs_6_ = bf16[208,128]{1,0:T(8,128)(2,1)S(1)} collective-permute-done((bf16[208,128]{1,0:T(8,128)(2,1)S(1)}, bf16[208,128]{1,0:T(8,128)(2,1)S(1)}, u32[]{:S(2)}, u32[]{:S(2)}) %collective-permute-start.14) | collective-permute-done | bytes 53280 | tf_op jit(solution)/shard_map/ppermute | solution.py:363
  59.6 2.2 %shard_map.63 = (f32[256,128]{1,0:T(8,128)S(1)}, f32[256,128]{1,0:T(8,128)S(1)}) custom-call(s32[3]{0:T(128)S(1)} %pad_add_fusion.info_ref.refs_0_, f32[8,8,8,128]{3,2,1,0:T(8,128)S(1)} %get-tuple-element.60.refs_1_, bf16[576,128]{1,0:T(8,128)(2,1)S(1)} %get-tuple-element.63.refs_2_, f32[2,432,128]{2,1,0:T(8,128)S(1)} %get-tuple-element.64.refs_3_, ...), custom_call_target="tpu_custom_call" | custom-call | tf_op jit(solution)/shard_map/pallas_call | solution.py:41
  61.9 7.3 %collective-permute-start.15 = (f32[256,128]{1,0:T(8,128)S(1)}, f32[256,128]{1,0:T(8,128)S(1)}, u32[]{:S(2)}, u32[]{:S(2)}) collective-permute-start(f32[256,128]{1,0:T(8,128)S(1)} %get-tuple-element.69), channel_id=1, source_target_pairs={{0,32},{32,0},{64,96},{96,64},{128,160},{160,128},{192,224},{224,1... | collective-permute-start | bytes 393224 | tf_op jit(solution)/shard_map/ppermute | solution.py:367
  69.1 1.0 %collective-permute-done.15.other_ref = f32[256,128]{1,0:T(8,128)S(1)} collective-permute-done((f32[256,128]{1,0:T(8,128)S(1)}, f32[256,128]{1,0:T(8,128)S(1)}, u32[]{:S(2)}, u32[]{:S(2)}) %collective-permute-start.15) | collective-permute-done | bytes 131104 | tf_op jit(solution)/shard_map/ppermute | solution.py:367
  70.1 1.6 %shard_map.64 = f32[4,8,4,256]{3,2,1,0:T(4,128)} custom-call(s32[3]{0:T(128)S(1)} %pad_add_fusion.info_ref.refs_0_, f32[256,128]{1,0:T(8,128)S(1)} %get-tuple-element.68.own_ref, f32[256,128]{1,0:T(8,128)S(1)} %collective-permute-done.15.other_ref, bf16[256,256]{1,0:T(8,128)(2,1)S(1)} %get-tuple-element.70.parity_ref), custom_call_target="tpu_custom_call" | custom-call | tf_op jit(solution)/shard_map/pallas_call | solution.py:41
  (13 shorter events, 0.1 us)
Async XLA Ops:
  0.1 0.9 %copy-start.1 = (f32[4,8,4,256]{3,2,1,0:T(4,128)S(1)}, f32[4,8,4,256]{3,2,1,0:T(4,128)}, u32[]{:S(2)}) copy-start(f32[4,8,4,256]{3,2,1,0:T(4,128)} %fields_ref.1) | copy-start | bytes 393220
  1.0 6.8 %copy-start.3 = (bf16[27,6,32]{2,0,1:T(8,128)(2,1)S(1)}, bf16[27,6,32]{2,0,1:T(8,128)(2,1)}, u32[]{:S(2)}) copy-start(bf16[27,6,32]{2,0,1:T(8,128)(2,1)} %param.8) | copy-start | bytes 31108
  1.9 9.1 %collective-permute-start = (f32[256,128]{1,0:T(8,128)S(1)}, f32[256,128]{1,0:T(8,128)S(1)}, u32[]{:S(2)}, u32[]{:S(2)}) collective-permute-start(f32[256,128]{1,0:T(8,128)S(1)} %get-tuple-element.38.own_ref), channel_id=1, source_target_pairs={{0,32},{32,0},{64,96},{96,64},{128,160},{160,128},{192,224},{224,1... | collective-permute-start | bytes 393224 | tf_op jit(solution)/shard_map/ppermute | solution.py:367
  5.2 5.2 %collective-permute-start.1 = (f32[32,128]{1,0:T(8,128)S(1)}, f32[32,128]{1,0:T(8,128)S(1)}, u32[]{:S(2)}, u32[]{:S(2)}) collective-permute-start(f32[32,128]{1,0:T(8,128)S(1)} %get-tuple-element.39), channel_id=1, source_target_pairs={{0,8},{8,16},{16,24},{24,0},{32,56},{40,32},{48,40},{56,48},{64,72... | collective-permute-start | bytes 49160 | tf_op jit(solution)/shard_map/ppermute | solution.py:380
  7.8 0.7 %copy-start.4 = (bf16[27,32,4]{1,2,0:T(4,128)(2,1)S(1)}, bf16[27,32,4]{1,2,0:T(4,128)(2,1)}, u32[]{:S(2)}) copy-start(bf16[27,32,4]{1,2,0:T(4,128)(2,1)} %param.6) | copy-start | bytes 20740
  7.8 3.2 %collective-permute-start.2 = (f32[32,128]{1,0:T(8,128)S(1)}, f32[32,128]{1,0:T(8,128)S(1)}, u32[]{:S(2)}, u32[]{:S(2)}) collective-permute-start(f32[32,128]{1,0:T(8,128)S(1)} %get-tuple-element.40), channel_id=1, source_target_pairs={{0,56},{8,32},{16,40},{24,48},{32,8},{40,16},{48,24},{56,0},{64,12... | collective-permute-start | bytes 49160 | tf_op jit(solution)/shard_map/ppermute | solution.py:380
  8.8 0.7 copy-start.2
  11.8 4.5 %collective-permute-start.4 = (bf16[128,128]{1,0:T(8,128)(2,1)S(1)}, bf16[128,128]{1,0:T(8,128)(2,1)S(1)}, u32[]{:S(2)}, u32[]{:S(2)}) collective-permute-start(bf16[128,128]{1,0:T(8,128)(2,1)S(1)} %get-tuple-element.44), channel_id=1, source_target_pairs={{0,192},{32,224},{64,128},{96,160},{128,64},{160,96},{192,0},{224,... | collective-permute-start | bytes 98312 | tf_op jit(solution)/shard_map/ppermute | solution.py:357
  14.6 3.2 %collective-permute-start.3 = (bf16[128,128]{1,0:T(8,128)(2,1)S(1)}, bf16[128,128]{1,0:T(8,128)(2,1)S(1)}, u32[]{:S(2)}, u32[]{:S(2)}) collective-permute-start(bf16[128,128]{1,0:T(8,128)(2,1)S(1)} %get-tuple-element.43.refs_2_), channel_id=1, source_target_pairs={{0,64},{32,96},{64,0},{96,32},{128,192},{160,224},{192,128},{224,1... | collective-permute-start | bytes 98312 | tf_op jit(solution)/shard_map/ppermute | solution.py:357
  17.8 8.3 %collective-permute-start.5 = (bf16[208,128]{1,0:T(8,128)(2,1)S(1)}, bf16[208,128]{1,0:T(8,128)(2,1)S(1)}, u32[]{:S(2)}, u32[]{:S(2)}) collective-permute-start(bf16[208,128]{1,0:T(8,128)(2,1)S(1)} %pad_maximum_fusion), channel_id=1, source_target_pairs={{0,1},{1,0},{2,3},{3,2},{4,5},{5,4},{6,7},{7,6},{8,9},{9,8},{10,11... | collective-permute-start | bytes 159752 | tf_op jit(solution)/shard_map/ppermute | solution.py:363
  19.1 9.0 %collective-permute-start.6 = (bf16[208,128]{1,0:T(8,128)(2,1)S(1)}, bf16[208,128]{1,0:T(8,128)(2,1)S(1)}, u32[]{:S(2)}, u32[]{:S(2)}) collective-permute-start(bf16[208,128]{1,0:T(8,128)(2,1)S(1)} %pad_maximum_fusion.1), channel_id=1, source_target_pairs={{0,7},{1,2},{2,1},{3,4},{4,3},{5,6},{6,5},{7,0},{8,15},{9,10},{10,... | collective-permute-start | bytes 159752 | tf_op jit(solution)/shard_map/ppermute | solution.py:363
  24.9 3.2 %copy-start = (bf16[32,240]{1,0:T(8,128)(2,1)S(1)}, bf16[32,240]{1,0:T(8,128)(2,1)}, u32[]{:S(2)}) copy-start(bf16[32,240]{1,0:T(8,128)(2,1)} %constant.45.clone.refs_10_) | copy-start | bytes 46084
  30.4 4.1 %collective-permute-start.8 = (bf16[128,128]{1,0:T(8,128)(2,1)S(1)}, bf16[128,128]{1,0:T(8,128)(2,1)S(1)}, u32[]{:S(2)}, u32[]{:S(2)}) collective-permute-start(bf16[128,128]{1,0:T(8,128)(2,1)S(1)} %get-tuple-element.54), channel_id=1, source_target_pairs={{0,192},{32,224},{64,128},{96,160},{128,64},{160,96},{192,0},{224,... | collective-permute-start | bytes 98312 | tf_op jit(solution)/shard_map/ppermute | solution.py:357
  31.9 2.8 %collective-permute-start.7 = (bf16[128,128]{1,0:T(8,128)(2,1)S(1)}, bf16[128,128]{1,0:T(8,128)(2,1)S(1)}, u32[]{:S(2)}, u32[]{:S(2)}) collective-permute-start(bf16[128,128]{1,0:T(8,128)(2,1)S(1)} %get-tuple-element.53.refs_2_), channel_id=1, source_target_pairs={{0,64},{32,96},{64,0},{96,32},{128,192},{160,224},{192,128},{224,1... | collective-permute-start | bytes 98312 | tf_op jit(solution)/shard_map/ppermute | solution.py:357
  34.6 7.1 %collective-permute-start.9 = (bf16[208,128]{1,0:T(8,128)(2,1)S(1)}, bf16[208,128]{1,0:T(8,128)(2,1)S(1)}, u32[]{:S(2)}, u32[]{:S(2)}) collective-permute-start(bf16[208,128]{1,0:T(8,128)(2,1)S(1)} %pad_maximum_fusion.2), channel_id=1, source_target_pairs={{0,1},{1,0},{2,3},{3,2},{4,5},{5,4},{6,7},{7,6},{8,9},{9,8},{10,11... | collective-permute-start | bytes 159752 | tf_op jit(solution)/shard_map/ppermute | solution.py:363
  34.8 9.1 %collective-permute-start.10 = (bf16[208,128]{1,0:T(8,128)(2,1)S(1)}, bf16[208,128]{1,0:T(8,128)(2,1)S(1)}, u32[]{:S(2)}, u32[]{:S(2)}) collective-permute-start(bf16[208,128]{1,0:T(8,128)(2,1)S(1)} %pad_maximum_fusion.3), channel_id=1, source_target_pairs={{0,7},{1,2},{2,1},{3,4},{4,3},{5,6},{6,5},{7,0},{8,15},{9,10},{10,... | collective-permute-start | bytes 159752 | tf_op jit(solution)/shard_map/ppermute | solution.py:363
  46.1 4.1 %collective-permute-start.12 = (bf16[128,128]{1,0:T(8,128)(2,1)S(1)}, bf16[128,128]{1,0:T(8,128)(2,1)S(1)}, u32[]{:S(2)}, u32[]{:S(2)}) collective-permute-start(bf16[128,128]{1,0:T(8,128)(2,1)S(1)} %get-tuple-element.62), channel_id=1, source_target_pairs={{0,192},{32,224},{64,128},{96,160},{128,64},{160,96},{192,0},{224,... | collective-permute-start | bytes 98312 | tf_op jit(solution)/shard_map/ppermute | solution.py:357
  47.5 2.8 %collective-permute-start.11 = (bf16[128,128]{1,0:T(8,128)(2,1)S(1)}, bf16[128,128]{1,0:T(8,128)(2,1)S(1)}, u32[]{:S(2)}, u32[]{:S(2)}) collective-permute-start(bf16[128,128]{1,0:T(8,128)(2,1)S(1)} %get-tuple-element.61.refs_2_), channel_id=1, source_target_pairs={{0,64},{32,96},{64,0},{96,32},{128,192},{160,224},{192,128},{224,1... | collective-permute-start | bytes 98312 | tf_op jit(solution)/shard_map/ppermute | solution.py:357
  50.2 7.4 %collective-permute-start.13 = (bf16[208,128]{1,0:T(8,128)(2,1)S(1)}, bf16[208,128]{1,0:T(8,128)(2,1)S(1)}, u32[]{:S(2)}, u32[]{:S(2)}) collective-permute-start(bf16[208,128]{1,0:T(8,128)(2,1)S(1)} %pad_maximum_fusion.4), channel_id=1, source_target_pairs={{0,1},{1,0},{2,3},{3,2},{4,5},{5,4},{6,7},{7,6},{8,9},{9,8},{10,11... | collective-permute-start | bytes 159752 | tf_op jit(solution)/shard_map/ppermute | solution.py:363
  50.4 9.3 %collective-permute-start.14 = (bf16[208,128]{1,0:T(8,128)(2,1)S(1)}, bf16[208,128]{1,0:T(8,128)(2,1)S(1)}, u32[]{:S(2)}, u32[]{:S(2)}) collective-permute-start(bf16[208,128]{1,0:T(8,128)(2,1)S(1)} %pad_maximum_fusion.5), channel_id=1, source_target_pairs={{0,7},{1,2},{2,1},{3,4},{4,3},{5,6},{6,5},{7,0},{8,15},{9,10},{10,... | collective-permute-start | bytes 159752 | tf_op jit(solution)/shard_map/ppermute | solution.py:363
  61.9 8.2 %collective-permute-start.15 = (f32[256,128]{1,0:T(8,128)S(1)}, f32[256,128]{1,0:T(8,128)S(1)}, u32[]{:S(2)}, u32[]{:S(2)}) collective-permute-start(f32[256,128]{1,0:T(8,128)S(1)} %get-tuple-element.69), channel_id=1, source_target_pairs={{0,32},{32,0},{64,96},{96,64},{128,160},{160,128},{192,224},{224,1... | collective-permute-start | bytes 393224 | tf_op jit(solution)/shard_map/ppermute | solution.py:367

commit v3 on v2

--- a/solution.py
+++ b/solution.py
@@ -140,7 +140,7 @@
     emit_messages(info_ref, q_ref, wide_a_ref, wide_b_ref, net_a_ref, net_b_ref)
 
 
-def weights_kernel(info_ref, w1_ref, w2_ref, b_ref, band1_ref, band2_ref, bias_ref, flat1, flat2, tall):
+def weights_kernel(info_ref, w1_ref, w2_ref, b_ref, band1_ref, band2_ref, flat1, flat2, tall):
     flat1[...] = jnp.zeros_like(flat1)
     flat2[...] = jnp.zeros_like(flat2)
     for dz in range(3):
@@ -149,15 +149,24 @@
                 tap = 9 * dz + 3 * dx + dy
                 flat1[:, pl.ds((dz * 3 + dy) * 48 + (1 + dx) * 4, 4)] = w1_ref[tap].astype(F32)
                 flat2[pl.ds((dz * 3 + dy) * 8, 6), pl.ds(dx * 32, 32)] = w2_ref[tap].astype(F32)
-    for xo in range(8):
-        band1_ref[pl.ds(xo * 32, 32), :] = pltpu.roll(flat1[...], 4 * xo, 1).astype(BF16)
-    for xo in range(6):
-        tall[pl.ds(xo * 72, 72), :] = pltpu.roll(flat2[...], 32 * xo, 1)
-    band2_ref[...] = tall[...].astype(BF16)
     square = jnp.broadcast_to(b_ref[...], (32, 32))
     diagonal = lanes_of((32, 32)) == lax.broadcasted_iota(jnp.int32, (32, 32), 0)
-    column = jnp.sum(jnp.where(diagonal, square, 0.0), axis=1, keepdims=True)
-    bias_ref[...] = jnp.broadcast_to(column, (32, 128))
+    bias = 0.5 * jnp.sum(jnp.where(diagonal, square, 0.0), axis=1, keepdims=True)
+    first = bias.astype(BF16).astype(F32)
+    second = (bias - first).astype(BF16).astype(F32)
+    lane = lanes_of((32, 128))
+    extra = jnp.where(lane == 48, first, jnp.where(lane == 49, second, bias - first - second))
+    for xo in range(8):
+        moved = 0.5 * pltpu.roll(flat1[...], 4 * xo, 1)
+        end = jnp.where((lane >= 48) & (lane < 51), extra, moved[:, 384:])
+        band1_ref[pl.ds(xo * 32, 32), pl.ds(0, 384)] = moved[:, :384].astype(BF16)
+        band1_ref[pl.ds(xo * 32, 32), pl.ds(384, 128)] = end.astype(BF16)
+    for xo in range(6):
+        for dz in range(3):
+            tall[pl.ds(xo * 24, 24), pl.ds(dz * 256, 256)] = pltpu.roll(
+                flat2[pl.ds(dz * 24, 24), :], 32 * xo, 1
+            )
+    band2_ref[...] = tall[...].astype(BF16)
 
 
 def slab(ref, start, pieces):
@@ -174,18 +183,22 @@
     return jnp.where(even, b, a), jnp.where(even, a, b)
 
 
-def layers(first, second, band1_ref, band2_ref, bias_ref):
+def first_layer(first, second, band1_ref, pre_ref):
+    ones = jnp.where(lax.broadcasted_iota(jnp.int32, (16, 256), 0) < 3, 1.0, 0.0).astype(BF16)
     rows = jnp.concatenate(
         [jnp.concatenate(first, axis=0), jnp.concatenate(second, axis=0)], axis=1
     )
-    bias = jnp.concatenate([bias_ref[...]] * 8, axis=0)
-    bias = jnp.concatenate([bias, bias], axis=1)
-    pre = jnp.dot(band1_ref[:, :432], rows, preferred_element_type=F32) + bias
-    inner = pre * (0.7978845608028654 + 0.7978845608028654 * 0.044715 * (pre * pre))
-    half = 0.5 * pre
-    hidden = (half + half * jnp.tanh(inner)).astype(BF16)
-    both = jnp.dot(band2_ref[...], hidden, preferred_element_type=F32)
-    return both[:, :128], both[:, 128:]
+    rows = jnp.concatenate([rows, ones], axis=0)
+    pre_ref[...] = jnp.dot(band1_ref[:, :448], rows, preferred_element_type=F32)
+
+
+def activate(pre_ref, hidden_ref):
+    scale = 2.0 * 0.7978845608028654
+    for xo in range(8):
+        at = pl.ds(xo * 32, 32)
+        half = pre_ref[at, :]
+        inner = half * (scale + (4.0 * 0.044715 * scale) * (half * half))
+        hidden_ref[at, :] = (half + half * jnp.tanh(inner)).astype(BF16)
 
 
 def half_of(pair, i):
@@ -200,15 +213,16 @@
 
 def before_kernel(weights, *refs):
     keep_base, keep_state, step = weights
-    info_ref, q_ref, coarse_ref, wide_a_ref, wide_b_ref, band1_ref, band2_ref, bias_ref = refs[:8]
-    base_ref = refs[8] if keep_base else None
-    columns, parts, partial = refs[-3:]
+    info_ref, q_ref, coarse_ref, wide_a_ref, wide_b_ref, band1_ref = refs[:6]
+    base_ref = refs[6] if keep_base else None
+    columns, hidden, partial, pre = refs[-4:]
     chip_even = info_ref[1] == 0
     for j in range(4):
         left, right = rows_of(chip_even, wide_a_ref, wide_b_ref, j * 16)
         slab(columns, j * 144, [left, coarse_ref[pl.ds(j * 16, 16), :], right])
     pieces = [columns[pl.ds(j * 144, 144), :] for j in range(4)]
-    parts[0], parts[1] = layers(pieces[:3], pieces[1:], band1_ref, band2_ref, bias_ref)
+    first_layer(pieces[:3], pieces[1:], band1_ref, pre)
+    activate(pre, hidden)
 
     low = lax.broadcasted_iota(jnp.int32, (8, 128), 0) < 4
     sides = [rows_of(chip_even, wide_a_ref, wide_b_ref, 64 + z * 8) for z in range(0, 8, 2)]
@@ -240,8 +254,8 @@
 
 
 def after_body(
-    step, info_ref, q_ref, own_columns, own_parts, partial_ref, net_a_ref, net_b_ref,
-    band1_ref, band2_ref, bias_ref, div_ref, columns, parts, stress, new_ref,
+    step, info_ref, q_ref, own_columns, own_hidden, partial_ref, net_a_ref, net_b_ref,
+    band1_ref, band2_ref, div_ref, columns, stress, pre, hidden, new_ref,
 ):
     chip_even, net_even = info_ref[1] == 0, info_ref[2] == 0
     left_at, right_at = jnp.where(chip_even, 160, 112), jnp.where(chip_even, 112, 160)
@@ -256,33 +270,53 @@
             return own_columns[pl.ds((j - 3) * 144, 144), :]
         return columns[pl.ds((j if j < 3 else j - 4) * 144, 144), :]
 
-    for j, k in ((1, 2), (5, 6), (0, 7)):
-        parts[j], parts[k] = layers(
-            [piece(j + i) for i in range(3)], [piece(k + i) for i in range(3)],
-            band1_ref, band2_ref, bias_ref,
+    pairs = ((1, 2), (5, 6), (0, 7))
+
+    def conv1(i):
+        first, second = ([piece(j + dz) for dz in range(3)] for j in pairs[i])
+        first_layer(first, second, band1_ref, pre.at[i])
+
+    def gelu(i):
+        activate(pre.at[i], hidden.at[i])
+
+    def hidden_of(j):
+        if 3 <= j < 5:
+            return own_hidden[:, pl.ds((j - 3) * 128, 128)]
+        i = (2, 0, 0, None, None, 1, 1, 2)[j]
+        return hidden[i, :, pl.ds(pairs[i].index(j) * 128, 128)]
+
+    def levels(k, m):
+        rows = jnp.concatenate(
+            [
+                jnp.concatenate([hidden_of(n + dz) for dz in range(3)], axis=0)
+                for n in (k, m)
+            ],
+            axis=1,
         )
-
-    def part(j, at):
-        return own_parts[j - 3, at, :] if 3 <= j < 5 else parts[j, at, :]
-
-    for k in range(6):
-        rows = []
-        for xo in range(6):
-            sums = []
-            for dy in range(3):
-                at = [pl.ds(xo * 72 + (dz * 3 + dy) * 8, 8) for dz in range(3)]
-                sums.append(part(k, at[0]) + part(k + 1, at[1]) + part(k + 2, at[2]))
-            rows.append(sums[1] + pltpu.roll(sums[0], 1, 1) + pltpu.roll(sums[2], 127, 1))
-        stress[pl.ds(k * 48, 48), :] = jnp.concatenate(rows, axis=0).astype(BF16)
-    forces = []
-    for k in range(1, 5, 2):
+        both = jnp.dot(band2_ref[...], rows, preferred_element_type=F32)
+        for n, sums in ((k, both[:, :128]), (m, both[:, 128:])):
+            tiles = []
+            for xo in range(6):
+                at = xo * 24
+                tiles.append(
+                    sums[at + 8 : at + 16]
+                    + pltpu.roll(sums[at : at + 8], 1, 1)
+                    + pltpu.roll(sums[at + 16 : at + 24], 127, 1)
+                )
+            stress[pl.ds(n * 48, 48), :] = jnp.concatenate(tiles, axis=0).astype(BF16)
+
+    low = lax.broadcasted_iota(jnp.int32, (8, 128), 0) < 4
+    ends = [rows_of(net_even, net_a_ref, net_b_ref, 48 + x * 8) for x in range(0, 8, 2)]
+    below, above = zip(*ends)
+
+    def advance(k, m):
         operands = []
-        for m in (k, k + 1):
-            wide = stress[pl.ds(m * 48, 48), :].astype(F32)
+        for n in (k, m):
+            wide = stress[pl.ds(n * 48, 48), :].astype(F32)
             operands.append(
                 jnp.concatenate(
                     [
-                        stress[pl.ds((m - 1) * 48, 144), :],
+                        stress[pl.ds((n - 1) * 48, 144), :],
                         pltpu.roll(wide, 1, 1).astype(BF16),
                         pltpu.roll(wide, 127, 1).astype(BF16),
                     ],
@@ -292,31 +326,41 @@
         both = step * jnp.dot(
             div_ref[...], jnp.concatenate(operands, axis=1), preferred_element_type=F32
         )
-        forces += [both[:, :128], both[:, 128:]]
-
-    low = lax.broadcasted_iota(jnp.int32, (8, 128), 0) < 4
-    ends = [rows_of(net_even, net_a_ref, net_b_ref, 48 + x * 8) for x in range(0, 8, 2)]
-    below, above = zip(*ends)
-    for z in range(8):
-        for x in range(8):
-            value = partial_ref[z, x] + forces[z // 2][(x // 2) * 8 : (x // 2) * 8 + 8]
-            if z == 0:
-                w = velocity(q_ref, z, x, 2, low)
-                value = value + (step * viscosity + (0.5 * step) * w) * half_of(below, x)
-            if z == 7:
-                w = velocity(q_ref, z, x, 2, low)
-                value = value + (step * viscosity - (0.5 * step) * w) * half_of(above, x)
-            new_ref[z, x] = value
+        for n, force in ((k, both[:, :128]), (m, both[:, 128:])):
+            for z in (2 * n - 2, 2 * n - 1):
+                for x in range(8):
+                    value = partial_ref[z, x] + force[(x // 2) * 8 : (x // 2) * 8 + 8]
+                    if z == 0:
+                        w = velocity(q_ref, z, x, 2, low)
+                        factor = step * viscosity + (0.5 * step) * w
+                        value = value + factor * half_of(below, x)
+                    if z == 7:
+                        w = velocity(q_ref, z, x, 2, low)
+                        factor = step * viscosity - (0.5 * step) * w
+                        value = value + factor * half_of(above, x)
+                    new_ref[z, x] = value
+
+    conv1(0)
+    conv1(1)
+    gelu(0)
+    conv1(2)
+    gelu(1)
+    levels(1, 2)
+    gelu(2)
+    levels(3, 4)
+    levels(0, 5)
+    advance(2, 3)
+    advance(1, 4)
 
 
 def after_kernel(step, *refs):
-    ins, outs, scratch = refs[:11], refs[11:16], refs[16:]
+    ins, outs, scratch = refs[:10], refs[10:15], refs[15:]
     after_body(step, *ins, *scratch, outs[0])
     emit_messages(ins[0], *outs)
 
 
 def last_kernel(step, *refs):
-    ins, outs, scratch, new = refs[:11], refs[11:13], refs[13:-1], refs[-1]
+    ins, outs, scratch, new = refs[:10], refs[10:12], refs[12:-1], refs[-1]
     core = ins[0][0]
     after_body(step, *ins, *scratch, new)
     outs[0][...] = new[:, pl.ds(core * 4, 4)].reshape(256, 128)
@@ -394,8 +438,8 @@
     cross = near(edge_shift(cross, True))
     fixed = call(
         weights_kernel,
-        [((256, 512), BF16), ((432, 256), BF16), ((32, 128), F32)],
-        [pltpu.VMEM((32, 512), F32), pltpu.VMEM((72, 256), F32), pltpu.VMEM((432, 256), F32)],
+        [((256, 512), BF16), ((144, 768), BF16)],
+        [pltpu.VMEM((32, 512), F32), pltpu.VMEM((72, 256), F32), pltpu.VMEM((144, 768), F32)],
         info, conv1_weight, conv2_weight, conv1_bias.reshape(1, 32),
     )
     fixed = (*map(near, fixed), near(jnp.asarray(divergence_matrix(), BF16)))
@@ -403,15 +447,16 @@
         assemble_kernel,
         [((8, 8, 8, 128), F32)] + MESSAGES,
         [],
-        info, near(native), other, same, cross, fixed[2],
+        info, near(native), other, same, cross, fixed[1],
     )
     state = base = near(base)
     even = net % 2 == 0
     stages = ((0.0, 1.0, time_step), (0.75, 0.25, 0.25 * time_step), (1.0 / 3.0, 2.0 / 3.0, 2.0 / 3.0 * time_step))
     scratch = [
         pltpu.VMEM((864, 128), BF16),
-        pltpu.VMEM((8, 432, 128), F32),
         pltpu.VMEM((288, 128), BF16),
+        pltpu.VMEM((3, 256, 256), F32),
+        pltpu.VMEM((3, 256, 256), BF16),
     ]
     for stage, weights in enumerate(stages):
         wide_a, wide_b, net_a, net_b = messages
@@ -422,9 +467,9 @@
         far_b = net_swap(jnp.concatenate([net_b, *rows_b], axis=0), 1)
         before = call(
             functools.partial(before_kernel, weights),
-            [((576, 128), BF16), ((2, 432, 128), F32), ((8, 8, 8, 128), F32)],
-            [],
-            info, state, *map(near, (wide_a, got_a, got_b)), *fixed[:3], *([base] if stage else []),
+            [((576, 128), BF16), ((256, 256), BF16), ((8, 8, 8, 128), F32)],
+            [pltpu.VMEM((256, 256), F32)],
+            info, state, *map(near, (wide_a, got_a, got_b)), fixed[0], *([base] if stage else []),
         )
         ins = (info, state, *map(near, before), near(far_a), near(far_b), *fixed)
         if stage < 2:

time: 71.8 us -> 70 us (0.975)
  Pallas kernels: 14.5 us -> 12.1 us
    pallas_call x10, Pallas kernels: 14.5 us -> 12.1 us  [call(): pl.pallas_call(kernel, out_shape=result or [pltpu.VMEM(s, d) for s, d in...]
where the time goes in v3:
time: 70 us; the launch traced here: 69.8 us
  starting transfers between devices  37.8 us (54%)
  waiting for transfers between devices  17 us (24%)
  Pallas kernels  12.1 us (17%)
  local copies, waits for them, and re-layouts  2.58 us (4%)
    ppermute x6, starting transfers between devices, net_swap(): return lax.ppermute(value, 'net', pairs)  19 us
    pallas_call x10, Pallas kernels, call(): pl.pallas_call(kernel, out_shape=result or [pltpu.VMEM(s, d) for s, d in...  12.1 us
    ppermute x2, starting transfers between devices, partner(): lax.ppermute(value, 'wide', [(i, i ^ 1) for i in range(lax.axis_size('wid...  10.6 us
    ppermute x6, waiting for transfers between devices, chip_swap(): return lax.ppermute(value, 'wide', pairs)  8.69 us
    ppermute x6, waiting for transfers between devices, net_swap(): return lax.ppermute(value, 'net', pairs)  6.72 us
    ppermute x6, starting transfers between devices, chip_swap(): return lax.ppermute(value, 'wide', pairs)  5.68 us
    ppermute x2, starting transfers between devices, edge_shift(): return lax.ppermute(value, ('wide', 'narrow'), pairs)  2.63 us
    unnamed x12, local copies, waits for them, and re-layouts  2.58 us
  transfers between devices with their start and end apart: 16, of which 11 were waited for; matrix products, arithmetic and copies ran while one was open for 0% of the time, Pallas kernels for 6%

profile of v3, /device:TPU:1, one launch (start us, length us, event | category | flops | bytes accessed | tf_op | source)
XLA Modules:
  0.0 69.8 jit_solution(14880719330210716055)
XLA Ops:
  0.0 0.1 pad_add_fusion.info_ref.refs_0_
  0.1 0.0 copy-start.1
  0.1 0.9 %copy-done.1 = f32[4,8,4,256]{3,2,1,0:T(4,128)S(1)} copy-done((f32[4,8,4,256]{3,2,1,0:T(4,128)S(1)}, f32[4,8,4,256]{3,2,1,0:T(4,128)}, u32[]{:S(2)}) %copy-start.1) | copy-done | bytes 131096
  1.0 0.0 copy-start.3
  1.0 0.9 %shard_map.55 = (f32[256,128]{1,0:T(8,128)S(1)}, f32[32,128]{1,0:T(8,128)S(1)}, f32[32,128]{1,0:T(8,128)S(1)}, bf16[256,256]{1,0:T(8,128)(2,1)S(1)}) custom-call(s32[3]{0:T(128)S(1)} %pad_add_fusion.info_ref.refs_0_, f32[4,8,4,256]{3,2,1,0:T(4,128)S(1)} %copy-done.1), custom_call_target="tpu_custom_call" | custom-call | tf_op jit(solution)/shard_map/pallas_call | solution.py:41
  1.9 3.3 %collective-permute-start = (f32[256,128]{1,0:T(8,128)S(1)}, f32[256,128]{1,0:T(8,128)S(1)}, u32[]{:S(2)}, u32[]{:S(2)}) collective-permute-start(f32[256,128]{1,0:T(8,128)S(1)} %get-tuple-element.37.own_ref), channel_id=1, source_target_pairs={{0,32},{32,0},{64,96},{96,64},{128,160},{160,128},{192,224},{224,1... | collective-permute-start | bytes 393224 | tf_op jit(solution)/shard_map/ppermute | solution.py:411
  5.2 2.6 %collective-permute-start.1 = (f32[32,128]{1,0:T(8,128)S(1)}, f32[32,128]{1,0:T(8,128)S(1)}, u32[]{:S(2)}, u32[]{:S(2)}) collective-permute-start(f32[32,128]{1,0:T(8,128)S(1)} %get-tuple-element.38), channel_id=1, source_target_pairs={{0,8},{8,16},{16,24},{24,0},{32,56},{40,32},{48,40},{56,48},{64,72... | collective-permute-start | bytes 49160 | tf_op jit(solution)/shard_map/ppermute | solution.py:424
  7.8 0.0 copy-start.4
  7.8 0.0 collective-permute-start.2
  7.8 0.0 copy-done.3
  7.8 0.7 %copy-done.4 = bf16[27,32,4]{1,2,0:T(4,128)(2,1)S(1)} copy-done((bf16[27,32,4]{1,2,0:T(4,128)(2,1)S(1)}, bf16[27,32,4]{1,2,0:T(4,128)(2,1)}, u32[]{:S(2)}) %copy-start.4) | copy-done | bytes 6936
  8.6 0.3 copy.6.w1_ref
  8.8 0.0 copy-start.2
  8.9 0.6 copy-done.2
  9.5 0.9 %shard_map.56 = (bf16[256,512]{1,0:T(8,128)(2,1)S(1)}, bf16[144,768]{1,0:T(8,128)(2,1)S(1)}) custom-call(s32[3]{0:T(128)S(1)} %pad_add_fusion.info_ref.refs_0_, bf16[27,32,4]{2,1,0:T(8,128)(2,1)S(1)} %copy.6.w1_ref, bf16[27,6,32]{2,1,0:T(8,128)(2,1)S(1)} %copy.7.w2_ref, f32[1,32]{1,0:T(1,128)S(1)} %bitcast.4), custom_call_target="tpu_custom_call" | custom-call | tf_op jit(solution)/shard_map/pallas_call | solution.py:41
  10.4 0.0 collective-permute-done.1.same_ref
  10.4 0.6 collective-permute-done.2.cross_ref
  11.0 0.0 collective-permute-done.other_ref
  11.0 0.8 %shard_map.57 = (f32[8,8,8,128]{3,2,1,0:T(8,128)S(1)}, bf16[128,128]{1,0:T(8,128)(2,1)S(1)}, bf16[128,128]{1,0:T(8,128)(2,1)S(1)}, bf16[112,128]{1,0:T(8,128)(2,1)S(1)}, bf16[112,128]{1,0:T(8,128)(2,1)S(1)}) custom-call(s32[3]{0:T(128)S(1)} %pad_add_fusion.info_ref.refs_0_, f32[256,128]{1,0:T(8,128)S(1)} %get-tuple-element.37.own_ref, ...), custom_call_target="tpu_custom_call" | custom-call | tf_op jit(solution)/shard_map/pallas_call | solution.py:41
  11.8 2.8 %collective-permute-start.4 = (bf16[128,128]{1,0:T(8,128)(2,1)S(1)}, bf16[128,128]{1,0:T(8,128)(2,1)S(1)}, u32[]{:S(2)}, u32[]{:S(2)}) collective-permute-start(bf16[128,128]{1,0:T(8,128)(2,1)S(1)} %get-tuple-element.43), channel_id=1, source_target_pairs={{0,192},{32,224},{64,128},{96,160},{128,64},{160,96},{192,0},{224,... | collective-permute-start | bytes 98312 | tf_op jit(solution)/shard_map/ppermute | solution.py:401
  14.6 0.0 collective-permute-start.3
  14.6 1.7 %collective-permute-done.4.refs_4_ = bf16[128,128]{1,0:T(8,128)(2,1)S(1)} collective-permute-done((bf16[128,128]{1,0:T(8,128)(2,1)S(1)}, bf16[128,128]{1,0:T(8,128)(2,1)S(1)}, u32[]{:S(2)}, u32[]{:S(2)}) %collective-permute-start.4) | collective-permute-done | bytes 32800 | tf_op jit(solution)/shard_map/ppermute | solution.py:401
  16.3 1.5 %collective-permute-done.3.refs_3_ = bf16[128,128]{1,0:T(8,128)(2,1)S(1)} collective-permute-done((bf16[128,128]{1,0:T(8,128)(2,1)S(1)}, bf16[128,128]{1,0:T(8,128)(2,1)S(1)}, u32[]{:S(2)}, u32[]{:S(2)}) %collective-permute-start.3) | collective-permute-done | bytes 32800 | tf_op jit(solution)/shard_map/ppermute | solution.py:401
  17.8 1.3 %collective-permute-start.5 = (bf16[208,128]{1,0:T(8,128)(2,1)S(1)}, bf16[208,128]{1,0:T(8,128)(2,1)S(1)}, u32[]{:S(2)}, u32[]{:S(2)}) collective-permute-start(bf16[208,128]{1,0:T(8,128)(2,1)S(1)} %pad_maximum_fusion), channel_id=1, source_target_pairs={{0,1},{1,0},{2,3},{3,2},{4,5},{5,4},{6,7},{7,6},{8,9},{9,8},{10,11... | collective-permute-start | bytes 159752 | tf_op jit(solution)/shard_map/ppermute | solution.py:407
  19.1 5.8 %collective-permute-start.6 = (bf16[208,128]{1,0:T(8,128)(2,1)S(1)}, bf16[208,128]{1,0:T(8,128)(2,1)S(1)}, u32[]{:S(2)}, u32[]{:S(2)}) collective-permute-start(bf16[208,128]{1,0:T(8,128)(2,1)S(1)} %pad_maximum_fusion.1), channel_id=1, source_target_pairs={{0,7},{1,2},{2,1},{3,4},{4,3},{5,6},{6,5},{7,0},{8,15},{9,10},{10,... | collective-permute-start | bytes 159752 | tf_op jit(solution)/shard_map/ppermute | solution.py:407
  24.9 0.0 copy-start
  24.9 1.0 %shard_map.58 = (bf16[576,128]{1,0:T(8,128)(2,1)S(1)}, bf16[256,256]{1,0:T(8,128)(2,1)S(1)}, f32[8,8,8,128]{3,2,1,0:T(8,128)S(1)}) custom-call(s32[3]{0:T(128)S(1)} %pad_add_fusion.info_ref.refs_0_, f32[8,8,8,128]{3,2,1,0:T(8,128)S(1)} %get-tuple-element.41.refs_1_.refs_6_, bf16[128,128]{1,0:T(8,128)(2,1)S(1)} %get-tuple-element.42.refs_2_, ...), custom_call_target="tpu_custom_call" | custom-call | tf_op jit(solution)/shard_map/pallas_call | solution.py:41
  25.9 0.0 collective-permute-done.5.refs_5_
  25.9 2.2 %collective-permute-done.6.refs_6_ = bf16[208,128]{1,0:T(8,128)(2,1)S(1)} collective-permute-done((bf16[208,128]{1,0:T(8,128)(2,1)S(1)}, bf16[208,128]{1,0:T(8,128)(2,1)S(1)}, u32[]{:S(2)}, u32[]{:S(2)}) %collective-permute-start.6) | collective-permute-done | bytes 53280 | tf_op jit(solution)/shard_map/ppermute | solution.py:407
  28.1 0.0 copy-done
  28.1 1.7 %shard_map.59 = (f32[8,8,8,128]{3,2,1,0:T(8,128)S(1)}, bf16[128,128]{1,0:T(8,128)(2,1)S(1)}, bf16[128,128]{1,0:T(8,128)(2,1)S(1)}, bf16[112,128]{1,0:T(8,128)(2,1)S(1)}, bf16[112,128]{1,0:T(8,128)(2,1)S(1)}) custom-call(s32[3]{0:T(128)S(1)} %pad_add_fusion.info_ref.refs_0_, f32[8,8,8,128]{3,2,1,0:T(8,128)S(1)} %get-tuple-element.41.refs_1_.refs_6_, ...), custom_call_target="tpu_custom_call" | custom-call | tf_op jit(solution)/shard_map/pallas_call | solution.py:41
  29.8 1.5 %collective-permute-start.8 = (bf16[128,128]{1,0:T(8,128)(2,1)S(1)}, bf16[128,128]{1,0:T(8,128)(2,1)S(1)}, u32[]{:S(2)}, u32[]{:S(2)}) collective-permute-start(bf16[128,128]{1,0:T(8,128)(2,1)S(1)} %get-tuple-element.52), channel_id=1, source_target_pairs={{0,192},{32,224},{64,128},{96,160},{128,64},{160,96},{192,0},{224,... | collective-permute-start | bytes 98312 | tf_op jit(solution)/shard_map/ppermute | solution.py:401
  31.3 0.0 collective-permute-start.7
  31.3 2.6 %collective-permute-done.8.refs_4_ = bf16[128,128]{1,0:T(8,128)(2,1)S(1)} collective-permute-done((bf16[128,128]{1,0:T(8,128)(2,1)S(1)}, bf16[128,128]{1,0:T(8,128)(2,1)S(1)}, u32[]{:S(2)}, u32[]{:S(2)}) %collective-permute-start.8) | collective-permute-done | bytes 32800 | tf_op jit(solution)/shard_map/ppermute | solution.py:401
  33.9 0.2 collective-permute-done.7.refs_3_
  34.1 0.1 collective-permute-start.9
  34.2 5.7 %collective-permute-start.10 = (bf16[208,128]{1,0:T(8,128)(2,1)S(1)}, bf16[208,128]{1,0:T(8,128)(2,1)S(1)}, u32[]{:S(2)}, u32[]{:S(2)}) collective-permute-start(bf16[208,128]{1,0:T(8,128)(2,1)S(1)} %pad_maximum_fusion.3), channel_id=1, source_target_pairs={{0,7},{1,2},{2,1},{3,4},{4,3},{5,6},{6,5},{7,0},{8,15},{9,10},{10,... | collective-permute-start | bytes 159752 | tf_op jit(solution)/shard_map/ppermute | solution.py:407
  40.0 1.0 %shard_map.60 = (bf16[576,128]{1,0:T(8,128)(2,1)S(1)}, bf16[256,256]{1,0:T(8,128)(2,1)S(1)}, f32[8,8,8,128]{3,2,1,0:T(8,128)S(1)}) custom-call(s32[3]{0:T(128)S(1)} %pad_add_fusion.info_ref.refs_0_, f32[8,8,8,128]{3,2,1,0:T(8,128)S(1)} %get-tuple-element.50.refs_1_, bf16[128,128]{1,0:T(8,128)(2,1)S(1)} %get-tuple-element.51.refs_2_, ...), custom_call_target="tpu_custom_call" | custom-call | tf_op jit(solution)/shard_map/pallas_call | solution.py:41
  41.0 0.0 collective-permute-done.9.refs_5_
  41.0 2.3 %collective-permute-done.10.refs_6_ = bf16[208,128]{1,0:T(8,128)(2,1)S(1)} collective-permute-done((bf16[208,128]{1,0:T(8,128)(2,1)S(1)}, bf16[208,128]{1,0:T(8,128)(2,1)S(1)}, u32[]{:S(2)}, u32[]{:S(2)}) %collective-permute-start.10) | collective-permute-done | bytes 53280 | tf_op jit(solution)/shard_map/ppermute | solution.py:407
  43.3 1.7 %shard_map.61 = (f32[8,8,8,128]{3,2,1,0:T(8,128)S(1)}, bf16[128,128]{1,0:T(8,128)(2,1)S(1)}, bf16[128,128]{1,0:T(8,128)(2,1)S(1)}, bf16[112,128]{1,0:T(8,128)(2,1)S(1)}, bf16[112,128]{1,0:T(8,128)(2,1)S(1)}) custom-call(s32[3]{0:T(128)S(1)} %pad_add_fusion.info_ref.refs_0_, f32[8,8,8,128]{3,2,1,0:T(8,128)S(1)} %get-tuple-element.50.refs_1_, ...), custom_call_target="tpu_custom_call" | custom-call | tf_op jit(solution)/shard_map/pallas_call | solution.py:41
  45.0 1.4 %collective-permute-start.12 = (bf16[128,128]{1,0:T(8,128)(2,1)S(1)}, bf16[128,128]{1,0:T(8,128)(2,1)S(1)}, u32[]{:S(2)}, u32[]{:S(2)}) collective-permute-start(bf16[128,128]{1,0:T(8,128)(2,1)S(1)} %get-tuple-element.60), channel_id=1, source_target_pairs={{0,192},{32,224},{64,128},{96,160},{128,64},{160,96},{192,0},{224,... | collective-permute-start | bytes 98312 | tf_op jit(solution)/shard_map/ppermute | solution.py:401
  46.4 0.0 collective-permute-start.11
  46.4 2.7 %collective-permute-done.12.refs_4_ = bf16[128,128]{1,0:T(8,128)(2,1)S(1)} collective-permute-done((bf16[128,128]{1,0:T(8,128)(2,1)S(1)}, bf16[128,128]{1,0:T(8,128)(2,1)S(1)}, u32[]{:S(2)}, u32[]{:S(2)}) %collective-permute-start.12) | collective-permute-done | bytes 32800 | tf_op jit(solution)/shard_map/ppermute | solution.py:401
  49.1 0.1 collective-permute-done.11.refs_3_
  49.1 0.1 collective-permute-start.13
  49.3 5.9 %collective-permute-start.14 = (bf16[208,128]{1,0:T(8,128)(2,1)S(1)}, bf16[208,128]{1,0:T(8,128)(2,1)S(1)}, u32[]{:S(2)}, u32[]{:S(2)}) collective-permute-start(bf16[208,128]{1,0:T(8,128)(2,1)S(1)} %pad_maximum_fusion.5), channel_id=1, source_target_pairs={{0,7},{1,2},{2,1},{3,4},{4,3},{5,6},{6,5},{7,0},{8,15},{9,10},{10,... | collective-permute-start | bytes 159752 | tf_op jit(solution)/shard_map/ppermute | solution.py:407
  55.2 1.0 %shard_map.62 = (bf16[576,128]{1,0:T(8,128)(2,1)S(1)}, bf16[256,256]{1,0:T(8,128)(2,1)S(1)}, f32[8,8,8,128]{3,2,1,0:T(8,128)S(1)}) custom-call(s32[3]{0:T(128)S(1)} %pad_add_fusion.info_ref.refs_0_, f32[8,8,8,128]{3,2,1,0:T(8,128)S(1)} %get-tuple-element.58.refs_1_, bf16[128,128]{1,0:T(8,128)(2,1)S(1)} %get-tuple-element.59.refs_2_, ...), custom_call_target="tpu_custom_call" | custom-call | tf_op jit(solution)/shard_map/pallas_call | solution.py:41
  56.2 0.0 collective-permute-done.13.refs_5_
  56.2 2.2 %collective-permute-done.14.refs_6_ = bf16[208,128]{1,0:T(8,128)(2,1)S(1)} collective-permute-done((bf16[208,128]{1,0:T(8,128)(2,1)S(1)}, bf16[208,128]{1,0:T(8,128)(2,1)S(1)}, u32[]{:S(2)}, u32[]{:S(2)}) %collective-permute-start.14) | collective-permute-done | bytes 53280 | tf_op jit(solution)/shard_map/ppermute | solution.py:407
  58.3 1.7 %shard_map.63 = (f32[256,128]{1,0:T(8,128)S(1)}, f32[256,128]{1,0:T(8,128)S(1)}) custom-call(s32[3]{0:T(128)S(1)} %pad_add_fusion.info_ref.refs_0_, f32[8,8,8,128]{3,2,1,0:T(8,128)S(1)} %get-tuple-element.58.refs_1_, bf16[576,128]{1,0:T(8,128)(2,1)S(1)} %get-tuple-element.61.refs_2_, bf16[256,256]{1,0:T(8,128)(2,1)S(1)} %get-tuple-element.62.refs_3_, ...), custom_call_target="tpu_custom_call" | custom-call | tf_op jit(solution)/shard_map/pallas_call | solution.py:41
  60.0 7.3 %collective-permute-start.15 = (f32[256,128]{1,0:T(8,128)S(1)}, f32[256,128]{1,0:T(8,128)S(1)}, u32[]{:S(2)}, u32[]{:S(2)}) collective-permute-start(f32[256,128]{1,0:T(8,128)S(1)} %get-tuple-element.67), channel_id=1, source_target_pairs={{0,32},{32,0},{64,96},{96,64},{128,160},{160,128},{192,224},{224,1... | collective-permute-start | bytes 393224 | tf_op jit(solution)/shard_map/ppermute | solution.py:411
  67.3 1.0 %collective-permute-done.15.other_ref = f32[256,128]{1,0:T(8,128)S(1)} collective-permute-done((f32[256,128]{1,0:T(8,128)S(1)}, f32[256,128]{1,0:T(8,128)S(1)}, u32[]{:S(2)}, u32[]{:S(2)}) %collective-permute-start.15) | collective-permute-done | bytes 131104 | tf_op jit(solution)/shard_map/ppermute | solution.py:411
  68.3 1.6 %shard_map.64 = f32[4,8,4,256]{3,2,1,0:T(4,128)} custom-call(s32[3]{0:T(128)S(1)} %pad_add_fusion.info_ref.refs_0_, f32[256,128]{1,0:T(8,128)S(1)} %get-tuple-element.66.own_ref, f32[256,128]{1,0:T(8,128)S(1)} %collective-permute-done.15.other_ref, bf16[256,256]{1,0:T(8,128)(2,1)S(1)} %get-tuple-element.68.parity_ref), custom_call_target="tpu_custom_call" | custom-call | tf_op jit(solution)/shard_map/pallas_call | solution.py:41
  (13 shorter events, 0.1 us)
Async XLA Ops:
  0.1 0.9 %copy-start.1 = (f32[4,8,4,256]{3,2,1,0:T(4,128)S(1)}, f32[4,8,4,256]{3,2,1,0:T(4,128)}, u32[]{:S(2)}) copy-start(f32[4,8,4,256]{3,2,1,0:T(4,128)} %fields_ref.1) | copy-start | bytes 393220
  1.0 6.8 %copy-start.3 = (bf16[27,6,32]{2,0,1:T(8,128)(2,1)S(1)}, bf16[27,6,32]{2,0,1:T(8,128)(2,1)}, u32[]{:S(2)}) copy-start(bf16[27,6,32]{2,0,1:T(8,128)(2,1)} %param.8) | copy-start | bytes 31108
  1.9 9.1 %collective-permute-start = (f32[256,128]{1,0:T(8,128)S(1)}, f32[256,128]{1,0:T(8,128)S(1)}, u32[]{:S(2)}, u32[]{:S(2)}) collective-permute-start(f32[256,128]{1,0:T(8,128)S(1)} %get-tuple-element.37.own_ref), channel_id=1, source_target_pairs={{0,32},{32,0},{64,96},{96,64},{128,160},{160,128},{192,224},{224,1... | collective-permute-start | bytes 393224 | tf_op jit(solution)/shard_map/ppermute | solution.py:411
  5.2 5.2 %collective-permute-start.1 = (f32[32,128]{1,0:T(8,128)S(1)}, f32[32,128]{1,0:T(8,128)S(1)}, u32[]{:S(2)}, u32[]{:S(2)}) collective-permute-start(f32[32,128]{1,0:T(8,128)S(1)} %get-tuple-element.38), channel_id=1, source_target_pairs={{0,8},{8,16},{16,24},{24,0},{32,56},{40,32},{48,40},{56,48},{64,72... | collective-permute-start | bytes 49160 | tf_op jit(solution)/shard_map/ppermute | solution.py:424
  7.8 0.7 %copy-start.4 = (bf16[27,32,4]{1,2,0:T(4,128)(2,1)S(1)}, bf16[27,32,4]{1,2,0:T(4,128)(2,1)}, u32[]{:S(2)}) copy-start(bf16[27,32,4]{1,2,0:T(4,128)(2,1)} %param.6) | copy-start | bytes 20740
  7.8 3.2 %collective-permute-start.2 = (f32[32,128]{1,0:T(8,128)S(1)}, f32[32,128]{1,0:T(8,128)S(1)}, u32[]{:S(2)}, u32[]{:S(2)}) collective-permute-start(f32[32,128]{1,0:T(8,128)S(1)} %get-tuple-element.39), channel_id=1, source_target_pairs={{0,56},{8,32},{16,40},{24,48},{32,8},{40,16},{48,24},{56,0},{64,12... | collective-permute-start | bytes 49160 | tf_op jit(solution)/shard_map/ppermute | solution.py:424
  8.8 0.7 copy-start.2
  11.8 4.5 %collective-permute-start.4 = (bf16[128,128]{1,0:T(8,128)(2,1)S(1)}, bf16[128,128]{1,0:T(8,128)(2,1)S(1)}, u32[]{:S(2)}, u32[]{:S(2)}) collective-permute-start(bf16[128,128]{1,0:T(8,128)(2,1)S(1)} %get-tuple-element.43), channel_id=1, source_target_pairs={{0,192},{32,224},{64,128},{96,160},{128,64},{160,96},{192,0},{224,... | collective-permute-start | bytes 98312 | tf_op jit(solution)/shard_map/ppermute | solution.py:401
  14.6 3.2 %collective-permute-start.3 = (bf16[128,128]{1,0:T(8,128)(2,1)S(1)}, bf16[128,128]{1,0:T(8,128)(2,1)S(1)}, u32[]{:S(2)}, u32[]{:S(2)}) collective-permute-start(bf16[128,128]{1,0:T(8,128)(2,1)S(1)} %get-tuple-element.42.refs_2_), channel_id=1, source_target_pairs={{0,64},{32,96},{64,0},{96,32},{128,192},{160,224},{192,128},{224,1... | collective-permute-start | bytes 98312 | tf_op jit(solution)/shard_map/ppermute | solution.py:401
  17.8 8.1 %collective-permute-start.5 = (bf16[208,128]{1,0:T(8,128)(2,1)S(1)}, bf16[208,128]{1,0:T(8,128)(2,1)S(1)}, u32[]{:S(2)}, u32[]{:S(2)}) collective-permute-start(bf16[208,128]{1,0:T(8,128)(2,1)S(1)} %pad_maximum_fusion), channel_id=1, source_target_pairs={{0,1},{1,0},{2,3},{3,2},{4,5},{5,4},{6,7},{7,6},{8,9},{9,8},{10,11... | collective-permute-start | bytes 159752 | tf_op jit(solution)/shard_map/ppermute | solution.py:407
  19.1 9.0 %collective-permute-start.6 = (bf16[208,128]{1,0:T(8,128)(2,1)S(1)}, bf16[208,128]{1,0:T(8,128)(2,1)S(1)}, u32[]{:S(2)}, u32[]{:S(2)}) collective-permute-start(bf16[208,128]{1,0:T(8,128)(2,1)S(1)} %pad_maximum_fusion.1), channel_id=1, source_target_pairs={{0,7},{1,2},{2,1},{3,4},{4,3},{5,6},{6,5},{7,0},{8,15},{9,10},{10,... | collective-permute-start | bytes 159752 | tf_op jit(solution)/shard_map/ppermute | solution.py:407
  24.9 3.2 %copy-start = (bf16[32,240]{1,0:T(8,128)(2,1)S(1)}, bf16[32,240]{1,0:T(8,128)(2,1)}, u32[]{:S(2)}) copy-start(bf16[32,240]{1,0:T(8,128)(2,1)} %constant.45.clone.refs_9_) | copy-start | bytes 46084
  29.8 4.1 %collective-permute-start.8 = (bf16[128,128]{1,0:T(8,128)(2,1)S(1)}, bf16[128,128]{1,0:T(8,128)(2,1)S(1)}, u32[]{:S(2)}, u32[]{:S(2)}) collective-permute-start(bf16[128,128]{1,0:T(8,128)(2,1)S(1)} %get-tuple-element.52), channel_id=1, source_target_pairs={{0,192},{32,224},{64,128},{96,160},{128,64},{160,96},{192,0},{224,... | collective-permute-start | bytes 98312 | tf_op jit(solution)/shard_map/ppermute | solution.py:401
  31.3 2.8 %collective-permute-start.7 = (bf16[128,128]{1,0:T(8,128)(2,1)S(1)}, bf16[128,128]{1,0:T(8,128)(2,1)S(1)}, u32[]{:S(2)}, u32[]{:S(2)}) collective-permute-start(bf16[128,128]{1,0:T(8,128)(2,1)S(1)} %get-tuple-element.51.refs_2_), channel_id=1, source_target_pairs={{0,64},{32,96},{64,0},{96,32},{128,192},{160,224},{192,128},{224,1... | collective-permute-start | bytes 98312 | tf_op jit(solution)/shard_map/ppermute | solution.py:401
  34.1 6.9 %collective-permute-start.9 = (bf16[208,128]{1,0:T(8,128)(2,1)S(1)}, bf16[208,128]{1,0:T(8,128)(2,1)S(1)}, u32[]{:S(2)}, u32[]{:S(2)}) collective-permute-start(bf16[208,128]{1,0:T(8,128)(2,1)S(1)} %pad_maximum_fusion.2), channel_id=1, source_target_pairs={{0,1},{1,0},{2,3},{3,2},{4,5},{5,4},{6,7},{7,6},{8,9},{9,8},{10,11... | collective-permute-start | bytes 159752 | tf_op jit(solution)/shard_map/ppermute | solution.py:407
  34.2 9.1 %collective-permute-start.10 = (bf16[208,128]{1,0:T(8,128)(2,1)S(1)}, bf16[208,128]{1,0:T(8,128)(2,1)S(1)}, u32[]{:S(2)}, u32[]{:S(2)}) collective-permute-start(bf16[208,128]{1,0:T(8,128)(2,1)S(1)} %pad_maximum_fusion.3), channel_id=1, source_target_pairs={{0,7},{1,2},{2,1},{3,4},{4,3},{5,6},{6,5},{7,0},{8,15},{9,10},{10,... | collective-permute-start | bytes 159752 | tf_op jit(solution)/shard_map/ppermute | solution.py:407
  45.0 4.1 %collective-permute-start.12 = (bf16[128,128]{1,0:T(8,128)(2,1)S(1)}, bf16[128,128]{1,0:T(8,128)(2,1)S(1)}, u32[]{:S(2)}, u32[]{:S(2)}) collective-permute-start(bf16[128,128]{1,0:T(8,128)(2,1)S(1)} %get-tuple-element.60), channel_id=1, source_target_pairs={{0,192},{32,224},{64,128},{96,160},{128,64},{160,96},{192,0},{224,... | collective-permute-start | bytes 98312 | tf_op jit(solution)/shard_map/ppermute | solution.py:401
  46.4 2.8 %collective-permute-start.11 = (bf16[128,128]{1,0:T(8,128)(2,1)S(1)}, bf16[128,128]{1,0:T(8,128)(2,1)S(1)}, u32[]{:S(2)}, u32[]{:S(2)}) collective-permute-start(bf16[128,128]{1,0:T(8,128)(2,1)S(1)} %get-tuple-element.59.refs_2_), channel_id=1, source_target_pairs={{0,64},{32,96},{64,0},{96,32},{128,192},{160,224},{192,128},{224,1... | collective-permute-start | bytes 98312 | tf_op jit(solution)/shard_map/ppermute | solution.py:401
  49.1 7.0 %collective-permute-start.13 = (bf16[208,128]{1,0:T(8,128)(2,1)S(1)}, bf16[208,128]{1,0:T(8,128)(2,1)S(1)}, u32[]{:S(2)}, u32[]{:S(2)}) collective-permute-start(bf16[208,128]{1,0:T(8,128)(2,1)S(1)} %pad_maximum_fusion.4), channel_id=1, source_target_pairs={{0,1},{1,0},{2,3},{3,2},{4,5},{5,4},{6,7},{7,6},{8,9},{9,8},{10,11... | collective-permute-start | bytes 159752 | tf_op jit(solution)/shard_map/ppermute | solution.py:407
  49.3 9.1 %collective-permute-start.14 = (bf16[208,128]{1,0:T(8,128)(2,1)S(1)}, bf16[208,128]{1,0:T(8,128)(2,1)S(1)}, u32[]{:S(2)}, u32[]{:S(2)}) collective-permute-start(bf16[208,128]{1,0:T(8,128)(2,1)S(1)} %pad_maximum_fusion.5), channel_id=1, source_target_pairs={{0,7},{1,2},{2,1},{3,4},{4,3},{5,6},{6,5},{7,0},{8,15},{9,10},{10,... | collective-permute-start | bytes 159752 | tf_op jit(solution)/shard_map/ppermute | solution.py:407
  60.0 8.3 %collective-permute-start.15 = (f32[256,128]{1,0:T(8,128)S(1)}, f32[256,128]{1,0:T(8,128)S(1)}, u32[]{:S(2)}, u32[]{:S(2)}) collective-permute-start(f32[256,128]{1,0:T(8,128)S(1)} %get-tuple-element.67), channel_id=1, source_target_pairs={{0,32},{32,0},{64,96},{96,64},{128,160},{160,128},{192,224},{224,1... | collective-permute-start | bytes 393224 | tf_op jit(solution)/shard_map/ppermute | solution.py:411
